TPU v7x, 32 devices: a whole 2x2x4 slice. The times are simulated.
32 devices in a mesh: gx: 16 (over z, y, x), gy: 2 (over core).
Axes of the slice: x: 2, y: 2, z: 4, core: 2. Of those that a mesh axis runs over, the one named last changes fastest.
Arguments:
- node_latents: bfloat16 [16, 2, 256, 512], P('gx', 'gy'), may hold values from -6 to 6
- edge_latents: bfloat16 [16, 2, 768, 512], P('gx', 'gy'), may hold values from -6 to 6
- edge_w1: bfloat16 [1536, 512], replicated, may hold values from -0.15625 to 0.15625
- edge_b1: float32 [512], replicated, may hold values from -3 to 3
- edge_w2: bfloat16 [512, 512], replicated, may hold values from -0.25 to 0.25
- node_w1: bfloat16 [1024, 512], replicated, may hold values from -0.1875 to 0.1875
- node_b1: float32 [512], replicated, may hold values from -3 to 3
- node_w2: bfloat16 [512, 512], replicated, may hold values from -0.25 to 0.25
- node_cot: bfloat16 [16, 2, 256, 512], P('gx', 'gy'), may hold values from -6 to 6
- edge_cot: bfloat16 [16, 2, 768, 512], P('gx', 'gy'), may hold values from -6 to 6
- send_count: int32 [16, 2, 4], P('gx', 'gy'), may hold values from 0 to 2, as said below
- send_list: int32 [16, 2, 4, 2], P('gx', 'gy'), may hold values from 0 to 1
- tile_recv: int32 [16, 2, 6], P('gx', 'gy'), may hold values from 0 to 1
- tile_send: int32 [16, 2, 6], P('gx', 'gy'), may hold values from 0 to 9, as said below
- tile_perm: int32 [16, 2, 6, 128], P('gx', 'gy'), may hold values from 0 to 127, each once within a row
Outputs:
- node_out: bfloat16 [16, 2, 256, 512], P('gx', 'gy')
- node_grad: bfloat16 [16, 2, 256, 512], P('gx', 'gy')
- edge_grad: bfloat16 [16, 2, 768, 512], P('gx', 'gy')
- weight_dir: bfloat16 [1835008], P(('gx', 'gy'))
Inputs may be any that keep to these rules, and one draw needn't show every extreme that they name: `send_count`: entries for a neighbour outside the grid of partitions are 0, all others at least 1; the partition at (0, 0) sends 2 blocks to its neighbour at gx+1. `tile_send`: A value of 2 or more is a halo slot 2 + d * 2 + s that direction d's neighbour fills (s below its send count).
All inputs are finite; a program needn't handle non-finite values.
Results may differ from a plain program's by a relative error of at most 0.0075.
Values may be sent and summed in bfloat16 or wider, within the bound.
No kernel may reach another device: no remote copies, remote signals or barrier semaphores. Data moves between devices by JAX's collectives and lax.ppermute only.
A program may use at most 128 MiB of HBM per device.

v0:
```python
import jax
import jax.numpy as jnp
from jax import lax
from jax.sharding import PartitionSpec as P


def padded(block, sides, width):
    for axis, dim in sides:
        count = lax.axis_size(axis)
        forward = [(i, i + 1) for i in range(count - 1)]
        backward = [(target, source) for source, target in forward]
        low = lax.ppermute(
            lax.slice_in_dim(block, block.shape[dim] - width, None, axis=dim), axis, forward
        )
        high = lax.ppermute(lax.slice_in_dim(block, 0, width, axis=dim), axis, backward)
        block = jnp.concatenate([low, block, high], axis=dim)
    return block


def silu_slope(values):
    logistic = jax.nn.sigmoid(values)
    return logistic * (1.0 + values * (1.0 - logistic))


def layer_norm(values):
    center = values - jnp.mean(values, axis=-1, keepdims=True)
    inverse_rms = lax.rsqrt(jnp.mean(center * center, axis=-1, keepdims=True) + 1e-05)
    return (center * inverse_rms, inverse_rms)


def norm_back(normed, inverse_rms, upstream):
    return inverse_rms * (
        upstream
        - jnp.mean(upstream, axis=-1, keepdims=True)
        - normed * jnp.mean(upstream * normed, axis=-1, keepdims=True)
    )


def inner_rows(factor, second):
    return lax.dot_general(
        factor, second, (((0,), (0,)), ((), ())), preferred_element_type=jnp.float32
    )


def times_transposed(factor, second):
    return lax.dot_general(
        factor, second, (((1,), (1,)), ((), ())), preferred_element_type=jnp.float32
    )


def matmul(factor, second):
    return jnp.dot(factor, second, preferred_element_type=jnp.float32)


def fetch_halo(packed):
    row_halo = padded(jnp.stack([packed[1], packed[0]]), (("gx", 0),), 1)
    col_halo = padded(jnp.stack([packed[3], packed[2]]), (("gy", 0),), 1)
    return jnp.concatenate([row_halo[0], row_halo[3], col_halo[0], col_halo[3]], axis=0)


def return_partials(halo_part):
    row_back = padded(
        jnp.stack([halo_part[0], halo_part[1]]).astype(jnp.bfloat16), (("gx", 0),), 1
    ).astype(jnp.float32)
    col_back = padded(
        jnp.stack([halo_part[2], halo_part[3]]).astype(jnp.bfloat16), (("gy", 0),), 1
    ).astype(jnp.float32)
    return jnp.stack([row_back[3], row_back[0], col_back[3], col_back[0]])


def on_device(
    node_latents,
    edge_latents,
    edge_w1,
    edge_b1,
    edge_w2,
    node_w1,
    node_b1,
    node_w2,
    node_cot,
    edge_cot,
    send_count,
    send_list,
    tile_recv,
    tile_send,
    tile_perm,
):
    feature = node_latents.shape[3]
    block_size = tile_perm.shape[3]
    tile_count = tile_perm.shape[2]
    slot_count = send_list.shape[3]
    node_count = node_latents.shape[2]
    block_count = node_count // block_size
    node_blocks = node_latents.reshape(block_count, block_size, feature)
    local_rows = node_latents.reshape(node_count, feature)
    edge_rows = edge_latents.reshape(tile_count * block_size, feature)
    cot_node = node_cot.reshape(node_count, feature)
    cot_edge = edge_cot.reshape(tile_count * block_size, feature)
    send_counts = send_count.reshape(4)
    send_lists = send_list.reshape(4, slot_count)
    recv_idx = tile_recv.reshape(tile_count)
    send_idx = tile_send.reshape(tile_count)
    perm_idx = tile_perm.reshape(tile_count, block_size)
    live_slots = jnp.arange(slot_count, dtype=jnp.int32)[None, :] < send_counts[:, None]
    packed = jnp.where(
        live_slots[:, :, None, None], node_blocks[send_lists], jnp.zeros((), jnp.bfloat16)
    )
    offsets = jnp.arange(block_size, dtype=jnp.int32)
    recv_rows = (recv_idx[:, None] * block_size + offsets[None, :]).reshape(-1)
    send_rows = (send_idx[:, None] * block_size + perm_idx).reshape(-1)
    h_recv = local_rows[recv_rows]
    halo_blocks = fetch_halo(packed)
    flat_ext = jnp.concatenate([node_blocks, halo_blocks], axis=0).reshape(-1, feature)
    h_send = flat_ext[send_rows]
    joined = jnp.concatenate([edge_rows, h_recv, h_send], axis=1)
    edge_affine = matmul(joined, edge_w1) + edge_b1
    edge_hidden = jax.nn.silu(edge_affine).astype(jnp.bfloat16)
    edge_linear = matmul(edge_hidden, edge_w2)
    message, edge_inv = layer_norm(edge_linear)
    recv_hot = (recv_idx[None, :] == jnp.arange(block_count, dtype=jnp.int32)[:, None]).astype(
        jnp.float32
    )
    aggregate = jnp.einsum(
        "bt,tnf->bnf",
        recv_hot,
        message.reshape(tile_count, block_size, feature),
        precision=lax.Precision.HIGHEST,
    )
    aggregate = aggregate.reshape(node_count, feature).astype(jnp.bfloat16)
    node_input = jnp.concatenate([local_rows, aggregate], axis=1)
    node_affine = matmul(node_input, node_w1) + node_b1
    node_hidden = jax.nn.silu(node_affine).astype(jnp.bfloat16)
    node_linear = matmul(node_hidden, node_w2)
    node_normed, node_inv = layer_norm(node_linear)
    node_out = (local_rows.astype(jnp.float32) + node_normed).astype(jnp.bfloat16)
    grad_node_linear = norm_back(node_normed, node_inv, cot_node.astype(jnp.float32)).astype(
        jnp.bfloat16
    )
    g_nw2 = inner_rows(node_hidden, grad_node_linear)
    grad_node_affine = (
        times_transposed(grad_node_linear, node_w2) * silu_slope(node_affine)
    ).astype(jnp.bfloat16)
    g_nw1 = inner_rows(node_input, grad_node_affine)
    grad_node_input = times_transposed(grad_node_affine, node_w1)
    grad_direct = grad_node_input[:, :feature]
    grad_aggregate = grad_node_input[:, feature:]
    grad_message = grad_aggregate[recv_rows] + cot_edge.astype(jnp.float32)
    grad_edge_linear = norm_back(message, edge_inv, grad_message).astype(jnp.bfloat16)
    g_ew2 = inner_rows(edge_hidden, grad_edge_linear)
    grad_edge_affine = (
        times_transposed(grad_edge_linear, edge_w2) * silu_slope(edge_affine)
    ).astype(jnp.bfloat16)
    g_ew1 = inner_rows(joined, grad_edge_affine)
    grad_joined = times_transposed(grad_edge_affine, edge_w1)
    grad_e = grad_joined[:, :feature]
    grad_r = grad_joined[:, feature : 2 * feature]
    grad_s = grad_joined[:, 2 * feature :]
    edge_grad = (cot_edge.astype(jnp.float32) + grad_e).astype(jnp.bfloat16)
    grad_recv = jnp.einsum(
        "bt,tnf->bnf",
        recv_hot,
        grad_r.reshape(tile_count, block_size, feature),
        precision=lax.Precision.HIGHEST,
    )
    inverse = jnp.argsort(perm_idx, axis=1)
    grad_send = jnp.take_along_axis(
        grad_s.reshape(tile_count, block_size, feature), inverse[:, :, None], axis=1
    )
    extended_count = block_count + 4 * slot_count
    send_hot = (send_idx[None, :] == jnp.arange(extended_count, dtype=jnp.int32)[:, None]).astype(
        jnp.float32
    )
    partial_sum = jnp.einsum("bt,tnf->bnf", send_hot, grad_send, precision=lax.Precision.HIGHEST)
    owned_part = (
        partial_sum[:block_count]
        + grad_recv
        + grad_direct.reshape(block_count, block_size, feature)
    )
    halo_part = partial_sum[block_count:].reshape(4, slot_count, block_size, feature)
    returned = return_partials(halo_part)
    back_hot = (
        (send_lists[:, :, None] == jnp.arange(block_count, dtype=jnp.int32)[None, None, :])
        & live_slots[:, :, None]
    ).astype(jnp.float32)
    contrib = jnp.einsum("qsb,qsnf->bnf", back_hot, returned, precision=lax.Precision.HIGHEST)
    node_grad = (
        cot_node.reshape(block_count, block_size, feature).astype(jnp.float32)
        + owned_part
        + contrib
    )
    node_grad = node_grad.astype(jnp.bfloat16).reshape(1, 1, node_count, feature)
    weight_grad = jnp.concatenate([g_ew1, g_ew2, g_nw1, g_nw2], axis=0)
    total_entries = 7 * feature * feature
    share_len = total_entries // lax.axis_size(("gx", "gy"))
    summed = lax.psum(weight_grad, ("gx", "gy"))
    bounds = [0, 3 * feature, 4 * feature, 6 * feature, 7 * feature]
    pieces = []
    for index in range(4):
        matrix = summed[bounds[index] : bounds[index + 1]]
        pieces.append(matrix * lax.rsqrt(jnp.mean(matrix * matrix) + 1e-06))
    normalized = jnp.concatenate(pieces, axis=0).reshape(total_entries)
    own_start = lax.axis_index(("gx", "gy")) * share_len
    weight_dir = lax.dynamic_slice_in_dim(normalized, own_start, share_len).astype(jnp.bfloat16)
    return (
        node_out.reshape(1, 1, node_count, feature),
        node_grad,
        edge_grad.reshape(1, 1, tile_count * block_size, feature),
        weight_dir,
    )


def solution(mesh):
    placed = (
        P("gx", "gy", None, None),
        P("gx", "gy", None, None),
        P(),
        P(),
        P(),
        P(),
        P(),
        P(),
        P("gx", "gy", None, None),
        P("gx", "gy", None, None),
        P("gx", "gy", None),
        P("gx", "gy", None, None),
        P("gx", "gy", None),
        P("gx", "gy", None),
        P("gx", "gy", None, None),
    )
    return jax.shard_map(
        on_device,
        mesh=mesh,
        in_specs=placed,
        out_specs=(
            P("gx", "gy", None, None),
            P("gx", "gy", None, None),
            P("gx", "gy", None, None),
            P(("gx", "gy")),
        ),
        check_vma=False,
    )
```

profile of v0, /device:TPU:0, one launch (start us, length us, event | category | flops | bytes accessed | tf_op | source)
XLA Modules:
  0.0 270.5 jit_solution(10264045444098275007)
XLA Ops:
  9.8 1.6 gather_fusion.1
  11.6 1.0 fusion.59
  12.6 5.6 %collective-permute-start = (bf16[1,2,128,512]{3,2,1,0:T(8,128)(2,1)}, bf16[1,2,128,512]{3,2,1,0:T(8,128)(2,1)}, u32[]{:S(2)}, u32[]{:S(2)}) collective-permute-start(bf16[1,2,128,512]{3,2,1,0:T(8,128)(2,1)} %get-tuple-element.28), channel_id=1, source_target_pairs={{0,2},{2,4},{4,6},{6,8},{8,10},{10,12},{12,14},{14,16},{16,18},{18... | collective-permute-start | bytes 786440 | tf_op jit(solution)/shard_map/ppermute | solution.py:12
  18.1 1.3 collective-permute-start.1
  19.4 2.2 collective-permute-start.2
  21.6 1.3 collective-permute-start.3
  24.5 3.4 %gather_fusion = bf16[768,512]{1,0:T(8,128)(2,1)} fusion(bf16[256,512]{1,0:T(8,128)(2,1)S(1)} %bitcast.130, s32[1024]{0:T(1024)S(1)} %get-tuple-element.40), kind=kCustom, calls=%fused_computation | custom fusion | bytes 1575936 | tf_op jit(solution)/shard_map/gather | solution.py:111
  27.9 1.0 collective-permute-done
  28.9 1.0 bitcast_dynamic-update-slice_fusion.3
  29.9 0.9 collective-permute-done.1
  30.9 1.0 bitcast_dynamic-update-slice_fusion.2
  31.8 1.0 bitcast_dynamic-update-slice_fusion.1
  32.8 1.0 bitcast_dynamic-update-slice_fusion
  33.8 3.3 %gather_fusion.2 = bf16[768,512]{1,0:T(8,128)(2,1)} fusion(bf16[1280,512]{1,0:T(8,128)(2,1)S(1)} %bitcast.134, s32[1024]{0:T(1024)S(1)} %get-tuple-element.39), kind=kCustom, calls=%fused_computation.2 | custom fusion | bytes 1575936 | tf_op jit(solution)/shard_map/gather | solution.py:114
  37.1 4.3 %multiply_convert_fusion.2 = (bf16[768,512]{1,0:T(8,128)(2,1)S(1)}, f32[768,512]{1,0:T(8,128)}) fusion(f32[512]{0:T(512)S(1)} %copy-done.26, bf16[1536,512]{1,0:T(8,128)(2,1)S(1)} %copy-done, bf16[768,512]{1,0:T(8,128)(2,1)} %gather_fusion.2, bf16[768,512]{1,0:T(8,128)(2,1)} %gather_fusion, bf16[768,512]{1,0:T(8,128)(2,1)} %bitcast.150), kind=kOutput, calls=%fused_computation.28 | convolution fusion | flops 1217396736 | bytes 6293504 | tf_op jit(solution)/shard_map/dot_general | solution.py:52
  43.3 1.9 fusion.12
  46.9 0.9 fusion.28
  47.8 1.5 fusion.54
  50.3 1.8 fusion.29
  52.1 0.9 fusion.58
  53.0 3.2 %gather_fusion.3 = f32[768,512]{1,0:T(8,128)} fusion(f32[256,512]{1,0:T(8,128)S(1)} %get-tuple-element.23, s32[1024]{0:T(1024)S(1)} %get-tuple-element.40), kind=kCustom, calls=%fused_computation.3 | custom fusion | bytes 3148800 | tf_op jit(solution)/shard_map/gather | solution.py:147
  56.1 2.7 fusion.20
  61.7 0.9 multiply_convert_fusion
  63.3 1.4 fusion.17
  65.1 3.4 %pad_maximum_fusion = f32[3584,512]{1,0:T(8,128)} fusion(f32[512,512]{1,0:T(8,128)S(1)} %copy-done.13, f32[1024,512]{1,0:T(8,128)S(1)} %copy-done.6, f32[512,512]{1,0:T(8,128)S(1)} %fusion.65, f32[1536,512]{1,0:T(8,128)S(1)} %fusion.17), kind=kLoop, calls=%fused_computation.5 | loop fusion | flops 5505024 | bytes 14680064 | tf_op jit(solution)/shard_map/concatenate | solution.py:192
  70.1 1.4 fusion.64
  71.5 1.9 fusion.19
  73.4 7.8 %gather_fusion.4 = f32[768,512]{1,0:T(8,128)} fusion(f32[6,128,512]{2,1,0:T(8,128)S(1)} %bitcast.133, s32[768]{0:T(1024)S(1)} %fusion.33), kind=kCustom, calls=%fused_computation.4 | custom fusion | bytes 3151872 | tf_op jit(solution)/shard_map/jit(take_along_axis)/gather | solution.py:166
  81.2 4.7 %fusion.62 = (bf16[10,128,512]{2,0,1:T(8,128)(2,1)S(1)}, f32[10,128,512]{2,0,1:T(8,128)S(1)}) fusion(f32[6,128,512]{2,1,0:T(8,128)} %bitcast.137, pred[6,128]{0,1:T(8,128)(4,1)S(1)} %copy.42, s32[6]{0:T(128)S(1)} %bitcast.149), kind=kOutput, calls=%fused_computation.139 | convolution fusion | flops 48234556 | bytes 5505816 | tf_op jit(solution)/shard_map/bt,tnf->bnf/dot_general | solution.py:173
  86.0 0.8 slice_bitcast_fusion.3
  86.8 3.4 %collective-permute-start.4 = (bf16[1,2,128,512]{3,1,2,0:T(2,128)(2,1)S(1)}, bf16[1,2,128,512]{3,1,2,0:T(2,128)(2,1)S(1)}, u32[]{:S(2)}, u32[]{:S(2)}) collective-permute-start(bf16[1,2,128,512]{3,1,2,0:T(2,128)(2,1)S(1)} %get-tuple-element.15), channel_id=1, source_target_pairs={{0,2},{2,4},{4,6},{6,8},{8,10},{10,12},{12,14},{14,16},{16,18},{18... | collective-permute-start | bytes 786440 | tf_op jit(solution)/shard_map/ppermute | solution.py:12
  90.3 1.3 collective-permute-start.5
  91.6 2.5 collective-permute-start.6
  94.1 1.5 collective-permute-start.7
  95.6 1.9 fusion.2
  97.7 6.4 %collective-permute-done.4 = bf16[1,2,128,512]{3,1,2,0:T(2,128)(2,1)S(1)} collective-permute-done((bf16[1,2,128,512]{3,1,2,0:T(2,128)(2,1)S(1)}, bf16[1,2,128,512]{3,1,2,0:T(2,128)(2,1)S(1)}, u32[]{:S(2)}, u32[]{:S(2)}) %collective-permute-start.4) | collective-permute-done | bytes 262176 | tf_op jit(solution)/shard_map/ppermute | solution.py:12
  104.1 3.6 %collective-permute-done.5 = bf16[1,2,128,512]{3,1,2,0:T(2,128)(2,1)S(1)} collective-permute-done((bf16[1,2,128,512]{3,1,2,0:T(2,128)(2,1)S(1)}, bf16[1,2,128,512]{3,1,2,0:T(2,128)(2,1)S(1)}, u32[]{:S(2)}, u32[]{:S(2)}) %collective-permute-start.5) | collective-permute-done | bytes 262176 | tf_op jit(solution)/shard_map/ppermute | solution.py:15
  109.0 1.1 pad_maximum_fusion.2
  110.2 3.2 %fusion.8 = f32[2,128,512]{2,0,1:T(2,128)S(1)} fusion(f32[4,2,128,512]{3,1,2,0:T(2,128)S(1)} %pad_maximum_fusion.2, pred[4,2]{0,1:T(4,128)(4,1)S(1)} %iota_compare_fusion.1, s32[4,2]{0,1:T(2,128)S(1)} %bitcast.146), kind=kOutput, calls=%fused_computation.32 | convolution fusion | flops 12582944 | bytes 2621480 | tf_op jit(solution)/shard_map/qsb,qsnf->bnf/dot_general | solution.py:185
  113.4 1.0 fusion.24
  114.4 128.1 %all-reduce.2.cloned.1.call-done = f32[3584,512]{1,0:T(8,128)} async-done(((f32[3584,512]{1,0:T(8,128)}), f32[3584,512]{1,0:T(8,128)}) %all-reduce.2.cloned.1.call-update) | async-done | bytes 7340048 | tf_op jit(solution)/shard_map/psum | solution.py:195
  242.5 3.3 %multiply_reduce_fusion = f32[]{:T(128)} fusion(f32[3584,512]{1,0:T(8,128)} %all-reduce.2.cloned.1.call-done), kind=kLoop, calls=%fused_computation.7 | loop fusion | flops 1572863 | bytes 3145732 | tf_op jit(solution)/shard_map/reduce_sum | solution.py:200
  246.5 2.7 %multiply_reduce_fusion.1 = f32[]{:T(128)} fusion(f32[3584,512]{1,0:T(8,128)} %all-reduce.2.cloned.1.call-done), kind=kLoop, calls=%fused_computation.19 | loop fusion | flops 1048575 | bytes 2097156 | tf_op jit(solution)/shard_map/reduce_sum | solution.py:200
  249.9 2.5 multiply_reduce_fusion.5
  253.8 2.3 slice_multiply_fusion
  256.1 1.9 slice_multiply_fusion.1
  258.0 1.8 slice_multiply_fusion.3
  260.5 1.9 copy.54
  (110 shorter events, 16.1 us)
Async XLA Ops:
  8.0 29.1 %copy-start = (bf16[1536,512]{1,0:T(8,128)(2,1)S(1)}, bf16[1536,512]{1,0:T(8,128)(2,1)}, u32[]{:S(2)}) copy-start(bf16[1536,512]{1,0:T(8,128)(2,1)} %param.17) | copy-start | bytes 4718596
  8.0 60.5 %sort.19.cloned.1.call-start = ((), (), s32[]{:S(2)}) async-start(), calls=%async_computation.1 | async-start | bytes 24608 | tf_op jit(solution)/shard_map/jit(argsort)/sort | solution.py:165
  11.5 11.3 %copy-start.19 = (s32[1,1,6,128]{3,1,2,0:T(1,128)S(1)}, s32[1,1,6,128]{3,1,2,0:T(1,128)}, u32[]{:S(2)}) copy-start(s32[1,1,6,128]{3,1,2,0:T(1,128)} %param.29) | copy-start | bytes 9220
  11.5 12.6 %copy-start.21 = (s32[1,1,6]{2,1,0:T(1,128)S(1)}, s32[1,1,6]{2,1,0:T(1,128)}, u32[]{:S(2)}) copy-start(s32[1,1,6]{2,1,0:T(1,128)} %param.27) | copy-start | bytes 76
  11.6 12.7 %copy-start.22 = (s32[1,1,6]{2,1,0:T(1,128)S(1)}, s32[1,1,6]{2,1,0:T(1,128)}, u32[]{:S(2)}) copy-start(s32[1,1,6]{2,1,0:T(1,128)} %param.28) | copy-start | bytes 76
  11.6 12.8 %copy-start.11 = (bf16[1,1,256,512]{3,2,1,0:T(8,128)(2,1)S(1)}, bf16[1,1,256,512]{3,2,1,0:T(8,128)(2,1)}, u32[]{:S(2)}) copy-start(bf16[1,1,256,512]{3,2,1,0:T(8,128)(2,1)} %param.23) | copy-start | bytes 786436
  11.6 12.9 %copy-start.1 = (bf16[1,1,256,512]{3,2,1,0:T(8,128)(2,1)S(1)}, bf16[1,1,256,512]{3,2,1,0:T(8,128)(2,1)}, u32[]{:S(2)}) copy-start(bf16[1,1,256,512]{3,2,1,0:T(8,128)(2,1)} %param.15) | copy-start | bytes 786436
  12.6 16.4 %collective-permute-start = (bf16[1,2,128,512]{3,2,1,0:T(8,128)(2,1)}, bf16[1,2,128,512]{3,2,1,0:T(8,128)(2,1)}, u32[]{:S(2)}, u32[]{:S(2)}) collective-permute-start(bf16[1,2,128,512]{3,2,1,0:T(8,128)(2,1)} %get-tuple-element.28), channel_id=1, source_target_pairs={{0,2},{2,4},{4,6},{6,8},{8,10},{10,12},{12,14},{14,16},{16,18},{18... | collective-permute-start | bytes 786440 | tf_op jit(solution)/shard_map/ppermute | solution.py:12
  18.1 12.7 %collective-permute-start.1 = (bf16[1,2,128,512]{3,2,1,0:T(8,128)(2,1)}, bf16[1,2,128,512]{3,2,1,0:T(8,128)(2,1)}, u32[]{:S(2)}, u32[]{:S(2)}) collective-permute-start(bf16[1,2,128,512]{3,2,1,0:T(8,128)(2,1)} %get-tuple-element.27), channel_id=1, source_target_pairs={{2,0},{4,2},{6,4},{8,6},{10,8},{12,10},{14,12},{16,14},{18,16},{20... | collective-permute-start | bytes 786440 | tf_op jit(solution)/shard_map/ppermute | solution.py:15
  19.4 12.4 %collective-permute-start.2 = (bf16[1,2,128,512]{3,2,1,0:T(8,128)(2,1)}, bf16[1,2,128,512]{3,2,1,0:T(8,128)(2,1)}, u32[]{:S(2)}, u32[]{:S(2)}) collective-permute-start(bf16[1,2,128,512]{3,2,1,0:T(8,128)(2,1)} %get-tuple-element.26), channel_id=1, source_target_pairs={{0,1},{2,3},{4,5},{6,7},{8,9},{10,11},{12,13},{14,15},{16,17},{18,... | collective-permute-start | bytes 786440 | tf_op jit(solution)/shard_map/ppermute | solution.py:12
  21.6 11.2 %collective-permute-start.3 = (bf16[1,2,128,512]{3,2,1,0:T(8,128)(2,1)}, bf16[1,2,128,512]{3,2,1,0:T(8,128)(2,1)}, u32[]{:S(2)}, u32[]{:S(2)}) collective-permute-start(bf16[1,2,128,512]{3,2,1,0:T(8,128)(2,1)} %get-tuple-element.25), channel_id=1, source_target_pairs={{1,0},{3,2},{5,4},{7,6},{9,8},{11,10},{13,12},{15,14},{17,16},{19,... | collective-permute-start | bytes 786440 | tf_op jit(solution)/shard_map/ppermute | solution.py:15
  24.1 218.4 %all-reduce.2.cloned.1.call-start = ((), (), s32[]{:S(2)}) async-start(), calls=%async_computation | async-start | bytes 14680064 | tf_op jit(solution)/shard_map/psum | solution.py:195
  33.8 3.3 %copy-start.26 = (f32[512]{0:T(512)S(1)}, f32[512]{0:T(512)}, u32[]{:S(2)}) copy-start(f32[512]{0:T(512)} %param.18) | copy-start | bytes 6148
  37.1 4.3 %copy-start.17 = (bf16[512,512]{1,0:T(8,128)(2,1)S(1)}, bf16[512,512]{1,0:T(8,128)(2,1)}, u32[]{:S(2)}) copy-start(bf16[512,512]{1,0:T(8,128)(2,1)} %param.19) | copy-start | bytes 1572868
  41.5 1.0 copy-start.9
  42.1 1.1 copy-start.2
  43.3 2.0 copy-start.14
  43.3 2.0 copy-start.25
  45.2 1.0 copy-start.24
  53.0 3.2 %copy-start.7 = (bf16[1,1,768,512]{3,2,1,0:T(8,128)(2,1)S(1)}, bf16[1,1,768,512]{3,2,1,0:T(8,128)(2,1)}, u32[]{:S(2)}) copy-start(bf16[1,1,768,512]{3,2,1,0:T(8,128)(2,1)} %param.24) | copy-start | bytes 2359300
  56.1 2.7 %copy-start.3 = (f32[768,512]{1,0:T(8,128)S(1)}, f32[768,512]{1,0:T(8,128)}, u32[]{:S(2)}) copy-start(f32[768,512]{1,0:T(8,128)} %copy-done.2) | copy-start | bytes 4718596
  56.1 2.8 %copy-start.4 = (f32[768,512]{1,0:T(8,128)S(1)}, f32[768,512]{1,0:T(8,128)}, u32[]{:S(2)}) copy-start(f32[768,512]{1,0:T(8,128)} %gather_fusion.3) | copy-start | bytes 4718596
  58.9 1.1 copy-start.10
  60.1 1.0 copy-start.18
  60.1 1.6 copy-start.27
  61.7 1.1 copy-start.15
  61.7 1.4 copy-start.16
  61.7 1.6 copy-start.23
  63.3 1.6 copy-start.6
  63.3 1.9 copy-start.13
  70.1 1.4 copy-start.8
  86.0 9.6 %copy-start.5 = (f32[768,512]{1,0:T(8,128)S(1)}, f32[768,512]{1,0:T(8,128)}, u32[]{:S(2)}) copy-start(f32[768,512]{1,0:T(8,128)} %get-tuple-element.13) | copy-start | bytes 4718596
  86.8 17.3 %collective-permute-start.4 = (bf16[1,2,128,512]{3,1,2,0:T(2,128)(2,1)S(1)}, bf16[1,2,128,512]{3,1,2,0:T(2,128)(2,1)S(1)}, u32[]{:S(2)}, u32[]{:S(2)}) collective-permute-start(bf16[1,2,128,512]{3,1,2,0:T(2,128)(2,1)S(1)} %get-tuple-element.15), channel_id=1, source_target_pairs={{0,2},{2,4},{4,6},{6,8},{8,10},{10,12},{12,14},{14,16},{16,18},{18... | collective-permute-start | bytes 786440 | tf_op jit(solution)/shard_map/ppermute | solution.py:12
  90.3 17.5 %collective-permute-start.5 = (bf16[1,2,128,512]{3,1,2,0:T(2,128)(2,1)S(1)}, bf16[1,2,128,512]{3,1,2,0:T(2,128)(2,1)S(1)}, u32[]{:S(2)}, u32[]{:S(2)}) collective-permute-start(bf16[1,2,128,512]{3,1,2,0:T(2,128)(2,1)S(1)} %get-tuple-element.18), channel_id=1, source_target_pairs={{2,0},{4,2},{6,4},{8,6},{10,8},{12,10},{14,12},{16,14},{18,16},{20... | collective-permute-start | bytes 786440 | tf_op jit(solution)/shard_map/ppermute | solution.py:15
  91.6 16.8 %collective-permute-start.6 = (bf16[1,2,128,512]{3,1,2,0:T(2,128)(2,1)S(1)}, bf16[1,2,128,512]{3,1,2,0:T(2,128)(2,1)S(1)}, u32[]{:S(2)}, u32[]{:S(2)}) collective-permute-start(bf16[1,2,128,512]{3,1,2,0:T(2,128)(2,1)S(1)} %get-tuple-element.17), channel_id=1, source_target_pairs={{0,1},{2,3},{4,5},{6,7},{8,9},{10,11},{12,13},{14,15},{16,17},{18,... | collective-permute-start | bytes 786440 | tf_op jit(solution)/shard_map/ppermute | solution.py:12
  94.1 14.3 %collective-permute-start.7 = (bf16[1,2,128,512]{3,1,2,0:T(2,128)(2,1)S(1)}, bf16[1,2,128,512]{3,1,2,0:T(2,128)(2,1)S(1)}, u32[]{:S(2)}, u32[]{:S(2)}) collective-permute-start(bf16[1,2,128,512]{3,1,2,0:T(2,128)(2,1)S(1)} %get-tuple-element.16), channel_id=1, source_target_pairs={{1,0},{3,2},{5,4},{7,6},{9,8},{11,10},{13,12},{15,14},{17,16},{19,... | collective-permute-start | bytes 786440 | tf_op jit(solution)/shard_map/ppermute | solution.py:15
  109.0 1.2 copy-start.20
  110.1 3.3 %copy-start.12 = (f32[256,512]{1,0:T(8,128)S(1)}, f32[256,512]{1,0:T(8,128)}, u32[]{:S(2)}) copy-start(f32[256,512]{1,0:T(8,128)} %get-tuple-element.24) | copy-start | bytes 1572868
Sparse Core Ops, SparseCore 0:
  24.2 2.3 sort.21.cloned.1.call-done
  (1 shorter events, 0.0 us)
Sparse Core Ops, SparseCore 1:
  68.6 173.8 all-reduce.1
where the time goes:
time: 271 us
  waiting for transfers between devices  140 us (52%)
  local copies, waits for them, and re-layouts  34.2 us (13%)
  other arithmetic  32 us (12%)
  matrix products  26.2 us (10%)
  starting transfers between devices  19.1 us (7%)
  between operations  18.9 us (7%)
    psum x1, waiting for transfers between devices, on_device(): summed = lax.psum(weight_grad, ('gx', 'gy'))  128 us
    ppermute x4, starting transfers between devices, padded(): lax.ppermute(lax.slice_in_dim(block, block.shape[dim] - width, None, axis...  13.7 us
    unnamed x64, local copies, waits for them, and re-layouts  9.38 us
    reduce_sum x3, other arithmetic, on_device(): pieces.append(matrix * lax.rsqrt(jnp.mean(matrix * matrix) + 1e-06))  8.52 us
    gather x1, local copies, waits for them, and re-layouts, on_device(): jnp.take_along_axis(grad_s.reshape(tile_count, block_size, feature), inve...  7.83 us
    ppermute x4, waiting for transfers between devices, padded(): lax.ppermute(lax.slice_in_dim(block, block.shape[dim] - width, None, axis...  7.47 us
    mul x3, other arithmetic, on_device(): pieces.append(matrix * lax.rsqrt(jnp.mean(matrix * matrix) + 1e-06))  5.99 us
    dot_general x4, matrix products, matmul(): return jnp.dot(factor, second, preferred_element_type=jnp.float32)  5.82 us
  transfers between devices with their start and end apart: 9, of which 5 were waited for; matrix products, arithmetic and copies ran while one was open for 13% of the time, Pallas kernels for 0%

commit v1 on v0

--- a/solution.py
+++ b/solution.py
@@ -1,7 +1,115 @@
+import functools
+
 import jax
 import jax.numpy as jnp
 from jax import lax
+from jax.experimental import pallas as pl
+from jax.experimental.pallas import tpu as pltpu
 from jax.sharding import PartitionSpec as P
+
+
+def swap(values, along_gx, along_gy):
+    n_gx, n_gy = lax.axis_size("gx"), lax.axis_size("gy")
+    pairs = []
+    for a in range(n_gx):
+        for b in range(n_gy):
+            target = (a ^ along_gx[b & 1]) * n_gy + (b ^ along_gy)
+            pairs.append((a * n_gy + b, target))
+    return lax.ppermute(values, ("gx", "gy"), pairs)
+
+
+def group_masks():
+    n_gx, n_gy = lax.axis_size("gx"), lax.axis_size("gy")
+    return [(a * 4, b * 2) for a in range(n_gx // 4) for b in range(n_gy // 2)]
+
+
+def piece_order(core, gx_index, gy_index):
+    n_gy = lax.axis_size("gy")
+    order = []
+    for first in range(2):
+        for second in range(2):
+            low = jnp.where(core == 0, first + 2 * second, 2 * first + second)
+            for mask_gx, mask_gy in group_masks():
+                order.append((gx_index ^ (low | mask_gx)) * n_gy + (gy_index ^ mask_gy))
+    return jnp.stack(order).astype(jnp.int32)
+
+
+def arrange_kernel(rows, index_ref, *refs):
+    parts, (send_ref, keep_ref, stacked) = refs[:-3], refs[-3:]
+    start = 0
+    for part in parts:
+        stacked[start : start + part.shape[0], :] = part[...]
+        start += part.shape[0]
+    count = keep_ref.shape[0]
+    for place in range(count):
+        own = pl.multiple_of(index_ref[0, place] * rows, 8)
+        keep_ref[place] = stacked[pl.ds(own, rows), :]
+        other = pl.multiple_of(index_ref[1, place] * rows, 8)
+        send_ref[place] = stacked[pl.ds(other, rows), :].astype(jnp.bfloat16)
+
+
+def arrange(parts, index, rows):
+    count = index.shape[1]
+    feature = parts[0].shape[1]
+    if rows % 16:
+        pieces = jnp.concatenate(parts, axis=0).reshape(2 * count, rows, feature)
+        return pieces[index[1]].astype(jnp.bfloat16), pieces[index[0]]
+    vmem = pl.BlockSpec(memory_space=pltpu.VMEM)
+    return pl.pallas_call(
+        functools.partial(arrange_kernel, rows),
+        out_shape=(
+            jax.ShapeDtypeStruct((count, rows, feature), jnp.bfloat16),
+            jax.ShapeDtypeStruct((count, rows, feature), jnp.float32),
+        ),
+        in_specs=[pl.BlockSpec(memory_space=pltpu.SMEM)] + [vmem] * len(parts),
+        out_specs=(vmem, vmem),
+        scratch_shapes=[pltpu.VMEM((2 * count * rows, feature), jnp.float32)],
+        compiler_params=pltpu.CompilerParams(vmem_limit_bytes=48 << 20),
+        name="arrange",
+    )(index, *parts)
+
+
+def scatter_sum(send, keep):
+    total = keep + swap(send, (0, 0), 1).astype(jnp.float32)
+    for masks in ((1, 2), (2, 1)):
+        total = total.reshape((2, total.shape[0] // 2) + total.shape[1:])
+        total = total[0] + swap(total[1].astype(jnp.bfloat16), masks, 0).astype(jnp.float32)
+    final = total[0]
+    for place, (mask_gx, mask_gy) in enumerate(group_masks()):
+        if place:
+            sent = total[place].astype(jnp.bfloat16)
+            final = final + swap(sent, (mask_gx, mask_gx), mask_gy).astype(jnp.float32)
+    return final
+
+
+def sum_everywhere(values):
+    bit = 1
+    while bit < lax.axis_size("gy"):
+        values = values + swap(values, (0, 0), bit)
+        bit *= 2
+    bit = 1
+    while bit < lax.axis_size("gx"):
+        values = values + swap(values, (bit, bit), 0)
+        bit *= 2
+    return values
+
+
+def directions(piece, piece_index, row_counts):
+    rows, feature = piece.shape
+    row_id = piece_index * rows + lax.broadcasted_iota(jnp.int32, (rows, 1), 0)
+    low = 0
+    inside = []
+    for count in row_counts:
+        inside.append(((row_id >= low) & (row_id < low + count)).astype(jnp.float32))
+        low += count
+    row_squares = jnp.sum(piece * piece, axis=1, keepdims=True)
+    squares = jnp.stack([jnp.sum(row_squares * mask) for mask in inside])
+    squares = sum_everywhere(jnp.broadcast_to(squares[:, None], (len(row_counts), 128)))
+    scale = jnp.zeros((rows, 1), jnp.float32)
+    for place, count in enumerate(row_counts):
+        inverse = lax.rsqrt(squares[place, 0] / (count * feature) + 1e-06)
+        scale = scale + inside[place] * inverse
+    return (piece * scale).astype(jnp.bfloat16).reshape(rows * feature)
 
 
 def padded(block, sides, width):
@@ -151,10 +259,9 @@
         times_transposed(grad_edge_linear, edge_w2) * silu_slope(edge_affine)
     ).astype(jnp.bfloat16)
     g_ew1 = inner_rows(joined, grad_edge_affine)
-    grad_joined = times_transposed(grad_edge_affine, edge_w1)
+    grad_joined = times_transposed(grad_edge_affine, edge_w1[: 2 * feature])
     grad_e = grad_joined[:, :feature]
     grad_r = grad_joined[:, feature : 2 * feature]
-    grad_s = grad_joined[:, 2 * feature :]
     edge_grad = (cot_edge.astype(jnp.float32) + grad_e).astype(jnp.bfloat16)
     grad_recv = jnp.einsum(
         "bt,tnf->bnf",
@@ -162,10 +269,16 @@
         grad_r.reshape(tile_count, block_size, feature),
         precision=lax.Precision.HIGHEST,
     )
-    inverse = jnp.argsort(perm_idx, axis=1)
-    grad_send = jnp.take_along_axis(
-        grad_s.reshape(tile_count, block_size, feature), inverse[:, :, None], axis=1
-    )
+    sender_hot = (perm_idx[:, :, None] == offsets[None, None, :]).astype(jnp.bfloat16)
+    grad_sender = jnp.einsum(
+        "tjn,tjf->tnf",
+        sender_hot,
+        grad_edge_affine.reshape(tile_count, block_size, feature),
+        preferred_element_type=jnp.float32,
+    ).astype(jnp.bfloat16)
+    grad_send = times_transposed(
+        grad_sender.reshape(tile_count * block_size, feature), edge_w1[2 * feature :]
+    ).reshape(tile_count, block_size, feature)
     extended_count = block_count + 4 * slot_count
     send_hot = (send_idx[None, :] == jnp.arange(extended_count, dtype=jnp.int32)[:, None]).astype(
         jnp.float32
@@ -189,18 +302,18 @@
         + contrib
     )
     node_grad = node_grad.astype(jnp.bfloat16).reshape(1, 1, node_count, feature)
-    weight_grad = jnp.concatenate([g_ew1, g_ew2, g_nw1, g_nw2], axis=0)
-    total_entries = 7 * feature * feature
-    share_len = total_entries // lax.axis_size(("gx", "gy"))
-    summed = lax.psum(weight_grad, ("gx", "gy"))
-    bounds = [0, 3 * feature, 4 * feature, 6 * feature, 7 * feature]
-    pieces = []
-    for index in range(4):
-        matrix = summed[bounds[index] : bounds[index + 1]]
-        pieces.append(matrix * lax.rsqrt(jnp.mean(matrix * matrix) + 1e-06))
-    normalized = jnp.concatenate(pieces, axis=0).reshape(total_entries)
-    own_start = lax.axis_index(("gx", "gy")) * share_len
-    weight_dir = lax.dynamic_slice_in_dim(normalized, own_start, share_len).astype(jnp.bfloat16)
+    weight_grads = (g_ew1, g_ew2, g_nw1, g_nw2)
+    row_counts = tuple(part.shape[0] for part in weight_grads)
+    gx_index, gy_index = lax.axis_index("gx"), lax.axis_index("gy")
+    device_count = lax.axis_size("gx") * lax.axis_size("gy")
+    rows = sum(row_counts) // device_count
+    core = gy_index & 1
+    index = jnp.stack(
+        [piece_order(core, gx_index, gy_index), piece_order(1 - core, gx_index, gy_index ^ 1)]
+    )
+    send, keep = arrange(weight_grads, index, rows)
+    piece = scatter_sum(send, keep)
+    weight_dir = directions(piece, gx_index * lax.axis_size("gy") + gy_index, row_counts)
     return (
         node_out.reshape(1, 1, node_count, feature),
         node_grad,

time: 271 us -> 140 us (0.52)
  waiting for transfers between devices: 140 us -> 21.9 us
  starting transfers between devices: 19.1 us -> 34.6 us
  between operations: 18.9 us -> 4.17 us
  other arithmetic: 32 us -> 19.7 us
  local copies, waits for them, and re-layouts: 34.2 us -> 26.1 us
  Pallas kernels: 0 us -> 5.21 us
    psum x1 -> x0, waiting for transfers between devices: 128 us -> none  [on_device(): summed = lax.psum(weight_grad, ('gx', 'gy'))]
    ppermute x0 -> x11, waiting for transfers between devices: none -> 16.8 us  [swap(): return lax.ppermute(values, ('gx', 'gy'), pairs)]
    ppermute x0 -> x11, starting transfers between devices: none -> 14.8 us  [swap(): return lax.ppermute(values, ('gx', 'gy'), pairs)]
    gather x1 -> x0, local copies, waits for them, and re-layouts: 7.83 us -> none  [on_device(): jnp.take_along_axis(grad_s.reshape(tile_count, block_size, feature), inve...]
    reduce_sum x3 -> x2, other arithmetic: 8.52 us -> 0.83 us  [the longest x1 0.68 us: directions(): squares = jnp.stack([jnp.sum(row_squares * mask) for mask in inside])]
    mul x3 -> x0, other arithmetic: 5.99 us -> none  [on_device(): pieces.append(matrix * lax.rsqrt(jnp.mean(matrix * matrix) + 1e-06))]
    pallas_call x0 -> x1, Pallas kernels: none -> 5.21 us  [arrange(): pl.pallas_call(functools.partial(arrange_kernel, rows), out_shape=(jax.Sh...]
    add x0 -> x8, other arithmetic: none -> 4.36 us  [the longest x1 2.69 us: scatter_sum(): total = keep + swap(send, (0, 0), 1).astype(jnp.float32)]
  transfers between devices with their start and end apart: 9 -> 19, of which waited for: 5 -> 9; matrix products, arithmetic and copies ran while one was open for 13% -> 20% of each run, Pallas kernels for 0% -> 0%
where the time goes in v1:
time: 140 us; the launch traced here: 139 us
  starting transfers between devices  34.6 us (25%)
  matrix products  27.2 us (19%)
  local copies, waits for them, and re-layouts  26.1 us (19%)
  waiting for transfers between devices  21.9 us (16%)
  other arithmetic  19.7 us (14%)
  Pallas kernels  5.21 us (4%)
  between operations  4.17 us (3%)
    ppermute x11, waiting for transfers between devices, swap(): return lax.ppermute(values, ('gx', 'gy'), pairs)  16.8 us
    ppermute x11, starting transfers between devices, swap(): return lax.ppermute(values, ('gx', 'gy'), pairs)  14.8 us
    ppermute x4, starting transfers between devices, padded(): lax.ppermute(lax.slice_in_dim(block, block.shape[dim] - width, None, axis...  14.7 us
    unnamed x69, local copies, waits for them, and re-layouts  8.95 us
    dot_general x4, matrix products, matmul(): return jnp.dot(factor, second, preferred_element_type=jnp.float32)  6.34 us
    dot_general x5, matrix products, times_transposed(): lax.dot_general(factor, second, (((1,), (1,)), ((), ())), preferred_eleme...  5.94 us
    pallas_call x1, Pallas kernels, arrange(): pl.pallas_call(functools.partial(arrange_kernel, rows), out_shape=(jax.Sh...  5.21 us
    ppermute x4, starting transfers between devices, padded(): lax.ppermute(lax.slice_in_dim(block, 0, width, axis=dim), axis, backward)  5.16 us
  transfers between devices with their start and end apart: 19, of which 9 were waited for; matrix products, arithmetic and copies ran while one was open for 20% of the time, Pallas kernels for 0%

profile of v1, /device:TPU:0, one launch (start us, length us, event | category | flops | bytes accessed | tf_op | source)
XLA Modules:
  0.0 138.9 jit_solution(17390040079110935913)
XLA Ops:
  2.4 1.6 %gather_fusion.1 = bf16[8,128,512]{2,1,0:T(8,128)(2,1)S(1)} fusion(bf16[2,128,512]{2,1,0:T(8,128)(2,1)} %bitcast.184, s32[1024]{0:T(1024)S(1)} %pad_clamp_fusion.1), kind=kCustom, calls=%fused_computation.1 | custom fusion | bytes 2097184 | tf_op jit(solution)/shard_map/gather | solution.py:214
  4.2 1.0 fusion.68
  5.1 5.6 %collective-permute-start = (bf16[1,2,128,512]{3,2,1,0:T(8,128)(2,1)}, bf16[1,2,128,512]{3,2,1,0:T(8,128)(2,1)}, u32[]{:S(2)}, u32[]{:S(2)}) collective-permute-start(bf16[1,2,128,512]{3,2,1,0:T(8,128)(2,1)} %get-tuple-element.31), channel_id=1, source_target_pairs={{0,2},{2,4},{4,6},{6,8},{8,10},{10,12},{12,14},{14,16},{16,18},{18... | collective-permute-start | bytes 786440 | tf_op jit(solution)/shard_map/ppermute | solution.py:120
  10.7 1.3 collective-permute-start.1
  12.0 1.5 %collective-permute-start.2 = (bf16[1,2,128,512]{3,2,1,0:T(8,128)(2,1)}, bf16[1,2,128,512]{3,2,1,0:T(8,128)(2,1)S(1)}, u32[]{:S(2)}, u32[]{:S(2)}) collective-permute-start(bf16[1,2,128,512]{3,2,1,0:T(8,128)(2,1)} %get-tuple-element.29), channel_id=1, source_target_pairs={{0,1},{2,3},{4,5},{6,7},{8,9},{10,11},{12,13},{14,15},{16,17},{18,... | collective-permute-start | bytes 786440 | tf_op jit(solution)/shard_map/ppermute | solution.py:120
  13.5 1.3 collective-permute-start.3
  15.5 3.3 %gather_fusion = bf16[768,512]{1,0:T(8,128)(2,1)} fusion(bf16[256,512]{1,0:T(8,128)(2,1)S(1)} %bitcast.186, s32[1024]{0:T(1024)S(1)} %get-tuple-element.50), kind=kCustom, calls=%fused_computation | custom fusion | bytes 1575936 | tf_op jit(solution)/shard_map/gather | solution.py:219
  18.8 2.7 %collective-permute-done = bf16[1,2,128,512]{3,2,1,0:T(8,128)(2,1)} collective-permute-done((bf16[1,2,128,512]{3,2,1,0:T(8,128)(2,1)}, bf16[1,2,128,512]{3,2,1,0:T(8,128)(2,1)}, u32[]{:S(2)}, u32[]{:S(2)}) %collective-permute-start) | collective-permute-done | bytes 262176 | tf_op jit(solution)/shard_map/ppermute | solution.py:120
  21.5 1.0 bitcast_dynamic-update-slice_fusion.3
  22.5 0.9 collective-permute-done.1
  23.4 1.0 bitcast_dynamic-update-slice_fusion.2
  24.5 3.3 %gather_fusion.2 = bf16[768,512]{1,0:T(8,128)(2,1)} fusion(bf16[1280,512]{1,0:T(8,128)(2,1)S(1)} %bitcast.189, s32[1024]{0:T(1024)S(1)} %get-tuple-element.49), kind=kCustom, calls=%fused_computation.2 | custom fusion | bytes 1575936 | tf_op jit(solution)/shard_map/gather | solution.py:222
  27.8 4.8 %multiply_convert_fusion.2 = (bf16[768,512]{1,0:T(8,128)(2,1)S(1)}, f32[768,512]{1,0:T(8,128)}) fusion(f32[512]{0:T(512)S(1)} %copy-done.29, bf16[1536,512]{1,0:T(8,128)(2,1)} %param.17, bf16[768,512]{1,0:T(8,128)(2,1)} %gather_fusion.2, bf16[768,512]{1,0:T(8,128)(2,1)} %gather_fusion, bf16[768,512]{1,0:T(8,128)(2,1)} %bitcast.207), kind=kOutput, calls=%fused_computation.24 | convolution fusion | flops 1217396736 | bytes 6293504 | tf_op jit(solution)/shard_map/dot_general | solution.py:160
  34.5 1.9 %fusion.14 = bf16[2,128,512]{2,0,1:T(2,128)(2,1)S(1)} fusion(f32[6,128,512]{2,1,0:T(8,128)S(1)} %bitcast.190, s32[6]{0:T(128)S(1)} %bitcast.204), kind=kOutput, calls=%fused_computation.33 | convolution fusion | flops 9568268 | bytes 1835032 | tf_op jit(solution)/shard_map/bt,tnf->bnf/dot_general | solution.py:231
  38.1 0.9 fusion.31
  41.4 1.1 fusion.67
  42.5 4.5 %gather_fusion.3 = f32[768,512]{1,0:T(8,128)} fusion(f32[256,512]{1,0:T(8,128)} %get-tuple-element.26, s32[1024]{0:T(1024)S(1)} %get-tuple-element.50), kind=kCustom, calls=%fused_computation.3 | custom fusion | bytes 3148800 | tf_op jit(solution)/shard_map/gather | solution.py:255
  47.0 2.9 %fusion.22 = (f32[768]{0:T(1024)S(1)}, f32[768]{0:T(1024)S(1)}) fusion(f32[768,512]{1,0:T(8,128)} %gather_fusion.3, bf16[1,1,768,512]{3,2,1,0:T(8,128)(2,1)} %param.24, f32[768]{0:T(1024)S(1)} %add_rsqrt_fusion, f32[768,512]{1,0:T(8,128)} %copy-done.3, f32[768]{0:T(1024)S(1)} %broadcast_multiply_fusion.2), kind=kLoop, calls=%fused_computation.42 | loop fusion | flops 2750976 | bytes 3944448 | tf_op jit(solution)/shard_map/reduce_sum | solution.py:142
  53.0 0.9 multiply_convert_fusion
  53.9 0.9 copy-done.10
  54.8 3.1 %fusion.19.refs_0_ = f32[1536,512]{1,0:T(8,128)} fusion(bf16[768,512]{1,0:T(8,128)(2,1)S(1)} %multiply_convert_fusion, bf16[768,512]{1,0:T(8,128)(2,1)S(1)} %copy-done.19, bf16[768,512]{1,0:T(8,128)(2,1)S(1)} %copy-done.18, bf16[768,512]{1,0:T(8,128)(2,1)S(1)} %bitcast.208), kind=kOutput, calls=%fused_computation.37 | convolution fusion | flops 1215037440 | bytes 6291456 | tf_op jit(solution)/shard_map/dot_general | solution.py:148
  58.0 5.2 %arrange.1 = (bf16[16,112,512]{2,1,0:T(8,128)(2,1)}, f32[16,112,512]{2,1,0:T(8,128)}) custom-call(s32[2,16]{1,0:T(2,128)S(1)} %pad_add_fusion.index_ref, f32[1536,512]{1,0:T(8,128)} %fusion.19.refs_0_, f32[512,512]{1,0:T(8,128)S(1)} %fusion.74.refs_1_, f32[1024,512]{1,0:T(8,128)S(1)} %fusion.33.refs_2_, f32[512,512]{1,0:T(8,128)S(1)} %fusion.62.refs_3_), custom_call_target="tpu_custom_call" | custom-call | tf_op jit(solution)/shard_map/arrange/pallas_call | solution.py:58
  63.2 4.0 %collective-permute-done.8 = bf16[16,112,512]{2,1,0:T(8,128)(2,1)S(1)} collective-permute-done((bf16[16,112,512]{2,1,0:T(8,128)(2,1)}, bf16[16,112,512]{2,1,0:T(8,128)(2,1)S(1)}, u32[]{:S(2)}, u32[]{:S(2)}) %collective-permute-start.8) | collective-permute-done | bytes 1835040 | tf_op jit(solution)/shard_map/ppermute | solution.py:18
  67.2 2.7 %convert_add_fusion = f32[16,112,512]{2,1,0:T(8,128)S(1)} fusion(f32[16,112,512]{2,1,0:T(8,128)} %get-tuple-element.6, bf16[16,112,512]{2,1,0:T(8,128)(2,1)S(1)} %collective-permute-done.8), kind=kLoop, calls=%fused_computation.4 | loop fusion | flops 1835008 | bytes 9175040 | tf_op jit(solution)/shard_map/add | solution.py:73
  69.9 1.8 %copy-done.6 = f32[16,112,512]{2,1,0:T(8,128)} copy-done((f32[16,112,512]{2,1,0:T(8,128)}, f32[16,112,512]{2,1,0:T(8,128)S(1)}, u32[]{:S(2)}) %copy-start.6) | copy-done | bytes 3670040
  71.8 1.6 %collective-permute-start.9 = (bf16[8,112,512]{2,1,0:T(8,128)(2,1)S(1)}, bf16[8,112,512]{2,1,0:T(8,128)(2,1)}, u32[]{:S(2)}, u32[]{:S(2)}) collective-permute-start(bf16[8,112,512]{2,1,0:T(8,128)(2,1)S(1)} %slice.222), channel_id=1, source_target_pairs={{0,2},{1,5},{2,0},{3,7},{4,6},{5,1},{6,4},{7,3},{8,10},{9,13},{10,... | collective-permute-start | bytes 2752520 | tf_op jit(solution)/shard_map/ppermute | solution.py:18
  73.4 1.9 %fusion.9 = f32[6,128,512]{2,1,0:T(8,128)S(1)} fusion(bf16[6,128,512]{2,1,0:T(8,128)(2,1)S(1)} %bitcast.193, bf16[1536,512]{1,0:T(8,128)(2,1)} %param.17, s32[6,128]{1,0:T(8,128)S(1)} %bitcast.200), kind=kOutput, calls=%fused_computation.28 | convolution fusion | flops 503808000 | bytes 2886656 | tf_op jit(solution)/shard_map/dot_general | solution.py:154
  75.2 2.2 %fusion.17 = f32[768,1024]{1,0:T(8,128)S(1)} fusion(bf16[768,512]{1,0:T(8,128)(2,1)S(1)} %copy-done.11, bf16[1536,512]{1,0:T(8,128)(2,1)} %param.17), kind=kOutput, calls=%fused_computation.34 | convolution fusion | flops 805306368 | bytes 4980736 | tf_op jit(solution)/shard_map/dot_general | solution.py:154
  77.5 2.9 %fusion.72 = (bf16[10,128,512]{2,0,1:T(8,128)(2,1)S(1)}, f32[10,128,512]{2,0,1:T(8,128)S(1)}) fusion(f32[6,128,512]{2,1,0:T(8,128)S(1)} %fusion.9, s32[6]{0:T(128)S(1)} %bitcast.206), kind=kOutput, calls=%fused_computation.158 | convolution fusion | flops 47841340 | bytes 5505048 | tf_op jit(solution)/shard_map/bt,tnf->bnf/dot_general | solution.py:286
  80.4 4.9 %collective-permute-done.9 = bf16[8,112,512]{2,1,0:T(8,128)(2,1)} collective-permute-done((bf16[8,112,512]{2,1,0:T(8,128)(2,1)S(1)}, bf16[8,112,512]{2,1,0:T(8,128)(2,1)}, u32[]{:S(2)}, u32[]{:S(2)}) %collective-permute-start.9) | collective-permute-done | bytes 917536 | tf_op jit(solution)/shard_map/ppermute | solution.py:18
  85.4 1.5 %slice_add_fusion = f32[8,112,512]{2,1,0:T(8,128)S(1)} fusion(f32[16,112,512]{2,1,0:T(8,128)S(1)} %copy-done.7, bf16[8,112,512]{2,1,0:T(8,128)(2,1)} %collective-permute-done.9), kind=kLoop, calls=%fused_computation.18 | loop fusion | flops 917504 | bytes 4587520 | tf_op jit(solution)/shard_map/add | solution.py:76
  87.0 1.3 fusion.21
  89.2 6.3 %collective-permute-done.10 = bf16[4,112,512]{2,1,0:T(8,128)(2,1)S(1)} collective-permute-done((bf16[4,112,512]{2,1,0:T(8,128)(2,1)S(1)}, bf16[4,112,512]{2,1,0:T(8,128)(2,1)S(1)}, u32[]{:S(2)}, u32[]{:S(2)}) %collective-permute-start.10) | collective-permute-done | bytes 458784 | tf_op jit(solution)/shard_map/ppermute | solution.py:18
  95.7 3.7 %collective-permute-start.13 = (bf16[112,512]{1,0:T(8,128)(2,1)S(1)}, bf16[112,512]{1,0:T(8,128)(2,1)S(1)}, u32[]{:S(2)}, u32[]{:S(2)}) collective-permute-start(bf16[112,512]{1,0:T(8,128)(2,1)S(1)} %get-tuple-element.35), channel_id=1, source_target_pairs={{0,24},{1,25},{2,26},{3,27},{4,28},{5,29},{6,30},{7,31},{8,16},{9,... | collective-permute-start | bytes 344072 | tf_op jit(solution)/shard_map/ppermute | solution.py:18
  100.2 2.1 %fusion.2 = f32[2,128,512]{2,0,1:T(2,128)S(1)} fusion(f32[6,128,512]{2,1,0:T(8,128)S(1)} %bitcast.191, s32[6]{0:T(128)S(1)} %bitcast.205), kind=kOutput, calls=%fused_computation.9 | convolution fusion | flops 9437196 | bytes 2097176 | tf_op jit(solution)/shard_map/bt,tnf->bnf/dot_general | solution.py:266
  102.5 1.3 collective-permute-start.7
  103.8 3.1 %collective-permute-start.6 = (bf16[1,2,128,512]{3,1,2,0:T(2,128)(2,1)S(1)}, bf16[1,2,128,512]{3,1,2,0:T(2,128)(2,1)S(1)}, u32[]{:S(2)}, u32[]{:S(2)}) collective-permute-start(bf16[1,2,128,512]{3,1,2,0:T(2,128)(2,1)S(1)} %get-tuple-element.20), channel_id=1, source_target_pairs={{0,1},{2,3},{4,5},{6,7},{8,9},{10,11},{12,13},{14,15},{16,17},{18,... | collective-permute-start | bytes 786440 | tf_op jit(solution)/shard_map/ppermute | solution.py:120
  106.8 1.3 collective-permute-start.5
  108.1 4.6 %collective-permute-start.4 = (bf16[1,2,128,512]{3,1,2,0:T(2,128)(2,1)S(1)}, bf16[1,2,128,512]{3,1,2,0:T(2,128)(2,1)S(1)}, u32[]{:S(2)}, u32[]{:S(2)}) collective-permute-start(bf16[1,2,128,512]{3,1,2,0:T(2,128)(2,1)S(1)} %get-tuple-element.18), channel_id=1, source_target_pairs={{0,2},{2,4},{4,6},{6,8},{8,10},{10,12},{12,14},{14,16},{16,18},{18... | collective-permute-start | bytes 786440 | tf_op jit(solution)/shard_map/ppermute | solution.py:120
  113.5 2.6 %pad_maximum_fusion.13 = f32[4]{0:T(128)S(1)} fusion(f32[1]{0:T(128)} %bitcast.78, f32[1]{0:T(128)} %bitcast.77, f32[1]{0:T(128)} %bitcast.76, f32[1]{0:T(128)} %bitcast.75), kind=kLoop, calls=%fused_computation.132 | loop fusion | flops 12 | bytes 32 | tf_op jit(solution)/shard_map/stack | solution.py:106
  117.5 2.4 %collective-permute-start.15 = (f32[4,128]{1,0:T(4,128)S(1)}, f32[4,128]{1,0:T(4,128)S(1)}, u32[]{:S(2)}, u32[]{:S(2)}) collective-permute-start(f32[4,128]{1,0:T(4,128)S(1)} %broadcast_add_fusion), channel_id=1, source_target_pairs={{0,2},{1,3},{2,0},{3,1},{4,6},{5,7},{6,4},{7,5},{8,10},{9,11},{10,... | collective-permute-start | bytes 6152 | tf_op jit(solution)/shard_map/ppermute | solution.py:18
  119.9 1.5 %collective-permute-done.4 = bf16[1,2,128,512]{3,1,2,0:T(2,128)(2,1)S(1)} collective-permute-done((bf16[1,2,128,512]{3,1,2,0:T(2,128)(2,1)S(1)}, bf16[1,2,128,512]{3,1,2,0:T(2,128)(2,1)S(1)}, u32[]{:S(2)}, u32[]{:S(2)}) %collective-permute-start.4) | collective-permute-done | bytes 262176 | tf_op jit(solution)/shard_map/ppermute | solution.py:120
  122.0 2.1 %collective-permute-start.16 = (f32[4,128]{1,0:T(4,128)S(1)}, f32[4,128]{1,0:T(4,128)S(1)}, u32[]{:S(2)}, u32[]{:S(2)}) collective-permute-start(f32[4,128]{1,0:T(4,128)S(1)} %fusion.91), channel_id=1, source_target_pairs={{0,4},{1,5},{2,6},{3,7},{4,0},{5,1},{6,2},{7,3},{8,12},{9,13},{10,... | collective-permute-start | bytes 6152 | tf_op jit(solution)/shard_map/ppermute | solution.py:18
  124.1 1.1 pad_maximum_fusion.1
  125.7 1.2 collective-permute-start.17
  126.9 3.2 %fusion.10 = f32[2,128,512]{2,0,1:T(2,128)S(1)} fusion(f32[4,2,128,512]{3,1,2,0:T(2,128)S(1)} %pad_maximum_fusion.1, pred[4,2]{0,1:T(4,128)(4,1)S(1)} %iota_compare_fusion.4, s32[4,2]{0,1:T(2,128)S(1)} %bitcast.201), kind=kOutput, calls=%fused_computation.30 | convolution fusion | flops 12582944 | bytes 2621480 | tf_op jit(solution)/shard_map/qsb,qsnf->bnf/dot_general | solution.py:298
  130.2 3.0 %collective-permute-start.18 = (f32[4,128]{1,0:T(4,128)S(1)}, f32[4,128]{1,0:T(4,128)S(1)}, u32[]{:S(2)}, u32[]{:S(2)}) collective-permute-start(f32[4,128]{1,0:T(4,128)S(1)} %add.413), channel_id=1, source_target_pairs={{0,16},{1,17},{2,18},{3,19},{4,20},{5,21},{6,22},{7,23},{8,24},{9,... | collective-permute-start | bytes 6152 | tf_op jit(solution)/shard_map/ppermute | solution.py:18
  133.2 1.0 fusion.26
  (141 shorter events, 18.9 us)
Async XLA Ops:
  0.6 35.8 %copy-start = (bf16[1024,512]{1,0:T(8,128)(2,1)S(1)}, bf16[1024,512]{1,0:T(8,128)(2,1)}, u32[]{:S(2)}) copy-start(bf16[1024,512]{1,0:T(8,128)(2,1)} %param.20) | copy-start | bytes 3145732
  4.1 10.7 %copy-start.25 = (s32[1,1,6]{2,1,0:T(1,128)S(1)}, s32[1,1,6]{2,1,0:T(1,128)}, u32[]{:S(2)}) copy-start(s32[1,1,6]{2,1,0:T(1,128)} %param.28) | copy-start | bytes 76
  4.1 10.8 %copy-start.24 = (s32[1,1,6]{2,1,0:T(1,128)S(1)}, s32[1,1,6]{2,1,0:T(1,128)}, u32[]{:S(2)}) copy-start(s32[1,1,6]{2,1,0:T(1,128)} %param.27) | copy-start | bytes 76
  4.1 10.8 %copy-start.14 = (bf16[1,1,256,512]{3,2,1,0:T(8,128)(2,1)S(1)}, bf16[1,1,256,512]{3,2,1,0:T(8,128)(2,1)}, u32[]{:S(2)}) copy-start(bf16[1,1,256,512]{3,2,1,0:T(8,128)(2,1)} %param.23) | copy-start | bytes 786436
  4.1 11.0 %copy-start.22 = (s32[1,1,6,128]{3,1,2,0:T(1,128)S(1)}, s32[1,1,6,128]{3,1,2,0:T(1,128)}, u32[]{:S(2)}) copy-start(s32[1,1,6,128]{3,1,2,0:T(1,128)} %param.29) | copy-start | bytes 9220
  4.1 11.3 %copy-start.2 = (bf16[1,1,256,512]{3,2,1,0:T(8,128)(2,1)S(1)}, bf16[1,1,256,512]{3,2,1,0:T(8,128)(2,1)}, u32[]{:S(2)}) copy-start(bf16[1,1,256,512]{3,2,1,0:T(8,128)(2,1)} %param.15) | copy-start | bytes 786436
  5.1 16.4 %collective-permute-start = (bf16[1,2,128,512]{3,2,1,0:T(8,128)(2,1)}, bf16[1,2,128,512]{3,2,1,0:T(8,128)(2,1)}, u32[]{:S(2)}, u32[]{:S(2)}) collective-permute-start(bf16[1,2,128,512]{3,2,1,0:T(8,128)(2,1)} %get-tuple-element.31), channel_id=1, source_target_pairs={{0,2},{2,4},{4,6},{6,8},{8,10},{10,12},{12,14},{14,16},{16,18},{18... | collective-permute-start | bytes 786440 | tf_op jit(solution)/shard_map/ppermute | solution.py:120
  10.7 12.7 %collective-permute-start.1 = (bf16[1,2,128,512]{3,2,1,0:T(8,128)(2,1)}, bf16[1,2,128,512]{3,2,1,0:T(8,128)(2,1)}, u32[]{:S(2)}, u32[]{:S(2)}) collective-permute-start(bf16[1,2,128,512]{3,2,1,0:T(8,128)(2,1)} %get-tuple-element.30), channel_id=1, source_target_pairs={{2,0},{4,2},{6,4},{8,6},{10,8},{12,10},{14,12},{16,14},{18,16},{20... | collective-permute-start | bytes 786440 | tf_op jit(solution)/shard_map/ppermute | solution.py:123
  12.0 12.4 %collective-permute-start.2 = (bf16[1,2,128,512]{3,2,1,0:T(8,128)(2,1)}, bf16[1,2,128,512]{3,2,1,0:T(8,128)(2,1)S(1)}, u32[]{:S(2)}, u32[]{:S(2)}) collective-permute-start(bf16[1,2,128,512]{3,2,1,0:T(8,128)(2,1)} %get-tuple-element.29), channel_id=1, source_target_pairs={{0,1},{2,3},{4,5},{6,7},{8,9},{10,11},{12,13},{14,15},{16,17},{18,... | collective-permute-start | bytes 786440 | tf_op jit(solution)/shard_map/ppermute | solution.py:120
  13.5 11.0 %collective-permute-start.3 = (bf16[1,2,128,512]{3,2,1,0:T(8,128)(2,1)}, bf16[1,2,128,512]{3,2,1,0:T(8,128)(2,1)S(1)}, u32[]{:S(2)}, u32[]{:S(2)}) collective-permute-start(bf16[1,2,128,512]{3,2,1,0:T(8,128)(2,1)} %get-tuple-element.28), channel_id=1, source_target_pairs={{1,0},{3,2},{5,4},{7,6},{9,8},{11,10},{13,12},{15,14},{17,16},{19,... | collective-permute-start | bytes 786440 | tf_op jit(solution)/shard_map/ppermute | solution.py:123
  24.5 3.3 %copy-start.29 = (f32[512]{0:T(512)S(1)}, f32[512]{0:T(512)}, u32[]{:S(2)}) copy-start(f32[512]{0:T(512)} %param.18) | copy-start | bytes 6148
  27.8 4.9 %copy-start.20 = (bf16[512,512]{1,0:T(8,128)(2,1)S(1)}, bf16[512,512]{1,0:T(8,128)(2,1)}, u32[]{:S(2)}) copy-start(bf16[512,512]{1,0:T(8,128)(2,1)} %param.19) | copy-start | bytes 1572868
  32.7 1.0 copy-start.12
  33.3 1.1 copy-start.3
  34.5 2.0 %copy-start.28 = (f32[512]{0:T(512)S(1)}, f32[512]{0:T(512)}, u32[]{:S(2)}) copy-start(f32[512]{0:T(512)} %param.21) | copy-start | bytes 6148
  36.4 1.0 copy-start.27
  47.0 3.0 %copy-start.4 = (f32[768,512]{1,0:T(8,128)S(1)}, f32[768,512]{1,0:T(8,128)}, u32[]{:S(2)}) copy-start(f32[768,512]{1,0:T(8,128)} %copy-done.3) | copy-start | bytes 4718596
  47.0 3.1 %copy-start.5 = (f32[768,512]{1,0:T(8,128)S(1)}, f32[768,512]{1,0:T(8,128)}, u32[]{:S(2)}) copy-start(f32[768,512]{1,0:T(8,128)} %gather_fusion.3) | copy-start | bytes 4718596
  47.0 3.3 %copy-start.8 = (bf16[1,1,768,512]{3,2,1,0:T(8,128)(2,1)S(1)}, bf16[1,1,768,512]{3,2,1,0:T(8,128)(2,1)}, u32[]{:S(2)}) copy-start(bf16[1,1,768,512]{3,2,1,0:T(8,128)(2,1)} %param.24) | copy-start | bytes 2359300
  50.3 1.1 copy-start.13
  51.4 1.0 copy-start.21
  51.4 1.6 %copy-start.30 = (f32[768,512]{1,0:T(8,128)S(1)}, f32[768,512]{1,0:T(8,128)}, u32[]{:S(2)}) copy-start(f32[768,512]{1,0:T(8,128)} %get-tuple-element.42) | copy-start | bytes 4718596
  53.0 1.8 %copy-start.18 = (bf16[768,512]{1,0:T(8,128)(2,1)S(1)}, bf16[768,512]{1,0:T(8,128)(2,1)}, u32[]{:S(2)}) copy-start(bf16[768,512]{1,0:T(8,128)(2,1)} %gather_fusion) | copy-start | bytes 2359300
  53.0 1.8 %copy-start.19 = (bf16[768,512]{1,0:T(8,128)(2,1)S(1)}, bf16[768,512]{1,0:T(8,128)(2,1)}, u32[]{:S(2)}) copy-start(bf16[768,512]{1,0:T(8,128)(2,1)} %gather_fusion.2) | copy-start | bytes 2359300
  53.0 1.8 %copy-start.26 = (bf16[1,1,768,512]{3,2,1,0:T(8,128)(2,1)S(1)}, bf16[1,1,768,512]{3,2,1,0:T(8,128)(2,1)}, u32[]{:S(2)}) copy-start(bf16[1,1,768,512]{3,2,1,0:T(8,128)(2,1)} %param.16) | copy-start | bytes 2359300
  63.2 4.0 %collective-permute-start.8 = (bf16[16,112,512]{2,1,0:T(8,128)(2,1)}, bf16[16,112,512]{2,1,0:T(8,128)(2,1)S(1)}, u32[]{:S(2)}, u32[]{:S(2)}) collective-permute-start(bf16[16,112,512]{2,1,0:T(8,128)(2,1)} %get-tuple-element.7), channel_id=1, source_target_pairs={{0,1},{1,0},{2,3},{3,2},{4,5},{5,4},{6,7},{7,6},{8,9},{9,8},{10,11... | collective-permute-start | bytes 5505032 | tf_op jit(solution)/shard_map/ppermute | solution.py:18
  69.9 1.8 %copy-start.6 = (f32[16,112,512]{2,1,0:T(8,128)}, f32[16,112,512]{2,1,0:T(8,128)S(1)}, u32[]{:S(2)}) copy-start(f32[16,112,512]{2,1,0:T(8,128)S(1)} %convert_add_fusion) | copy-start | bytes 11010052
  71.7 1.7 %copy-start.11 = (bf16[768,512]{1,0:T(8,128)(2,1)S(1)}, bf16[768,512]{1,0:T(8,128)(2,1)}, u32[]{:S(2)}) copy-start(bf16[768,512]{1,0:T(8,128)(2,1)} %copy-done.10) | copy-start | bytes 2359300
  71.8 13.6 %collective-permute-start.9 = (bf16[8,112,512]{2,1,0:T(8,128)(2,1)S(1)}, bf16[8,112,512]{2,1,0:T(8,128)(2,1)}, u32[]{:S(2)}, u32[]{:S(2)}) collective-permute-start(bf16[8,112,512]{2,1,0:T(8,128)(2,1)S(1)} %slice.222), channel_id=1, source_target_pairs={{0,2},{1,5},{2,0},{3,7},{4,6},{5,1},{6,4},{7,3},{8,10},{9,13},{10,... | collective-permute-start | bytes 2752520 | tf_op jit(solution)/shard_map/ppermute | solution.py:18
  77.5 7.9 %copy-start.7 = (f32[16,112,512]{2,1,0:T(8,128)S(1)}, f32[16,112,512]{2,1,0:T(8,128)}, u32[]{:S(2)}) copy-start(f32[16,112,512]{2,1,0:T(8,128)} %copy-done.6) | copy-start | bytes 11010052
  80.4 6.6 %copy-start.9 = (bf16[1,1,768,512]{3,2,1,0:T(8,128)(2,1)S(1)}, bf16[1,1,768,512]{3,2,1,0:T(8,128)(2,1)}, u32[]{:S(2)}) copy-start(bf16[1,1,768,512]{3,2,1,0:T(8,128)(2,1)} %param.24) | copy-start | bytes 2359300
  86.9 8.5 %collective-permute-start.10 = (bf16[4,112,512]{2,1,0:T(8,128)(2,1)S(1)}, bf16[4,112,512]{2,1,0:T(8,128)(2,1)S(1)}, u32[]{:S(2)}, u32[]{:S(2)}) collective-permute-start(bf16[4,112,512]{2,1,0:T(8,128)(2,1)S(1)} %slice.223), channel_id=1, source_target_pairs={{0,4},{1,3},{2,6},{3,1},{4,0},{5,7},{6,2},{7,5},{8,12},{9,11},{10,... | collective-permute-start | bytes 1376264 | tf_op jit(solution)/shard_map/ppermute | solution.py:18
  95.7 11.1 %collective-permute-start.13 = (bf16[112,512]{1,0:T(8,128)(2,1)S(1)}, bf16[112,512]{1,0:T(8,128)(2,1)S(1)}, u32[]{:S(2)}, u32[]{:S(2)}) collective-permute-start(bf16[112,512]{1,0:T(8,128)(2,1)S(1)} %get-tuple-element.35), channel_id=1, source_target_pairs={{0,24},{1,25},{2,26},{3,27},{4,28},{5,29},{6,30},{7,31},{8,16},{9,... | collective-permute-start | bytes 344072 | tf_op jit(solution)/shard_map/ppermute | solution.py:18
  99.4 8.8 %collective-permute-start.12 = (bf16[112,512]{1,0:T(8,128)(2,1)S(1)}, bf16[112,512]{1,0:T(8,128)(2,1)S(1)}, u32[]{:S(2)}, u32[]{:S(2)}) collective-permute-start(bf16[112,512]{1,0:T(8,128)(2,1)S(1)} %get-tuple-element.36), channel_id=1, source_target_pairs={{0,16},{1,17},{2,18},{3,19},{4,20},{5,21},{6,22},{7,23},{8,24},{9,... | collective-permute-start | bytes 344072 | tf_op jit(solution)/shard_map/ppermute | solution.py:18
  99.4 13.3 %collective-permute-start.11 = (bf16[112,512]{1,0:T(8,128)(2,1)S(1)}, bf16[112,512]{1,0:T(8,128)(2,1)S(1)}, u32[]{:S(2)}, u32[]{:S(2)}) collective-permute-start(bf16[112,512]{1,0:T(8,128)(2,1)S(1)} %get-tuple-element.34), channel_id=1, source_target_pairs={{0,8},{1,9},{2,10},{3,11},{4,12},{5,13},{6,14},{7,15},{8,0},{9,1},... | collective-permute-start | bytes 344072 | tf_op jit(solution)/shard_map/ppermute | solution.py:18
  102.5 13.8 %collective-permute-start.7 = (bf16[1,2,128,512]{3,1,2,0:T(2,128)(2,1)S(1)}, bf16[1,2,128,512]{3,1,2,0:T(2,128)(2,1)S(1)}, u32[]{:S(2)}, u32[]{:S(2)}) collective-permute-start(bf16[1,2,128,512]{3,1,2,0:T(2,128)(2,1)S(1)} %get-tuple-element.19), channel_id=1, source_target_pairs={{1,0},{3,2},{5,4},{7,6},{9,8},{11,10},{13,12},{15,14},{17,16},{19,... | collective-permute-start | bytes 786440 | tf_op jit(solution)/shard_map/ppermute | solution.py:123
  103.8 12.5 %collective-permute-start.6 = (bf16[1,2,128,512]{3,1,2,0:T(2,128)(2,1)S(1)}, bf16[1,2,128,512]{3,1,2,0:T(2,128)(2,1)S(1)}, u32[]{:S(2)}, u32[]{:S(2)}) collective-permute-start(bf16[1,2,128,512]{3,1,2,0:T(2,128)(2,1)S(1)} %get-tuple-element.20), channel_id=1, source_target_pairs={{0,1},{2,3},{4,5},{6,7},{8,9},{10,11},{12,13},{14,15},{16,17},{18,... | collective-permute-start | bytes 786440 | tf_op jit(solution)/shard_map/ppermute | solution.py:120
  106.8 13.0 %collective-permute-start.5 = (bf16[1,2,128,512]{3,1,2,0:T(2,128)(2,1)S(1)}, bf16[1,2,128,512]{3,1,2,0:T(2,128)(2,1)S(1)}, u32[]{:S(2)}, u32[]{:S(2)}) collective-permute-start(bf16[1,2,128,512]{3,1,2,0:T(2,128)(2,1)S(1)} %get-tuple-element.21), channel_id=1, source_target_pairs={{2,0},{4,2},{6,4},{8,6},{10,8},{12,10},{14,12},{16,14},{18,16},{20... | collective-permute-start | bytes 786440 | tf_op jit(solution)/shard_map/ppermute | solution.py:123
  108.1 13.2 %collective-permute-start.4 = (bf16[1,2,128,512]{3,1,2,0:T(2,128)(2,1)S(1)}, bf16[1,2,128,512]{3,1,2,0:T(2,128)(2,1)S(1)}, u32[]{:S(2)}, u32[]{:S(2)}) collective-permute-start(bf16[1,2,128,512]{3,1,2,0:T(2,128)(2,1)S(1)} %get-tuple-element.18), channel_id=1, source_target_pairs={{0,2},{2,4},{4,6},{6,8},{8,10},{10,12},{12,14},{14,16},{16,18},{18... | collective-permute-start | bytes 786440 | tf_op jit(solution)/shard_map/ppermute | solution.py:120
  116.2 1.2 collective-permute-start.14
  117.5 4.5 %collective-permute-start.15 = (f32[4,128]{1,0:T(4,128)S(1)}, f32[4,128]{1,0:T(4,128)S(1)}, u32[]{:S(2)}, u32[]{:S(2)}) collective-permute-start(f32[4,128]{1,0:T(4,128)S(1)} %broadcast_add_fusion), channel_id=1, source_target_pairs={{0,2},{1,3},{2,0},{3,1},{4,6},{5,7},{6,4},{7,5},{8,10},{9,11},{10,... | collective-permute-start | bytes 6152 | tf_op jit(solution)/shard_map/ppermute | solution.py:18
  122.0 3.6 %collective-permute-start.16 = (f32[4,128]{1,0:T(4,128)S(1)}, f32[4,128]{1,0:T(4,128)S(1)}, u32[]{:S(2)}, u32[]{:S(2)}) collective-permute-start(f32[4,128]{1,0:T(4,128)S(1)} %fusion.91), channel_id=1, source_target_pairs={{0,4},{1,5},{2,6},{3,7},{4,0},{5,1},{6,2},{7,3},{8,12},{9,13},{10,... | collective-permute-start | bytes 6152 | tf_op jit(solution)/shard_map/ppermute | solution.py:18
  124.1 2.8 %copy-start.23 = (s32[1,1,4,2]{2,3,1,0:T(2,128)S(1)}, s32[1,1,4,2]{2,3,1,0:T(2,128)}, u32[]{:S(2)}) copy-start(s32[1,1,4,2]{2,3,1,0:T(2,128)} %param.26) | copy-start | bytes 100
  125.2 8.0 %copy-start.16 = (bf16[1,1,256,512]{3,2,1,0:T(8,128)(2,1)S(1)}, bf16[1,1,256,512]{3,2,1,0:T(8,128)(2,1)}, u32[]{:S(2)}) copy-start(bf16[1,1,256,512]{3,2,1,0:T(8,128)(2,1)} %param.23) | copy-start | bytes 786436
  125.3 8.0 %copy-start.17 = (f32[256,512]{1,0:T(8,128)S(1)}, f32[256,512]{1,0:T(8,128)}, u32[]{:S(2)}) copy-start(f32[256,512]{1,0:T(8,128)} %get-tuple-element.27) | copy-start | bytes 1572868
  125.7 4.5 %collective-permute-start.17 = (f32[4,128]{1,0:T(4,128)S(1)}, f32[4,128]{1,0:T(4,128)S(1)}, u32[]{:S(2)}, u32[]{:S(2)}) collective-permute-start(f32[4,128]{1,0:T(4,128)S(1)} %add.412), channel_id=1, source_target_pairs={{0,8},{1,9},{2,10},{3,11},{4,12},{5,13},{6,14},{7,15},{8,0},{9,1},... | collective-permute-start | bytes 6152 | tf_op jit(solution)/shard_map/ppermute | solution.py:18
  130.2 4.6 %collective-permute-start.18 = (f32[4,128]{1,0:T(4,128)S(1)}, f32[4,128]{1,0:T(4,128)S(1)}, u32[]{:S(2)}, u32[]{:S(2)}) collective-permute-start(f32[4,128]{1,0:T(4,128)S(1)} %add.413), channel_id=1, source_target_pairs={{0,16},{1,17},{2,18},{3,19},{4,20},{5,21},{6,22},{7,23},{8,24},{9,... | collective-permute-start | bytes 6152 | tf_op jit(solution)/shard_map/ppermute | solution.py:18
  133.2 5.7 %copy-start.1 = (bf16[1024,512]{1,0:T(8,128)(2,1)S(1)}, bf16[1024,512]{1,0:T(8,128)(2,1)}, u32[]{:S(2)}) copy-start(bf16[1024,512]{1,0:T(8,128)(2,1)} %param.20) | copy-start | bytes 3145732
  (2 other events, 1.9 us)

commit v2 on v0

v2 whole, which is shorter than its diff:
```python
import functools

import jax
import jax.numpy as jnp
from jax import lax
from jax.experimental import pallas as pl
from jax.experimental.pallas import tpu as pltpu
from jax.sharding import PartitionSpec as P


def swap(values, along_gx, along_gy):
    n_gx, n_gy = lax.axis_size("gx"), lax.axis_size("gy")
    pairs = []
    for a in range(n_gx):
        for b in range(n_gy):
            target = (a ^ along_gx[b & 1]) * n_gy + (b ^ along_gy)
            pairs.append((a * n_gy + b, target))
    return lax.ppermute(values, ("gx", "gy"), pairs)


def group_masks():
    n_gx, n_gy = lax.axis_size("gx"), lax.axis_size("gy")
    return [(a * 4, b * 2) for a in range(n_gx // 4) for b in range(n_gy // 2)]


def piece_order(core, gx_index, gy_index):
    n_gy = lax.axis_size("gy")
    order = []
    for first in range(2):
        for second in range(2):
            low = jnp.where(core == 0, first + 2 * second, 2 * first + second)
            for mask_gx, mask_gy in group_masks():
                order.append((gx_index ^ (low | mask_gx)) * n_gy + (gy_index ^ mask_gy))
    return order


VMEM = pl.BlockSpec(memory_space=pltpu.VMEM)
SMEM = pl.BlockSpec(memory_space=pltpu.SMEM)


def silu_slope(values):
    logistic = jax.nn.sigmoid(values)
    return logistic * (1.0 + values * (1.0 - logistic))


def layer_norm(values):
    center = values - jnp.mean(values, axis=-1, keepdims=True)
    inverse_rms = lax.rsqrt(jnp.mean(center * center, axis=-1, keepdims=True) + 1e-05)
    return (center * inverse_rms, inverse_rms)


def norm_back(normed, inverse_rms, upstream):
    return inverse_rms * (
        upstream
        - jnp.mean(upstream, axis=-1, keepdims=True)
        - normed * jnp.mean(upstream * normed, axis=-1, keepdims=True)
    )


def inner_rows(factor, second):
    return lax.dot_general(
        factor, second, (((0,), (0,)), ((), ())), preferred_element_type=jnp.float32
    )


def times_transposed(factor, second):
    return lax.dot_general(
        factor, second, (((1,), (1,)), ((), ())), preferred_element_type=jnp.float32
    )


def matmul(factor, second):
    return jnp.dot(factor, second, preferred_element_type=jnp.float32)


def sender_hot(perm_ref, tile, block):
    row = perm_ref[pl.ds(tile, 1), :]
    return (lax.broadcasted_iota(jnp.int32, (block, block), 0) == row).astype(jnp.bfloat16)


def routes():
    if lax.axis_size("gy") == 2:
        return [("gx", 1, (0,)), ("gx", -1, (1,)), ("gy", 0, (2, 3))]
    return [("gx", 1, (0,)), ("gx", -1, (1,)), ("gy", 1, (2,)), ("gy", -1, (3,))]


def move(values, axis, step):
    count = lax.axis_size(axis)
    if step:
        pairs = [(i, i + step) for i in range(count) if 0 <= i + step < count]
    else:
        pairs = [(i, i ^ 1) for i in range(count)]
    return lax.ppermute(values, axis, pairs)


def pick(chosen):
    return chosen[0] if len(chosen) == 1 else chosen[0] + lax.axis_index("gy")


def opposite(chosen):
    return chosen[0] if len(chosen) == 1 else chosen[1] - lax.axis_index("gy")


def pack_kernel(chosen, nodes_ref, count_ref, list_ref, *packet_refs):
    for packet_ref, directions_ in zip(packet_refs, chosen):
        direction = pick(directions_)
        for slot in range(packet_ref.shape[0]):
            block = nodes_ref[list_ref[0, 0, direction, slot]]
            live = slot < count_ref[0, 0, direction]
            packet_ref[slot] = jnp.where(live, block, jnp.zeros_like(block))


def pack(node_blocks, send_count, send_list):
    slots = send_list.shape[3]
    chosen = [route[2] for route in routes()]
    packet = jax.ShapeDtypeStruct((slots,) + node_blocks.shape[1:], node_blocks.dtype)
    return pl.pallas_call(
        functools.partial(pack_kernel, chosen),
        out_shape=[packet] * len(chosen),
        in_specs=[VMEM, SMEM, SMEM],
        out_specs=[VMEM] * len(chosen),
        name="pack",
    )(node_blocks, send_count, send_list)


def main_kernel(chosen, rows, *refs):
    halo_refs, refs = refs[: len(chosen)], refs[len(chosen) :]
    (
        recv_ref, send_ref, perm_ref, nodes_ref, edges_ref, ew1_ref, eb1_ref, ew2_ref,
        nw1_ref, nb1_ref, nw2_ref, ncot_ref, ecot_ref,
        out_ref, gea_ref, base_ref, away_ref, keep_ref,
        ext, h_recv, h_send, affine, hidden, message, inverse, total, gel, stacked,
    ) = refs
    blocks, block, feature = nodes_ref.shape
    tiles = perm_ref.shape[0]
    nodes = blocks * block
    edges = tiles * block
    slots = halo_refs[0].shape[0]
    ext[:blocks] = nodes_ref[...]
    for halo_ref, directions_ in zip(halo_refs, chosen):
        if len(directions_) > 1:
            for other in directions_:
                ext[pl.ds(blocks + other * slots, slots)] = jnp.zeros_like(halo_ref)
        ext[pl.ds(blocks + opposite(directions_) * slots, slots)] = halo_ref[...]

    for tile in range(tiles):
        span = pl.ds(tile * block, block)
        h_recv[span, :] = nodes_ref[recv_ref[0, 0, tile]]
        hot = sender_hot(perm_ref, tile, block)
        h_send[span, :] = inner_rows(hot, ext[send_ref[0, 0, tile]]).astype(jnp.bfloat16)

    chunk = 2 * block if tiles % 2 == 0 else block

    def forward(step, _):
        span = pl.ds(pl.multiple_of(step * chunk, chunk), chunk)
        values = matmul(edges_ref[span, :], ew1_ref[:feature])
        values += matmul(h_recv[span, :], ew1_ref[feature : 2 * feature])
        values += matmul(h_send[span, :], ew1_ref[2 * feature :])
        values += eb1_ref[...]
        affine[span, :] = values
        hidden[span, :] = (values * jax.nn.sigmoid(values)).astype(jnp.bfloat16)
        normed, inverse_rms = layer_norm(matmul(hidden[span, :], ew2_ref[...]))
        message[span, :] = normed
        inverse[span, :] = jnp.broadcast_to(inverse_rms, (chunk, inverse.shape[1]))
        return 0

    lax.fori_loop(0, edges // chunk, forward, 0)

    total[...] = jnp.zeros_like(total)
    for tile in range(tiles):
        total[recv_ref[0, 0, tile]] += message[tile * block : (tile + 1) * block, :]
    aggregate = total[...].reshape(nodes, feature).astype(jnp.bfloat16)

    local = nodes_ref[...].reshape(nodes, feature)
    node_affine = matmul(local, nw1_ref[:feature]) + matmul(aggregate, nw1_ref[feature:])
    node_affine += nb1_ref[...]
    node_hidden = (node_affine * jax.nn.sigmoid(node_affine)).astype(jnp.bfloat16)
    node_normed, node_inverse = layer_norm(matmul(node_hidden, nw2_ref[...]))
    out_ref[...] = (local.astype(jnp.float32) + node_normed).astype(jnp.bfloat16)
    cot = ncot_ref[...].astype(jnp.float32)
    grad_linear = norm_back(node_normed, node_inverse, cot).astype(jnp.bfloat16)
    low = 3 * feature
    stacked[low + 3 * feature :, :] = inner_rows(node_hidden, grad_linear)
    grad_affine = times_transposed(grad_linear, nw2_ref[...]) * silu_slope(node_affine)
    grad_affine = grad_affine.astype(jnp.bfloat16)
    stacked[low + feature : low + 2 * feature, :] = inner_rows(local, grad_affine)
    stacked[low + 2 * feature : low + 3 * feature, :] = inner_rows(aggregate, grad_affine)
    base_ref[...] = cot + times_transposed(grad_affine, nw1_ref[:feature])
    total[...] = times_transposed(grad_affine, nw1_ref[feature:]).reshape(total.shape)

    for tile in range(tiles):
        span = pl.ds(tile * block, block)
        upstream = total[recv_ref[0, 0, tile]] + ecot_ref[span, :].astype(jnp.float32)
        back = norm_back(message[span, :], inverse[span, :1], upstream)
        gel[span, :] = back.astype(jnp.bfloat16)
    stacked[low : low + feature, :] = inner_rows(hidden[...], gel[...])

    def backward(step, _):
        span = pl.ds(pl.multiple_of(step * chunk, chunk), chunk)
        values = times_transposed(gel[span, :], ew2_ref[...]) * silu_slope(affine[span, :])
        gea_ref[span, :] = values.astype(jnp.bfloat16)
        return 0

    lax.fori_loop(0, edges // chunk, backward, 0)
    stacked[:feature, :] = inner_rows(edges_ref[...], gea_ref[...])
    stacked[feature : 2 * feature, :] = inner_rows(h_recv[...], gea_ref[...])
    stacked[2 * feature : 3 * feature, :] = inner_rows(h_send[...], gea_ref[...])

    gx_index, gy_index = lax.axis_index("gx"), lax.axis_index("gy")
    core = lax.rem(gy_index, 2)
    own = piece_order(core, gx_index, gy_index)
    other = piece_order(1 - core, gx_index, gy_index ^ 1)
    if rows % 16 == 0:
        for place in range(len(own)):
            start = pl.multiple_of(own[place] * rows, 8)
            keep_ref[place] = stacked[pl.ds(start, rows), :]
            start = pl.multiple_of(other[place] * rows, 8)
            away_ref[place] = stacked[pl.ds(start, rows), :].astype(jnp.bfloat16)
    else:
        keep_ref[...] = stacked[...]


def main(halos, recv, send, perm, node_blocks, edges, weights, node_cot, edge_cot):
    edge_w1, edge_b1, edge_w2, node_w1, node_b1, node_w2 = weights
    blocks, block, feature = node_blocks.shape
    nodes, edge_count = blocks * block, edges.shape[0]
    device_count = lax.axis_size("gx") * lax.axis_size("gy")
    rows = 7 * feature // device_count
    count = device_count // 2
    slots = halos[0].shape[0]
    bf16, f32 = jnp.bfloat16, jnp.float32
    keep = (count, rows, feature) if rows % 16 == 0 else (7 * feature, feature)
    results = [
        ((nodes, feature), bf16),
        ((edge_count, feature), bf16),
        ((nodes, feature), f32),
        ((count, rows, feature), bf16),
        (keep, f32),
    ]
    flops = 6 * feature * feature * (4 * edge_count + 3 * nodes)
    chosen = [route[2] for route in routes()]
    out, gea, base, away, kept = pl.pallas_call(
        functools.partial(main_kernel, chosen, rows),
        out_shape=[jax.ShapeDtypeStruct(*result) for result in results],
        in_specs=[VMEM] * len(halos) + [SMEM] * 2 + [VMEM] * 11,
        out_specs=[VMEM] * len(results),
        scratch_shapes=[
            pltpu.VMEM((blocks + 4 * slots, block, feature), bf16),
            pltpu.VMEM((edge_count, feature), bf16),
            pltpu.VMEM((edge_count, feature), bf16),
            pltpu.VMEM((edge_count, feature), f32),
            pltpu.VMEM((edge_count, feature), bf16),
            pltpu.VMEM((edge_count, feature), f32),
            pltpu.VMEM((edge_count, 128), f32),
            pltpu.VMEM((blocks, block, feature), f32),
            pltpu.VMEM((edge_count, feature), bf16),
            pltpu.VMEM((7 * feature, feature), f32),
        ],
        cost_estimate=pl.CostEstimate(
            flops=flops, bytes_accessed=12 << 20, transcendentals=2 * (nodes + edge_count) * feature
        ),
        name="layer",
    )(
        *halos, recv, send, perm, node_blocks, edges, edge_w1, edge_b1.reshape(1, feature),
        edge_w2, node_w1, node_b1.reshape(1, feature), node_w2, node_cot, edge_cot,
    )
    if rows % 16:
        gx_index, gy_index = lax.axis_index("gx"), lax.axis_index("gy")
        core = gy_index & 1
        pieces = kept.reshape(2 * count, rows, feature)
        other = piece_order(1 - core, gx_index, gy_index ^ 1)
        away = pieces[jnp.stack(other)].astype(bf16)
        kept = pieces[jnp.stack(piece_order(core, gx_index, gy_index))]
    return out, gea, base, away, kept


def tail_kernel(chosen, recv_ref, send_ref, perm_ref, gea_ref, ew1_ref, ecot_ref, base_ref, *refs):
    grad_ref, part_ref = refs[:2]
    packet_refs, (ext,) = refs[2:-1], refs[-1:]
    tiles, block = perm_ref.shape
    feature = gea_ref.shape[1]
    blocks = part_ref.shape[0]
    slots = packet_refs[0].shape[0]
    ext[...] = jnp.zeros_like(ext)
    ext[:blocks] = base_ref[...].reshape(part_ref.shape)

    def visit(tile, _):
        span = pl.ds(pl.multiple_of(tile * block, block), block)
        slope = gea_ref[span, :]
        grad = times_transposed(slope, ew1_ref[:feature])
        grad_ref[span, :] = (ecot_ref[span, :].astype(jnp.float32) + grad).astype(jnp.bfloat16)
        ext[recv_ref[0, 0, tile]] += times_transposed(slope, ew1_ref[feature : 2 * feature])
        moved = matmul(sender_hot(perm_ref, tile, block), slope).astype(jnp.bfloat16)
        ext[send_ref[0, 0, tile]] += times_transposed(moved, ew1_ref[2 * feature :])
        return 0

    lax.fori_loop(0, tiles, visit, 0)
    part_ref[...] = ext[:blocks]
    for packet_ref, directions_ in zip(packet_refs, chosen):
        start = blocks + opposite(directions_) * slots
        packet_ref[...] = ext[pl.ds(start, slots)].astype(jnp.bfloat16)


def tail(recv, send, perm, gea, edge_w1, edge_cot, base, blocks, slots):
    edge_count, feature = gea.shape
    block = perm.shape[1]
    chosen = [route[2] for route in routes()]
    results = [
        ((edge_count, feature), jnp.bfloat16),
        ((blocks, block, feature), jnp.float32),
    ] + [((slots, block, feature), jnp.bfloat16)] * len(chosen)
    return pl.pallas_call(
        functools.partial(tail_kernel, chosen),
        out_shape=[jax.ShapeDtypeStruct(*result) for result in results],
        in_specs=[SMEM] * 2 + [VMEM] * 5,
        out_specs=[VMEM] * len(results),
        scratch_shapes=[pltpu.VMEM((blocks + 4 * slots, block, feature), jnp.float32)],
        cost_estimate=pl.CostEstimate(
            flops=6 * feature * feature * edge_count, bytes_accessed=6 << 20, transcendentals=0
        ),
        name="input_grads",
    )(recv, send, perm, gea, edge_w1, edge_cot, base)


def finish_kernel(chosen, count_ref, list_ref, part_ref, *refs):
    packet_refs, grad_ref = refs[:-1], refs[-1]
    for block in range(part_ref.shape[0]):
        value = part_ref[block]
        for packet_ref, directions_ in zip(packet_refs, chosen):
            direction = pick(directions_)
            for slot in range(packet_ref.shape[0]):
                here = list_ref[0, 0, direction, slot] == block
                live = here & (slot < count_ref[0, 0, direction])
                given = packet_ref[slot].astype(jnp.float32)
                value += jnp.where(live, given, jnp.zeros_like(given))
        grad_ref[block] = value.astype(jnp.bfloat16)


def finish(send_count, send_list, part, packets):
    chosen = [route[2] for route in routes()]
    return pl.pallas_call(
        functools.partial(finish_kernel, chosen),
        out_shape=jax.ShapeDtypeStruct(part.shape, jnp.bfloat16),
        in_specs=[SMEM] * 2 + [VMEM] * (1 + len(packets)),
        out_specs=VMEM,
        cost_estimate=pl.CostEstimate(flops=0, bytes_accessed=2 << 20, transcendentals=0),
        name="node_grad",
    )(send_count, send_list, part, *packets)


def on_device(
    node_latents,
    edge_latents,
    edge_w1,
    edge_b1,
    edge_w2,
    node_w1,
    node_b1,
    node_w2,
    node_cot,
    edge_cot,
    send_count,
    send_list,
    tile_recv,
    tile_send,
    tile_perm,
):
    node_count, feature = node_latents.shape[2:]
    tile_count, block_size = tile_perm.shape[2:]
    slot_count = send_list.shape[3]
    block_count = node_count // block_size
    node_blocks = node_latents.reshape(block_count, block_size, feature)
    edge_rows = edge_latents.reshape(tile_count * block_size, feature)
    cot_node = node_cot.reshape(node_count, feature)
    cot_edge = edge_cot.reshape(tile_count * block_size, feature)
    perm = tile_perm.reshape(tile_count, block_size)
    packets = pack(node_blocks, send_count, send_list)
    halos = [move(packet, axis, step) for packet, (axis, step, _) in zip(packets, routes())]
    weights = (edge_w1, edge_b1, edge_w2, node_w1, node_b1, node_w2)
    node_out, gea, base, away, keep = main(
        halos, tile_recv, tile_send, perm, node_blocks, edge_rows, weights, cot_node, cot_edge
    )
    edge_grad, part, *packets = tail(
        tile_recv, tile_send, perm, gea, edge_w1, cot_edge, base, block_count, slot_count
    )
    piece, packets = scatter_sum(away, keep, packets)
    halos = [move(packet, axis, -step) for packet, (axis, step, _) in zip(packets, routes())]
    node_grad = finish(send_count, send_list, part, halos)
    row_counts = (3 * feature, feature, 2 * feature, feature)
    piece_index = lax.axis_index("gx") * lax.axis_size("gy") + lax.axis_index("gy")
    weight_dir = directions(piece, piece_index, row_counts)
    return (
        node_out.reshape(1, 1, node_count, feature),
        node_grad.reshape(1, 1, node_count, feature),
        edge_grad.reshape(1, 1, tile_count * block_size, feature),
        weight_dir,
    )


def scatter_sum(send, keep, packets):
    total = keep + swap(send, (0, 0), 1).astype(jnp.float32)
    for masks in ((1, 2), (2, 1)):
        total = total.reshape((2, total.shape[0] // 2) + total.shape[1:])
        total = total[0] + swap(total[1].astype(jnp.bfloat16), masks, 0).astype(jnp.float32)
    total, packets = lax.optimization_barrier((total, packets))
    final = total[0]
    for place, (mask_gx, mask_gy) in enumerate(group_masks()):
        if place:
            sent = total[place].astype(jnp.bfloat16)
            final = final + swap(sent, (mask_gx, mask_gx), mask_gy).astype(jnp.float32)
    return final, packets


def sum_everywhere(values):
    bit = 1
    while bit < lax.axis_size("gy"):
        values = values + swap(values, (0, 0), bit)
        bit *= 2
    bit = 1
    while bit < lax.axis_size("gx"):
        values = values + swap(values, (bit, bit), 0)
        bit *= 2
    return values


def directions(piece, piece_index, row_counts):
    rows, feature = piece.shape
    row_id = piece_index * rows + lax.broadcasted_iota(jnp.int32, (rows, 1), 0)
    low = 0
    inside = []
    for count in row_counts:
        inside.append(((row_id >= low) & (row_id < low + count)).astype(jnp.float32))
        low += count
    row_squares = jnp.sum(piece * piece, axis=1, keepdims=True)
    squares = jnp.stack([jnp.sum(row_squares * mask) for mask in inside])
    squares = sum_everywhere(jnp.broadcast_to(squares[:, None], (len(row_counts), 128)))
    scale = jnp.zeros((rows, 1), jnp.float32)
    for place, count in enumerate(row_counts):
        inverse = lax.rsqrt(squares[place, 0] / (count * feature) + 1e-06)
        scale = scale + inside[place] * inverse
    return (piece * scale).astype(jnp.bfloat16).reshape(rows * feature)


def solution(mesh):
    placed = (
        P("gx", "gy", None, None),
        P("gx", "gy", None, None),
        P(),
        P(),
        P(),
        P(),
        P(),
        P(),
        P("gx", "gy", None, None),
        P("gx", "gy", None, None),
        P("gx", "gy", None),
        P("gx", "gy", None, None),
        P("gx", "gy", None),
        P("gx", "gy", None),
        P("gx", "gy", None, None),
    )
    return jax.shard_map(
        on_device,
        mesh=mesh,
        in_specs=placed,
        out_specs=(
            P("gx", "gy", None, None),
            P("gx", "gy", None, None),
            P("gx", "gy", None, None),
            P(("gx", "gy")),
        ),
        check_vma=False,
    )
```

time: 271 us -> 114 us (0.42)
  waiting for transfers between devices: 140 us -> 45.6 us
  local copies, waits for them, and re-layouts: 34.2 us -> 5.77 us
  Pallas kernels: 0 us -> 26.7 us
  matrix products: 26.2 us -> 0 us
  other arithmetic: 32 us -> 6.93 us
  between operations: 18.9 us -> 3.56 us
  starting transfers between devices: 19.1 us -> 25 us
    psum x1 -> x0, waiting for transfers between devices: 128 us -> none  [on_device(): summed = lax.psum(weight_grad, ('gx', 'gy'))]
    ppermute x8 -> x17, waiting for transfers between devices: 12.1 us -> 45.6 us  [the longest x11 33.1 us: swap(): return lax.ppermute(values, ('gx', 'gy'), pairs)]
    pallas_call x0 -> x4, Pallas kernels: none -> 26.7 us  [the longest x1 14.8 us: main(): pl.pallas_call(functools.partial(main_kernel, chosen, rows), out_shape=[j...]
    dot_general x16 -> x0, matrix products: 26.2 us -> none  [the longest x4 5.82 us: matmul(): return jnp.dot(factor, second, preferred_element_type=jnp.float32)]
    gather x5 -> x0, local copies, waits for them, and re-layouts: 19.2 us -> none  [the longest x1 7.83 us: on_device(): jnp.take_along_axis(grad_s.reshape(tile_count, block_size, feature), inve...]
    reduce_sum x8 -> x2, other arithmetic: 12.8 us -> 0.82 us  [the longest x1 0.68 us: directions(): squares = jnp.stack([jnp.sum(row_squares * mask) for mask in inside])]
    mul x6 -> x0, other arithmetic: 6.26 us -> none  [the longest x3 5.99 us: on_device(): pieces.append(matrix * lax.rsqrt(jnp.mean(matrix * matrix) + 1e-06))]
    ppermute x8 -> x17, starting transfers between devices: 19 us -> 25 us  [the longest x11 12.8 us: swap(): return lax.ppermute(values, ('gx', 'gy'), pairs)]
  transfers between devices with their start and end apart: 9 -> 17, of which waited for: 5 -> 12; matrix products, arithmetic and copies ran while one was open for 13% -> 2% of each run, Pallas kernels for 0% -> 7%
where the time goes in v2:
time: 114 us
  waiting for transfers between devices  45.6 us (40%)
  Pallas kernels  26.7 us (23%)
  starting transfers between devices  25 us (22%)
  other arithmetic  6.93 us (6%)
  local copies, waits for them, and re-layouts  5.77 us (5%)
  between operations  3.56 us (3%)
    ppermute x11, waiting for transfers between devices, swap(): return lax.ppermute(values, ('gx', 'gy'), pairs)  33.1 us
    pallas_call x1, Pallas kernels, main(): pl.pallas_call(functools.partial(main_kernel, chosen, rows), out_shape=[j...  14.8 us
    ppermute x11, starting transfers between devices, swap(): return lax.ppermute(values, ('gx', 'gy'), pairs)  12.8 us
    ppermute x6, waiting for transfers between devices, move(): return lax.ppermute(values, axis, pairs)  12.5 us
    ppermute x6, starting transfers between devices, move(): return lax.ppermute(values, axis, pairs)  12.2 us
    pallas_call x1, Pallas kernels, tail(): pl.pallas_call(functools.partial(tail_kernel, chosen), out_shape=[jax.Sha...  7.68 us
    unnamed x21, local copies, waits for them, and re-layouts  4.9 us
    add x1, other arithmetic, scatter_sum(): total = keep + swap(send, (0, 0), 1).astype(jnp.float32)  2.69 us
  transfers between devices with their start and end apart: 17, of which 12 were waited for; matrix products, arithmetic and copies ran while one was open for 2% of the time, Pallas kernels for 7%

profile of v2, /device:TPU:0, one launch (start us, length us, event | category | flops | bytes accessed | tf_op | source)
XLA Modules:
  0.0 113.5 jit_solution(9857229267356861548)
XLA Ops:
  0.6 1.3 %copy.19.list_ref = s32[1,1,4,2]{3,2,1,0:T(4,128)} copy(s32[1,1,4,2]{2,3,1,0:T(2,128)} %param.26) | data formatting | bytes 64 | tf_op args[11]
  2.0 1.9 %pack.1 = (bf16[2,128,512]{2,1,0:T(8,128)(2,1)}, bf16[2,128,512]{2,1,0:T(8,128)(2,1)}, bf16[2,128,512]{2,1,0:T(8,128)(2,1)}) custom-call(bf16[2,128,512]{2,1,0:T(8,128)(2,1)} %bitcast.39, s32[1,1,4]{2,1,0:T(1,128)} %count_ref.3, s32[1,1,4,2]{3,2,1,0:T(4,128)} %copy.19.list_ref), custom_call_target="tpu_custom_call" | custom-call | tf_op jit(solution)/shard_map/pack/pallas_call | solution.py:117
  3.8 4.9 %collective-permute-start = (bf16[2,128,512]{2,1,0:T(8,128)(2,1)}, bf16[2,128,512]{2,1,0:T(8,128)(2,1)S(1)}, u32[]{:S(2)}, u32[]{:S(2)}) collective-permute-start(bf16[2,128,512]{2,1,0:T(8,128)(2,1)} %get-tuple-element.21), channel_id=1, source_target_pairs={{0,2},{2,4},{4,6},{6,8},{8,10},{10,12},{12,14},{14,16},{16,18},{18... | collective-permute-start | bytes 786440 | tf_op jit(solution)/shard_map/ppermute | solution.py:93
  8.7 1.3 %collective-permute-start.1 = (bf16[2,128,512]{2,1,0:T(8,128)(2,1)}, bf16[2,128,512]{2,1,0:T(8,128)(2,1)S(1)}, u32[]{:S(2)}, u32[]{:S(2)}) collective-permute-start(bf16[2,128,512]{2,1,0:T(8,128)(2,1)} %get-tuple-element.22), channel_id=1, source_target_pairs={{2,0},{4,2},{6,4},{8,6},{10,8},{12,10},{14,12},{16,14},{18,16},{20... | collective-permute-start | bytes 786440 | tf_op jit(solution)/shard_map/ppermute | solution.py:93
  10.0 0.1 collective-permute-start.2
  10.1 1.3 %copy.24 = s32[1,1,6,128]{3,2,1,0:T(8,128)} copy(s32[1,1,6,128]{3,1,2,0:T(1,128)} %param.29) | data formatting | bytes 6144
  11.4 8.8 %collective-permute-done.refs_0_ = bf16[2,128,512]{2,1,0:T(8,128)(2,1)S(1)} collective-permute-done((bf16[2,128,512]{2,1,0:T(8,128)(2,1)}, bf16[2,128,512]{2,1,0:T(8,128)(2,1)S(1)}, u32[]{:S(2)}, u32[]{:S(2)}) %collective-permute-start) | collective-permute-done | bytes 262176 | tf_op jit(solution)/shard_map/ppermute | solution.py:93
  20.2 1.8 %collective-permute-done.1.refs_1_ = bf16[2,128,512]{2,1,0:T(8,128)(2,1)S(1)} collective-permute-done((bf16[2,128,512]{2,1,0:T(8,128)(2,1)}, bf16[2,128,512]{2,1,0:T(8,128)(2,1)S(1)}, u32[]{:S(2)}, u32[]{:S(2)}) %collective-permute-start.1) | collective-permute-done | bytes 262176 | tf_op jit(solution)/shard_map/ppermute | solution.py:93
  22.0 0.7 copy-done.7
  22.8 14.8 %layer.1 = (bf16[256,512]{1,0:T(8,128)(2,1)}, bf16[768,512]{1,0:T(8,128)(2,1)}, f32[256,512]{1,0:T(8,128)}, bf16[16,112,512]{2,1,0:T(8,128)(2,1)}, f32[16,112,512]{2,1,0:T(8,128)}) custom-call(bf16[2,128,512]{2,1,0:T(8,128)(2,1)} %copy-done.6, bf16[2,128,512]{2,1,0:T(8,128)(2,1)} %copy-done.7, bf16[2,128,512]{2,1,0:T(8,128)(2,1)} %copy-done.8, ...), custom_call_target="tpu_custom_call" | custom-call | flops 6039797760 | bytes 12582912 | tf_op jit(solution)/shard_map/layer/pallas_call | solution.py:242
  37.7 4.0 %collective-permute-done.3 = bf16[16,112,512]{2,1,0:T(8,128)(2,1)S(1)} collective-permute-done((bf16[16,112,512]{2,1,0:T(8,128)(2,1)}, bf16[16,112,512]{2,1,0:T(8,128)(2,1)S(1)}, u32[]{:S(2)}, u32[]{:S(2)}) %collective-permute-start.3) | collective-permute-done | bytes 1835040 | tf_op jit(solution)/shard_map/ppermute | solution.py:18
  41.7 2.7 %convert_add_fusion = f32[16,112,512]{2,1,0:T(8,128)S(1)} fusion(f32[16,112,512]{2,1,0:T(8,128)} %get-tuple-element.28, bf16[16,112,512]{2,1,0:T(8,128)(2,1)S(1)} %collective-permute-done.3), kind=kLoop, calls=%fused_computation | loop fusion | flops 1835008 | bytes 9175040 | tf_op jit(solution)/shard_map/add | solution.py:401
  44.4 0.1 slice.76
  44.5 1.6 %collective-permute-start.4 = (bf16[8,112,512]{2,1,0:T(8,128)(2,1)S(1)}, bf16[8,112,512]{2,1,0:T(8,128)(2,1)S(1)}, u32[]{:S(2)}, u32[]{:S(2)}) collective-permute-start(bf16[8,112,512]{2,1,0:T(8,128)(2,1)S(1)} %slice.76), channel_id=1, source_target_pairs={{0,2},{1,5},{2,0},{3,7},{4,6},{5,1},{6,4},{7,3},{8,10},{9,13},{10,... | collective-permute-start | bytes 2752520 | tf_op jit(solution)/shard_map/ppermute | solution.py:18
  46.1 11.9 %collective-permute-done.4 = bf16[8,112,512]{2,1,0:T(8,128)(2,1)S(1)} collective-permute-done((bf16[8,112,512]{2,1,0:T(8,128)(2,1)S(1)}, bf16[8,112,512]{2,1,0:T(8,128)(2,1)S(1)}, u32[]{:S(2)}, u32[]{:S(2)}) %collective-permute-start.4) | collective-permute-done | bytes 917536 | tf_op jit(solution)/shard_map/ppermute | solution.py:18
  58.0 0.4 slice_add_fusion
  58.4 0.1 collective-permute-start.5
  58.5 7.7 %input_grads.1 = (bf16[768,512]{1,0:T(8,128)(2,1)}, f32[2,128,512]{2,1,0:T(8,128)}, bf16[2,128,512]{2,1,0:T(8,128)(2,1)}, bf16[2,128,512]{2,1,0:T(8,128)(2,1)}, bf16[2,128,512]{2,1,0:T(8,128)(2,1)}) custom-call(s32[1,1,6]{2,1,0:T(1,128)} %recv_ref.1, s32[1,1,6]{2,1,0:T(1,128)} %send_ref.1, s32[6,128]{1,0:T(8,128)} %bitcast.44, ...), custom_call_target="tpu_custom_call" | custom-call | flops 1207959552 | bytes 6291456 | tf_op jit(solution)/shard_map/input_grads/pallas_call | solution.py:312
  66.1 0.8 collective-permute-done.5
  66.9 0.2 slice_add_fusion.1
  67.2 3.3 %collective-permute-start.10 = (bf16[112,512]{1,0:T(8,128)(2,1)S(1)}, bf16[112,512]{1,0:T(8,128)(2,1)S(1)}, u32[]{:S(2)}, u32[]{:S(2)}) collective-permute-start(bf16[112,512]{1,0:T(8,128)(2,1)S(1)} %get-tuple-element.44), channel_id=1, source_target_pairs={{0,16},{1,17},{2,18},{3,19},{4,20},{5,21},{6,22},{7,23},{8,24},{9,... | collective-permute-start | bytes 344072 | tf_op jit(solution)/shard_map/ppermute | solution.py:18
  70.5 1.3 %collective-permute-start.11 = (bf16[112,512]{1,0:T(8,128)(2,1)S(1)}, bf16[112,512]{1,0:T(8,128)(2,1)S(1)}, u32[]{:S(2)}, u32[]{:S(2)}) collective-permute-start(bf16[112,512]{1,0:T(8,128)(2,1)S(1)} %get-tuple-element.43), channel_id=1, source_target_pairs={{0,24},{1,25},{2,26},{3,27},{4,28},{5,29},{6,30},{7,31},{8,16},{9,... | collective-permute-start | bytes 344072 | tf_op jit(solution)/shard_map/ppermute | solution.py:18
  71.8 0.2 collective-permute-start.9
  72.1 6.9 %collective-permute-done.10 = bf16[112,512]{1,0:T(8,128)(2,1)S(1)} collective-permute-done((bf16[112,512]{1,0:T(8,128)(2,1)S(1)}, bf16[112,512]{1,0:T(8,128)(2,1)S(1)}, u32[]{:S(2)}, u32[]{:S(2)}) %collective-permute-start.10) | collective-permute-done | bytes 114720 | tf_op jit(solution)/shard_map/ppermute | solution.py:18
  79.0 0.2 collective-permute-done.9
  79.2 0.1 multiply_reduce_fusion
  79.3 0.7 select_reduce_fusion.3
  80.0 2.6 %pad_maximum_fusion = f32[4]{0:T(128)S(1)} fusion(f32[1]{0:T(128)} %bitcast.16, f32[1]{0:T(128)} %bitcast.15, f32[1]{0:T(128)} %bitcast.14, f32[1]{0:T(128)} %bitcast.13), kind=kLoop, calls=%fused_computation.20 | loop fusion | flops 12 | bytes 32 | tf_op jit(solution)/shard_map/stack | solution.py:435
  82.6 0.1 broadcast_in_dim.2
  82.7 1.2 %collective-permute-done.12 = f32[4,128]{1,0:T(4,128)S(1)} collective-permute-done((f32[4,128]{1,0:T(4,128)S(1)}, f32[4,128]{1,0:T(4,128)S(1)}, u32[]{:S(2)}, u32[]{:S(2)}) %collective-permute-start.12) | collective-permute-done | bytes 2080 | tf_op jit(solution)/shard_map/ppermute | solution.py:18
  83.9 0.5 collective-permute-start.13
  84.5 3.0 %collective-permute-done.13 = f32[4,128]{1,0:T(4,128)S(1)} collective-permute-done((f32[4,128]{1,0:T(4,128)S(1)}, f32[4,128]{1,0:T(4,128)S(1)}, u32[]{:S(2)}, u32[]{:S(2)}) %collective-permute-start.13) | collective-permute-done | bytes 2080 | tf_op jit(solution)/shard_map/ppermute | solution.py:18
  87.5 0.1 fusion.4
  87.6 0.3 collective-permute-start.14
  87.8 3.3 %collective-permute-done.14 = f32[4,128]{1,0:T(4,128)S(1)} collective-permute-done((f32[4,128]{1,0:T(4,128)S(1)}, f32[4,128]{1,0:T(4,128)S(1)}, u32[]{:S(2)}, u32[]{:S(2)}) %collective-permute-start.14) | collective-permute-done | bytes 2080 | tf_op jit(solution)/shard_map/ppermute | solution.py:18
  91.2 1.8 %collective-permute-start.15 = (f32[4,128]{1,0:T(4,128)S(1)}, f32[4,128]{1,0:T(4,128)S(1)}, u32[]{:S(2)}, u32[]{:S(2)}) collective-permute-start(f32[4,128]{1,0:T(4,128)S(1)} %add.106), channel_id=1, source_target_pairs={{0,8},{1,9},{2,10},{3,11},{4,12},{5,13},{6,14},{7,15},{8,0},{9,1},... | collective-permute-start | bytes 6152 | tf_op jit(solution)/shard_map/ppermute | solution.py:18
  93.0 1.8 %collective-permute-done.15 = f32[4,128]{1,0:T(4,128)S(1)} collective-permute-done((f32[4,128]{1,0:T(4,128)S(1)}, f32[4,128]{1,0:T(4,128)S(1)}, u32[]{:S(2)}, u32[]{:S(2)}) %collective-permute-start.15) | collective-permute-done | bytes 2080 | tf_op jit(solution)/shard_map/ppermute | solution.py:18
  94.7 3.7 %collective-permute-start.16 = (f32[4,128]{1,0:T(4,128)S(1)}, f32[4,128]{1,0:T(4,128)S(1)}, u32[]{:S(2)}, u32[]{:S(2)}) collective-permute-start(f32[4,128]{1,0:T(4,128)S(1)} %add.107), channel_id=1, source_target_pairs={{0,16},{1,17},{2,18},{3,19},{4,20},{5,21},{6,22},{7,23},{8,24},{9,... | collective-permute-start | bytes 6152 | tf_op jit(solution)/shard_map/ppermute | solution.py:18
  98.5 1.3 %collective-permute-start.6 = (bf16[2,128,512]{2,1,0:T(8,128)(2,1)S(1)}, bf16[2,128,512]{2,1,0:T(8,128)(2,1)S(1)}, u32[]{:S(2)}, u32[]{:S(2)}) collective-permute-start(bf16[2,128,512]{2,1,0:T(8,128)(2,1)S(1)} %copy-done.5), channel_id=1, source_target_pairs={{2,0},{4,2},{6,4},{8,6},{10,8},{12,10},{14,12},{16,14},{18,16},{20... | collective-permute-start | bytes 786440 | tf_op jit(solution)/shard_map/ppermute | solution.py:93
  99.8 4.6 %collective-permute-start.7 = (bf16[2,128,512]{2,1,0:T(8,128)(2,1)S(1)}, bf16[2,128,512]{2,1,0:T(8,128)(2,1)S(1)}, u32[]{:S(2)}, u32[]{:S(2)}) collective-permute-start(bf16[2,128,512]{2,1,0:T(8,128)(2,1)S(1)} %copy-done.4), channel_id=1, source_target_pairs={{0,2},{2,4},{4,6},{6,8},{8,10},{10,12},{12,14},{14,16},{16,18},{18... | collective-permute-start | bytes 786440 | tf_op jit(solution)/shard_map/ppermute | solution.py:93
  104.3 0.1 collective-permute-start.8
  104.4 0.6 fusion.3
  107.8 0.1 fusion.2
  107.9 0.7 copy.22
  108.6 1.9 %collective-permute-done.7.refs_1_ = bf16[2,128,512]{2,1,0:T(8,128)(2,1)S(1)} collective-permute-done((bf16[2,128,512]{2,1,0:T(8,128)(2,1)S(1)}, bf16[2,128,512]{2,1,0:T(8,128)(2,1)S(1)}, u32[]{:S(2)}, u32[]{:S(2)}) %collective-permute-start.7) | collective-permute-done | bytes 262176 | tf_op jit(solution)/shard_map/ppermute | solution.py:93
  110.4 0.7 copy-done.1
  111.1 0.1 copy-done.2
  111.2 2.3 %node_grad.1 = bf16[2,128,512]{2,1,0:T(8,128)(2,1)} custom-call(s32[1,1,4]{2,1,0:T(1,128)} %count_ref.3, s32[1,1,4,2]{3,2,1,0:T(4,128)} %copy.19.list_ref, f32[2,128,512]{2,1,0:T(8,128)} %get-tuple-element.27.part_ref, bf16[2,128,512]{2,1,0:T(8,128)(2,1)} %copy-done, bf16[2,128,512]{2,1,0:T(8,128)(2,1)} %copy-done.1, bf16[2,128,512]{2,1,0:T(8,128)(2,1)} %copy-done.2), custom_call_target="tpu_custom_call" | custom-call | bytes 2097152 | tf_op jit(solution)/shard_map/node_grad/pallas_call | solution.py:341
  (30 shorter events, 0.3 us)
Async XLA Ops:
  3.8 16.4 %collective-permute-start = (bf16[2,128,512]{2,1,0:T(8,128)(2,1)}, bf16[2,128,512]{2,1,0:T(8,128)(2,1)S(1)}, u32[]{:S(2)}, u32[]{:S(2)}) collective-permute-start(bf16[2,128,512]{2,1,0:T(8,128)(2,1)} %get-tuple-element.21), channel_id=1, source_target_pairs={{0,2},{2,4},{4,6},{6,8},{8,10},{10,12},{12,14},{14,16},{16,18},{18... | collective-permute-start | bytes 786440 | tf_op jit(solution)/shard_map/ppermute | solution.py:93
  8.7 13.3 %collective-permute-start.1 = (bf16[2,128,512]{2,1,0:T(8,128)(2,1)}, bf16[2,128,512]{2,1,0:T(8,128)(2,1)S(1)}, u32[]{:S(2)}, u32[]{:S(2)}) collective-permute-start(bf16[2,128,512]{2,1,0:T(8,128)(2,1)} %get-tuple-element.22), channel_id=1, source_target_pairs={{2,0},{4,2},{6,4},{8,6},{10,8},{12,10},{14,12},{16,14},{18,16},{20... | collective-permute-start | bytes 786440 | tf_op jit(solution)/shard_map/ppermute | solution.py:93
  10.0 12.0 %collective-permute-start.2 = (bf16[2,128,512]{2,1,0:T(8,128)(2,1)}, bf16[2,128,512]{2,1,0:T(8,128)(2,1)S(1)}, u32[]{:S(2)}, u32[]{:S(2)}) collective-permute-start(bf16[2,128,512]{2,1,0:T(8,128)(2,1)} %get-tuple-element.23), channel_id=1, source_target_pairs={{0,1},{1,0},{2,3},{3,2},{4,5},{5,4},{6,7},{7,6},{8,9},{9,8},{10,11... | collective-permute-start | bytes 786440 | tf_op jit(solution)/shard_map/ppermute | solution.py:93
  20.2 1.8 %copy-start.6 = (bf16[2,128,512]{2,1,0:T(8,128)(2,1)}, bf16[2,128,512]{2,1,0:T(8,128)(2,1)S(1)}, u32[]{:S(2)}) copy-start(bf16[2,128,512]{2,1,0:T(8,128)(2,1)S(1)} %collective-permute-done.refs_0_) | copy-start | bytes 786436
  22.0 0.7 copy-start.7
  22.0 0.8 copy-start.8
  37.7 4.0 %collective-permute-start.3 = (bf16[16,112,512]{2,1,0:T(8,128)(2,1)}, bf16[16,112,512]{2,1,0:T(8,128)(2,1)S(1)}, u32[]{:S(2)}, u32[]{:S(2)}) collective-permute-start(bf16[16,112,512]{2,1,0:T(8,128)(2,1)} %get-tuple-element.29), channel_id=1, source_target_pairs={{0,1},{1,0},{2,3},{3,2},{4,5},{5,4},{6,7},{7,6},{8,9},{9,8},{10,11... | collective-permute-start | bytes 5505032 | tf_op jit(solution)/shard_map/ppermute | solution.py:18
  44.5 13.5 %collective-permute-start.4 = (bf16[8,112,512]{2,1,0:T(8,128)(2,1)S(1)}, bf16[8,112,512]{2,1,0:T(8,128)(2,1)S(1)}, u32[]{:S(2)}, u32[]{:S(2)}) collective-permute-start(bf16[8,112,512]{2,1,0:T(8,128)(2,1)S(1)} %slice.76), channel_id=1, source_target_pairs={{0,2},{1,5},{2,0},{3,7},{4,6},{5,1},{6,4},{7,3},{8,10},{9,13},{10,... | collective-permute-start | bytes 2752520 | tf_op jit(solution)/shard_map/ppermute | solution.py:18
  58.4 8.5 %collective-permute-start.5 = (bf16[4,112,512]{2,1,0:T(8,128)(2,1)S(1)}, bf16[4,112,512]{2,1,0:T(8,128)(2,1)S(1)}, u32[]{:S(2)}, u32[]{:S(2)}) collective-permute-start(bf16[4,112,512]{2,1,0:T(8,128)(2,1)S(1)} %slice.77), channel_id=1, source_target_pairs={{0,4},{1,3},{2,6},{3,1},{4,0},{5,7},{6,2},{7,5},{8,12},{9,11},{10,... | collective-permute-start | bytes 1376264 | tf_op jit(solution)/shard_map/ppermute | solution.py:18
  67.1 31.4 %copy-start.5 = (bf16[2,128,512]{2,1,0:T(8,128)(2,1)S(1)}, bf16[2,128,512]{2,1,0:T(8,128)(2,1)}, u32[]{:S(2)}) copy-start(bf16[2,128,512]{2,1,0:T(8,128)(2,1)} %get-tuple-element.33) | copy-start | bytes 786436
  67.1 32.7 %copy-start.4 = (bf16[2,128,512]{2,1,0:T(8,128)(2,1)S(1)}, bf16[2,128,512]{2,1,0:T(8,128)(2,1)}, u32[]{:S(2)}) copy-start(bf16[2,128,512]{2,1,0:T(8,128)(2,1)} %get-tuple-element.34) | copy-start | bytes 786436
  67.1 37.2 %copy-start.3 = (bf16[2,128,512]{2,1,0:T(8,128)(2,1)S(1)}, bf16[2,128,512]{2,1,0:T(8,128)(2,1)}, u32[]{:S(2)}) copy-start(bf16[2,128,512]{2,1,0:T(8,128)(2,1)} %get-tuple-element.35) | copy-start | bytes 786436
  67.2 11.7 %collective-permute-start.10 = (bf16[112,512]{1,0:T(8,128)(2,1)S(1)}, bf16[112,512]{1,0:T(8,128)(2,1)S(1)}, u32[]{:S(2)}, u32[]{:S(2)}) collective-permute-start(bf16[112,512]{1,0:T(8,128)(2,1)S(1)} %get-tuple-element.44), channel_id=1, source_target_pairs={{0,16},{1,17},{2,18},{3,19},{4,20},{5,21},{6,22},{7,23},{8,24},{9,... | collective-permute-start | bytes 344072 | tf_op jit(solution)/shard_map/ppermute | solution.py:18
  70.5 8.5 %collective-permute-start.11 = (bf16[112,512]{1,0:T(8,128)(2,1)S(1)}, bf16[112,512]{1,0:T(8,128)(2,1)S(1)}, u32[]{:S(2)}, u32[]{:S(2)}) collective-permute-start(bf16[112,512]{1,0:T(8,128)(2,1)S(1)} %get-tuple-element.43), channel_id=1, source_target_pairs={{0,24},{1,25},{2,26},{3,27},{4,28},{5,29},{6,30},{7,31},{8,16},{9,... | collective-permute-start | bytes 344072 | tf_op jit(solution)/shard_map/ppermute | solution.py:18
  71.8 7.3 %collective-permute-start.9 = (bf16[112,512]{1,0:T(8,128)(2,1)S(1)}, bf16[112,512]{1,0:T(8,128)(2,1)S(1)}, u32[]{:S(2)}, u32[]{:S(2)}) collective-permute-start(bf16[112,512]{1,0:T(8,128)(2,1)S(1)} %get-tuple-element.42), channel_id=1, source_target_pairs={{0,8},{1,9},{2,10},{3,11},{4,12},{5,13},{6,14},{7,15},{8,0},{9,1},... | collective-permute-start | bytes 344072 | tf_op jit(solution)/shard_map/ppermute | solution.py:18
  82.7 1.2 %collective-permute-start.12 = (f32[4,128]{1,0:T(4,128)S(1)}, f32[4,128]{1,0:T(4,128)S(1)}, u32[]{:S(2)}, u32[]{:S(2)}) collective-permute-start(f32[4,128]{1,0:T(4,128)S(1)} %broadcast_in_dim.2), channel_id=1, source_target_pairs={{0,1},{1,0},{2,3},{3,2},{4,5},{5,4},{6,7},{7,6},{8,9},{9,8},{10,11... | collective-permute-start | bytes 6152 | tf_op jit(solution)/shard_map/ppermute | solution.py:18
  83.9 3.6 %collective-permute-start.13 = (f32[4,128]{1,0:T(4,128)S(1)}, f32[4,128]{1,0:T(4,128)S(1)}, u32[]{:S(2)}, u32[]{:S(2)}) collective-permute-start(f32[4,128]{1,0:T(4,128)S(1)} %broadcast_add_fusion), channel_id=1, source_target_pairs={{0,2},{1,3},{2,0},{3,1},{4,6},{5,7},{6,4},{7,5},{8,10},{9,11},{10,... | collective-permute-start | bytes 6152 | tf_op jit(solution)/shard_map/ppermute | solution.py:18
  87.6 3.6 %collective-permute-start.14 = (f32[4,128]{1,0:T(4,128)S(1)}, f32[4,128]{1,0:T(4,128)S(1)}, u32[]{:S(2)}, u32[]{:S(2)}) collective-permute-start(f32[4,128]{1,0:T(4,128)S(1)} %fusion.4), channel_id=1, source_target_pairs={{0,4},{1,5},{2,6},{3,7},{4,0},{5,1},{6,2},{7,3},{8,12},{9,13},{10,... | collective-permute-start | bytes 6152 | tf_op jit(solution)/shard_map/ppermute | solution.py:18
  91.2 3.6 %collective-permute-start.15 = (f32[4,128]{1,0:T(4,128)S(1)}, f32[4,128]{1,0:T(4,128)S(1)}, u32[]{:S(2)}, u32[]{:S(2)}) collective-permute-start(f32[4,128]{1,0:T(4,128)S(1)} %add.106), channel_id=1, source_target_pairs={{0,8},{1,9},{2,10},{3,11},{4,12},{5,13},{6,14},{7,15},{8,0},{9,1},... | collective-permute-start | bytes 6152 | tf_op jit(solution)/shard_map/ppermute | solution.py:18
  94.7 9.7 %collective-permute-start.16 = (f32[4,128]{1,0:T(4,128)S(1)}, f32[4,128]{1,0:T(4,128)S(1)}, u32[]{:S(2)}, u32[]{:S(2)}) collective-permute-start(f32[4,128]{1,0:T(4,128)S(1)} %add.107), channel_id=1, source_target_pairs={{0,16},{1,17},{2,18},{3,19},{4,20},{5,21},{6,22},{7,23},{8,24},{9,... | collective-permute-start | bytes 6152 | tf_op jit(solution)/shard_map/ppermute | solution.py:18
  98.5 10.1 %collective-permute-start.6 = (bf16[2,128,512]{2,1,0:T(8,128)(2,1)S(1)}, bf16[2,128,512]{2,1,0:T(8,128)(2,1)S(1)}, u32[]{:S(2)}, u32[]{:S(2)}) collective-permute-start(bf16[2,128,512]{2,1,0:T(8,128)(2,1)S(1)} %copy-done.5), channel_id=1, source_target_pairs={{2,0},{4,2},{6,4},{8,6},{10,8},{12,10},{14,12},{16,14},{18,16},{20... | collective-permute-start | bytes 786440 | tf_op jit(solution)/shard_map/ppermute | solution.py:93
  99.8 10.7 %collective-permute-start.7 = (bf16[2,128,512]{2,1,0:T(8,128)(2,1)S(1)}, bf16[2,128,512]{2,1,0:T(8,128)(2,1)S(1)}, u32[]{:S(2)}, u32[]{:S(2)}) collective-permute-start(bf16[2,128,512]{2,1,0:T(8,128)(2,1)S(1)} %copy-done.4), channel_id=1, source_target_pairs={{0,2},{2,4},{4,6},{6,8},{8,10},{10,12},{12,14},{14,16},{16,18},{18... | collective-permute-start | bytes 786440 | tf_op jit(solution)/shard_map/ppermute | solution.py:93
  104.3 6.1 %collective-permute-start.8 = (bf16[2,128,512]{2,1,0:T(8,128)(2,1)S(1)}, bf16[2,128,512]{2,1,0:T(8,128)(2,1)S(1)}, u32[]{:S(2)}, u32[]{:S(2)}) collective-permute-start(bf16[2,128,512]{2,1,0:T(8,128)(2,1)S(1)} %copy-done.3), channel_id=1, source_target_pairs={{0,1},{1,0},{2,3},{3,2},{4,5},{5,4},{6,7},{7,6},{8,9},{9,8},{10,11... | collective-permute-start | bytes 786440 | tf_op jit(solution)/shard_map/ppermute | solution.py:93
  108.6 1.9 %copy-start = (bf16[2,128,512]{2,1,0:T(8,128)(2,1)}, bf16[2,128,512]{2,1,0:T(8,128)(2,1)S(1)}, u32[]{:S(2)}) copy-start(bf16[2,128,512]{2,1,0:T(8,128)(2,1)S(1)} %collective-permute-done.6.refs_0_) | copy-start | bytes 786436
  110.4 0.7 copy-start.1
  110.4 0.8 copy-start.2

commit v3 on v2

--- a/solution.py
+++ b/solution.py
@@ -34,6 +34,7 @@
     return order
 
 
+LAYER_GRANT = 34 << 20
 VMEM = pl.BlockSpec(memory_space=pltpu.VMEM)
 SMEM = pl.BlockSpec(memory_space=pltpu.SMEM)
 
@@ -79,31 +80,33 @@
 
 
 def routes():
-    if lax.axis_size("gy") == 2:
-        return [("gx", 1, (0,)), ("gx", -1, (1,)), ("gy", 0, (2, 3))]
-    return [("gx", 1, (0,)), ("gx", -1, (1,)), ("gy", 1, (2,)), ("gy", -1, (3,))]
-
-
-def move(values, axis, step):
+    kinds = [("gx", "odd"), ("gx", "even")]
+    return kinds + [("gy", kind) for kind in ("odd", "even")[lax.axis_size("gy") == 2 :]]
+
+
+def upward(axis, kind):
+    parity = lax.rem(lax.axis_index(axis), 2)
+    return 1 - parity if kind == "even" else parity
+
+
+def sent_to(axis, kind):
+    return (2 if axis == "gy" else 0) + 1 - upward(axis, kind)
+
+
+def heard_from(axis, kind):
+    return (2 if axis == "gy" else 0) + upward(axis, kind)
+
+
+def move(values, axis, kind):
     count = lax.axis_size(axis)
-    if step:
-        pairs = [(i, i + step) for i in range(count) if 0 <= i + step < count]
-    else:
-        pairs = [(i, i ^ 1) for i in range(count)]
+    low = range(kind == "odd", count - 1, 2)
+    pairs = [pair for i in low for pair in ((i, i + 1), (i + 1, i))]
     return lax.ppermute(values, axis, pairs)
 
 
-def pick(chosen):
-    return chosen[0] if len(chosen) == 1 else chosen[0] + lax.axis_index("gy")
-
-
-def opposite(chosen):
-    return chosen[0] if len(chosen) == 1 else chosen[1] - lax.axis_index("gy")
-
-
 def pack_kernel(chosen, nodes_ref, count_ref, list_ref, *packet_refs):
-    for packet_ref, directions_ in zip(packet_refs, chosen):
-        direction = pick(directions_)
+    for packet_ref, route in zip(packet_refs, chosen):
+        direction = sent_to(*route)
         for slot in range(packet_ref.shape[0]):
             block = nodes_ref[list_ref[0, 0, direction, slot]]
             live = slot < count_ref[0, 0, direction]
@@ -112,24 +115,60 @@
 
 def pack(node_blocks, send_count, send_list):
     slots = send_list.shape[3]
-    chosen = [route[2] for route in routes()]
+    chosen = routes()
     packet = jax.ShapeDtypeStruct((slots,) + node_blocks.shape[1:], node_blocks.dtype)
     return pl.pallas_call(
         functools.partial(pack_kernel, chosen),
         out_shape=[packet] * len(chosen),
         in_specs=[VMEM, SMEM, SMEM],
         out_specs=[VMEM] * len(chosen),
+        compiler_params=pltpu.CompilerParams(vmem_limit_bytes=4 << 20),
         name="pack",
     )(node_blocks, send_count, send_list)
+
+
+def local_kernel(recv_ref, nodes_ref, edges_ref, ew1_ref, eb1_ref, part_ref, h_recv_ref):
+    block, feature = nodes_ref.shape[1:]
+    tiles = edges_ref.shape[0] // block
+    for tile in range(tiles):
+        h_recv_ref[tile * block : (tile + 1) * block, :] = nodes_ref[recv_ref[0, 0, tile]]
+    chunk = 2 * block if tiles % 2 == 0 else block
+
+    def visit(step, _):
+        span = pl.ds(pl.multiple_of(step * chunk, chunk), chunk)
+        values = matmul(edges_ref[span, :], ew1_ref[:feature])
+        values += matmul(h_recv_ref[span, :], ew1_ref[feature : 2 * feature])
+        part_ref[span, :] = values + eb1_ref[...]
+        return 0
+
+    lax.fori_loop(0, edges_ref.shape[0] // chunk, visit, 0)
+
+
+def local(recv, node_blocks, edges, edge_w1, edge_b1):
+    edge_count, feature = edges.shape
+    return pl.pallas_call(
+        local_kernel,
+        out_shape=[
+            jax.ShapeDtypeStruct((edge_count, feature), jnp.float32),
+            jax.ShapeDtypeStruct((edge_count, feature), jnp.bfloat16),
+        ],
+        in_specs=[SMEM] + [VMEM] * 4,
+        out_specs=[VMEM] * 2,
+        compiler_params=pltpu.CompilerParams(vmem_limit_bytes=12 << 20),
+        cost_estimate=pl.CostEstimate(
+            flops=4 * feature * feature * edge_count, bytes_accessed=4 << 20, transcendentals=0
+        ),
+        name="local_part",
+    )(recv, node_blocks, edges, edge_w1, edge_b1.reshape(1, feature))
 
 
 def main_kernel(chosen, rows, *refs):
     halo_refs, refs = refs[: len(chosen)], refs[len(chosen) :]
     (
-        recv_ref, send_ref, perm_ref, nodes_ref, edges_ref, ew1_ref, eb1_ref, ew2_ref,
+        recv_ref, send_ref, perm_ref, nodes_ref, edges_ref, part_ref, h_recv, ew1_ref, ew2_ref,
         nw1_ref, nb1_ref, nw2_ref, ncot_ref, ecot_ref,
         out_ref, gea_ref, base_ref, away_ref, keep_ref,
-        ext, h_recv, h_send, affine, hidden, message, inverse, total, gel, stacked,
+        ext, h_send, affine, hidden, message, inverse, total, gel, stacked,
     ) = refs
     blocks, block, feature = nodes_ref.shape
     tiles = perm_ref.shape[0]
@@ -137,15 +176,12 @@
     edges = tiles * block
     slots = halo_refs[0].shape[0]
     ext[:blocks] = nodes_ref[...]
-    for halo_ref, directions_ in zip(halo_refs, chosen):
-        if len(directions_) > 1:
-            for other in directions_:
-                ext[pl.ds(blocks + other * slots, slots)] = jnp.zeros_like(halo_ref)
-        ext[pl.ds(blocks + opposite(directions_) * slots, slots)] = halo_ref[...]
+    ext[blocks:] = jnp.zeros((ext.shape[0] - blocks,) + ext.shape[1:], ext.dtype)
+    for halo_ref, route in zip(halo_refs, chosen):
+        ext[pl.ds(blocks + heard_from(*route) * slots, slots)] = halo_ref[...]
 
     for tile in range(tiles):
         span = pl.ds(tile * block, block)
-        h_recv[span, :] = nodes_ref[recv_ref[0, 0, tile]]
         hot = sender_hot(perm_ref, tile, block)
         h_send[span, :] = inner_rows(hot, ext[send_ref[0, 0, tile]]).astype(jnp.bfloat16)
 
@@ -153,10 +189,7 @@
 
     def forward(step, _):
         span = pl.ds(pl.multiple_of(step * chunk, chunk), chunk)
-        values = matmul(edges_ref[span, :], ew1_ref[:feature])
-        values += matmul(h_recv[span, :], ew1_ref[feature : 2 * feature])
-        values += matmul(h_send[span, :], ew1_ref[2 * feature :])
-        values += eb1_ref[...]
+        values = part_ref[span, :] + matmul(h_send[span, :], ew1_ref[2 * feature :])
         affine[span, :] = values
         hidden[span, :] = (values * jax.nn.sigmoid(values)).astype(jnp.bfloat16)
         normed, inverse_rms = layer_norm(matmul(hidden[span, :], ew2_ref[...]))
@@ -220,8 +253,8 @@
         keep_ref[...] = stacked[...]
 
 
-def main(halos, recv, send, perm, node_blocks, edges, weights, node_cot, edge_cot):
-    edge_w1, edge_b1, edge_w2, node_w1, node_b1, node_w2 = weights
+def main(halos, recv, send, perm, node_blocks, edges, part, h_recv, weights, node_cot, edge_cot):
+    edge_w1, edge_w2, node_w1, node_b1, node_w2 = weights
     blocks, block, feature = node_blocks.shape
     nodes, edge_count = blocks * block, edges.shape[0]
     device_count = lax.axis_size("gx") * lax.axis_size("gy")
@@ -237,16 +270,15 @@
         ((count, rows, feature), bf16),
         (keep, f32),
     ]
-    flops = 6 * feature * feature * (4 * edge_count + 3 * nodes)
-    chosen = [route[2] for route in routes()]
+    flops = 6 * feature * feature * (3 * edge_count + 3 * nodes)
+    chosen = routes()
     out, gea, base, away, kept = pl.pallas_call(
         functools.partial(main_kernel, chosen, rows),
         out_shape=[jax.ShapeDtypeStruct(*result) for result in results],
-        in_specs=[VMEM] * len(halos) + [SMEM] * 2 + [VMEM] * 11,
+        in_specs=[VMEM] * len(halos) + [SMEM] * 2 + [VMEM] * 12,
         out_specs=[VMEM] * len(results),
         scratch_shapes=[
             pltpu.VMEM((blocks + 4 * slots, block, feature), bf16),
-            pltpu.VMEM((edge_count, feature), bf16),
             pltpu.VMEM((edge_count, feature), bf16),
             pltpu.VMEM((edge_count, feature), f32),
             pltpu.VMEM((edge_count, feature), bf16),
@@ -256,13 +288,14 @@
             pltpu.VMEM((edge_count, feature), bf16),
             pltpu.VMEM((7 * feature, feature), f32),
         ],
+        compiler_params=pltpu.CompilerParams(vmem_limit_bytes=LAYER_GRANT),
         cost_estimate=pl.CostEstimate(
             flops=flops, bytes_accessed=12 << 20, transcendentals=2 * (nodes + edge_count) * feature
         ),
         name="layer",
     )(
-        *halos, recv, send, perm, node_blocks, edges, edge_w1, edge_b1.reshape(1, feature),
-        edge_w2, node_w1, node_b1.reshape(1, feature), node_w2, node_cot, edge_cot,
+        *halos, recv, send, perm, node_blocks, edges, part, h_recv, edge_w1, edge_w2,
+        node_w1, node_b1.reshape(1, feature), node_w2, node_cot, edge_cot,
     )
     if rows % 16:
         gx_index, gy_index = lax.axis_index("gx"), lax.axis_index("gy")
@@ -296,15 +329,15 @@
 
     lax.fori_loop(0, tiles, visit, 0)
     part_ref[...] = ext[:blocks]
-    for packet_ref, directions_ in zip(packet_refs, chosen):
-        start = blocks + opposite(directions_) * slots
+    for packet_ref, route in zip(packet_refs, chosen):
+        start = blocks + heard_from(*route) * slots
         packet_ref[...] = ext[pl.ds(start, slots)].astype(jnp.bfloat16)
 
 
 def tail(recv, send, perm, gea, edge_w1, edge_cot, base, blocks, slots):
     edge_count, feature = gea.shape
     block = perm.shape[1]
-    chosen = [route[2] for route in routes()]
+    chosen = routes()
     results = [
         ((edge_count, feature), jnp.bfloat16),
         ((blocks, block, feature), jnp.float32),
@@ -315,6 +348,7 @@
         in_specs=[SMEM] * 2 + [VMEM] * 5,
         out_specs=[VMEM] * len(results),
         scratch_shapes=[pltpu.VMEM((blocks + 4 * slots, block, feature), jnp.float32)],
+        compiler_params=pltpu.CompilerParams(vmem_limit_bytes=14 << 20),
         cost_estimate=pl.CostEstimate(
             flops=6 * feature * feature * edge_count, bytes_accessed=6 << 20, transcendentals=0
         ),
@@ -326,8 +360,8 @@
     packet_refs, grad_ref = refs[:-1], refs[-1]
     for block in range(part_ref.shape[0]):
         value = part_ref[block]
-        for packet_ref, directions_ in zip(packet_refs, chosen):
-            direction = pick(directions_)
+        for packet_ref, route in zip(packet_refs, chosen):
+            direction = sent_to(*route)
             for slot in range(packet_ref.shape[0]):
                 here = list_ref[0, 0, direction, slot] == block
                 live = here & (slot < count_ref[0, 0, direction])
@@ -337,12 +371,13 @@
 
 
 def finish(send_count, send_list, part, packets):
-    chosen = [route[2] for route in routes()]
+    chosen = routes()
     return pl.pallas_call(
         functools.partial(finish_kernel, chosen),
         out_shape=jax.ShapeDtypeStruct(part.shape, jnp.bfloat16),
         in_specs=[SMEM] * 2 + [VMEM] * (1 + len(packets)),
         out_specs=VMEM,
+        compiler_params=pltpu.CompilerParams(vmem_limit_bytes=6 << 20),
         cost_estimate=pl.CostEstimate(flops=0, bytes_accessed=2 << 20, transcendentals=0),
         name="node_grad",
     )(send_count, send_list, part, *packets)
@@ -375,20 +410,21 @@
     cot_edge = edge_cot.reshape(tile_count * block_size, feature)
     perm = tile_perm.reshape(tile_count, block_size)
     packets = pack(node_blocks, send_count, send_list)
-    halos = [move(packet, axis, step) for packet, (axis, step, _) in zip(packets, routes())]
-    weights = (edge_w1, edge_b1, edge_w2, node_w1, node_b1, node_w2)
+    halos = [move(packet, *route) for packet, route in zip(packets, routes())]
+    partial, h_recv = local(tile_recv, node_blocks, edge_rows, edge_w1, edge_b1)
+    weights = (edge_w1, edge_w2, node_w1, node_b1, node_w2)
     node_out, gea, base, away, keep = main(
-        halos, tile_recv, tile_send, perm, node_blocks, edge_rows, weights, cot_node, cot_edge
+        halos, tile_recv, tile_send, perm, node_blocks, edge_rows, partial, h_recv, weights,
+        cot_node, cot_edge,
     )
     edge_grad, part, *packets = tail(
         tile_recv, tile_send, perm, gea, edge_w1, cot_edge, base, block_count, slot_count
     )
-    piece, packets = scatter_sum(away, keep, packets)
-    halos = [move(packet, axis, -step) for packet, (axis, step, _) in zip(packets, routes())]
+    terms = scatter_sum(away, keep)
+    halos = [move(packet, *route) for packet, route in zip(packets, routes())]
     node_grad = finish(send_count, send_list, part, halos)
     row_counts = (3 * feature, feature, 2 * feature, feature)
-    piece_index = lax.axis_index("gx") * lax.axis_size("gy") + lax.axis_index("gy")
-    weight_dir = directions(piece, piece_index, row_counts)
+    weight_dir = directions(terms, row_counts)
     return (
         node_out.reshape(1, 1, node_count, feature),
         node_grad.reshape(1, 1, node_count, feature),
@@ -397,18 +433,17 @@
     )
 
 
-def scatter_sum(send, keep, packets):
+def scatter_sum(send, keep):
     total = keep + swap(send, (0, 0), 1).astype(jnp.float32)
     for masks in ((1, 2), (2, 1)):
         total = total.reshape((2, total.shape[0] // 2) + total.shape[1:])
-        total = total[0] + swap(total[1].astype(jnp.bfloat16), masks, 0).astype(jnp.float32)
-    total, packets = lax.optimization_barrier((total, packets))
-    final = total[0]
+        heard = swap(total[1].astype(jnp.bfloat16), masks, 0)
+        total = total[0] + heard.astype(jnp.float32)
+    terms = [total[0]]
     for place, (mask_gx, mask_gy) in enumerate(group_masks()):
         if place:
-            sent = total[place].astype(jnp.bfloat16)
-            final = final + swap(sent, (mask_gx, mask_gx), mask_gy).astype(jnp.float32)
-    return final, packets
+            terms.append(swap(total[place].astype(jnp.bfloat16), (mask_gx, mask_gx), mask_gy))
+    return terms
 
 
 def sum_everywhere(values):
@@ -423,22 +458,63 @@
     return values
 
 
-def directions(piece, piece_index, row_counts):
+def squares_kernel(row_counts, *refs):
+    term_refs, (piece_ref, square_ref) = refs[:-2], refs[-2:]
+    piece = term_refs[0][...]
+    for term_ref in term_refs[1:]:
+        piece += term_ref[...].astype(jnp.float32)
+    piece_ref[...] = piece
+    rows = piece.shape[0]
+    index = lax.axis_index("gx") * lax.axis_size("gy") + lax.axis_index("gy")
+    row_id = index * rows + lax.broadcasted_iota(jnp.int32, (rows, 1), 0)
+    row_squares = jnp.sum(piece * piece, axis=1, keepdims=True)
+    low = 0
+    for place, count in enumerate(row_counts):
+        inside = (row_id >= low) & (row_id < low + count)
+        square = jnp.sum(jnp.where(inside, row_squares, 0.0), axis=0, keepdims=True)
+        square_ref[place : place + 1, :] = jnp.broadcast_to(square, (1, square_ref.shape[1]))
+        low += count
+
+
+def scale_kernel(row_counts, piece_ref, square_ref, grad_ref):
+    piece = piece_ref[...]
     rows, feature = piece.shape
-    row_id = piece_index * rows + lax.broadcasted_iota(jnp.int32, (rows, 1), 0)
+    index = lax.axis_index("gx") * lax.axis_size("gy") + lax.axis_index("gy")
+    row_id = index * rows + lax.broadcasted_iota(jnp.int32, (rows, 1), 0)
+    scale = jnp.zeros((rows, 1), jnp.float32)
     low = 0
-    inside = []
-    for count in row_counts:
-        inside.append(((row_id >= low) & (row_id < low + count)).astype(jnp.float32))
+    for place, count in enumerate(row_counts):
+        inside = (row_id >= low) & (row_id < low + count)
+        mean = square_ref[place : place + 1, :1] / (count * feature)
+        scale = jnp.where(inside, lax.rsqrt(mean + 1e-06), scale)
         low += count
-    row_squares = jnp.sum(piece * piece, axis=1, keepdims=True)
-    squares = jnp.stack([jnp.sum(row_squares * mask) for mask in inside])
-    squares = sum_everywhere(jnp.broadcast_to(squares[:, None], (len(row_counts), 128)))
-    scale = jnp.zeros((rows, 1), jnp.float32)
-    for place, count in enumerate(row_counts):
-        inverse = lax.rsqrt(squares[place, 0] / (count * feature) + 1e-06)
-        scale = scale + inside[place] * inverse
-    return (piece * scale).astype(jnp.bfloat16).reshape(rows * feature)
+    grad_ref[...] = (piece * scale).astype(jnp.bfloat16)
+
+
+def directions(terms, row_counts):
+    shape = terms[0].shape
+    params = pltpu.CompilerParams(vmem_limit_bytes=4 << 20)
+    piece, squares = pl.pallas_call(
+        functools.partial(squares_kernel, row_counts),
+        out_shape=[
+            jax.ShapeDtypeStruct(shape, jnp.float32),
+            jax.ShapeDtypeStruct((len(row_counts), 128), jnp.float32),
+        ],
+        in_specs=[VMEM] * len(terms),
+        out_specs=[VMEM] * 2,
+        compiler_params=params,
+        name="squares",
+    )(*terms)
+    squares = sum_everywhere(squares)
+    grads = pl.pallas_call(
+        functools.partial(scale_kernel, row_counts),
+        out_shape=jax.ShapeDtypeStruct(shape, jnp.bfloat16),
+        in_specs=[VMEM] * 2,
+        out_specs=VMEM,
+        compiler_params=params,
+        name="scale",
+    )(piece, squares)
+    return grads.reshape(shape[0] * shape[1])
 
 
 def solution(mesh):
@@ -459,6 +535,7 @@
         P("gx", "gy", None),
         P("gx", "gy", None, None),
     )
+
     return jax.shard_map(
         on_device,
         mesh=mesh,

time: 114 us -> 107 us (0.939)
  local copies, waits for them, and re-layouts: 5.77 us -> 13.2 us
  Pallas kernels: 26.7 us -> 20.6 us
  other arithmetic: 6.93 us -> 1.38 us
  between operations: 3.56 us -> 0.86 us
  starting transfers between devices: 25 us -> 23.2 us
  waiting for transfers between devices: 45.6 us -> 47.1 us
    ppermute x11, waiting for transfers between devices: 33.1 us -> 42.9 us  [swap(): return lax.ppermute(values, ('gx', 'gy'), pairs)]
    ppermute x6, waiting for transfers between devices: 12.5 us -> 4.12 us  [move(): return lax.ppermute(values, axis, pairs)]
    unnamed x21 -> x41, local copies, waits for them, and re-layouts: 4.9 us -> 13 us
    pallas_call x1, Pallas kernels: 14.8 us -> 10 us  [main(): pl.pallas_call(functools.partial(main_kernel, chosen, rows), out_shape=[j...]
    another operation x2 -> x1, other arithmetic: 2.66 us -> 0.2 us  [the longest x1 2.6 us: directions(): squares = jnp.stack([jnp.sum(row_squares * mask) for mask in inside])]
    pallas_call x0 -> x3, Pallas kernels: none -> 2.17 us  [the longest x1 1.9 us: local(): pl.pallas_call(local_kernel, out_shape=[jax.ShapeDtypeStruct((edge_count,...]
    add x1, other arithmetic: 2.69 us -> 0.84 us  [scatter_sum(): total = keep + swap(send, (0, 0), 1).astype(jnp.float32)]
    pallas_call x1, Pallas kernels: 7.68 us -> 6.05 us  [tail(): pl.pallas_call(functools.partial(tail_kernel, chosen), out_shape=[jax.Sha...]
  transfers between devices with their start and end apart: 17 -> 17, of which waited for: 12 -> 10; matrix products, arithmetic and copies ran while one was open for 2% -> 1% of each run, Pallas kernels for 7% -> 9%
where the time goes in v3:
time: 107 us; the launch traced here: 106 us
  waiting for transfers between devices  47.1 us (44%)
  starting transfers between devices  23.2 us (22%)
  Pallas kernels  20.6 us (19%)
  local copies, waits for them, and re-layouts  13.2 us (12%)
  other arithmetic  1.38 us (1%)
    ppermute x11, waiting for transfers between devices, swap(): return lax.ppermute(values, ('gx', 'gy'), pairs)  42.9 us
    unnamed x41, local copies, waits for them, and re-layouts  13 us
    ppermute x11, starting transfers between devices, swap(): return lax.ppermute(values, ('gx', 'gy'), pairs)  12 us
    ppermute x6, starting transfers between devices, move(): return lax.ppermute(values, axis, pairs)  11.3 us
    pallas_call x1, Pallas kernels, main(): pl.pallas_call(functools.partial(main_kernel, chosen, rows), out_shape=[j...  10 us
    pallas_call x1, Pallas kernels, tail(): pl.pallas_call(functools.partial(tail_kernel, chosen), out_shape=[jax.Sha...  6.05 us
    ppermute x6, waiting for transfers between devices, move(): return lax.ppermute(values, axis, pairs)  4.12 us
  transfers between devices with their start and end apart: 17, of which 10 were waited for; matrix products, arithmetic and copies ran while one was open for 1% of the time, Pallas kernels for 9%

profile of v3, /device:TPU:0, one launch (start us, length us, event | category | flops | bytes accessed | tf_op | source)
XLA Modules:
  0.0 106.3 jit_solution(1866271680132199545)
XLA Ops:
  0.7 0.8 copy.19.list_ref
  1.4 0.9 copy-done
  2.4 0.7 copy-done.3
  3.1 0.7 pack.1
  3.8 0.7 collective-permute-start
  4.4 5.8 %collective-permute-start.1 = (bf16[2,128,512]{2,1,0:T(8,128)(2,1)S(1)}, bf16[2,128,512]{2,1,0:T(8,128)(2,1)S(1)}, u32[]{:S(2)}, u32[]{:S(2)}) collective-permute-start(bf16[2,128,512]{2,1,0:T(8,128)(2,1)S(1)} %get-tuple-element.22), channel_id=1, source_target_pairs={{0,2},{2,0},{4,6},{6,4},{8,10},{10,8},{12,14},{14,12},{16,18},{18,... | collective-permute-start | bytes 786440 | tf_op jit(solution)/shard_map/ppermute | solution.py:104
  10.2 0.7 copy.24
  10.9 0.9 copy-done.1
  11.8 1.4 %copy-done.5 = bf16[1536,512]{1,0:T(8,128)(2,1)S(1)} copy-done((bf16[1536,512]{1,0:T(8,128)(2,1)S(1)}, bf16[1536,512]{1,0:T(8,128)(2,1)}, u32[]{:S(2)}) %copy-start.5) | copy-done | bytes 1572888
  13.2 1.1 %copy-done.8 = bf16[1,1,768,512]{3,2,1,0:T(8,128)(2,1)S(1)} copy-done((bf16[1,1,768,512]{3,2,1,0:T(8,128)(2,1)S(1)}, bf16[1,1,768,512]{3,2,1,0:T(8,128)(2,1)}, u32[]{:S(2)}) %copy-start.8) | copy-done | bytes 786456
  14.4 0.7 copy-done.14
  15.1 0.7 copy-done.16
  15.7 1.9 %local_part.1 = (f32[768,512]{1,0:T(8,128)S(1)}, bf16[768,512]{1,0:T(8,128)(2,1)S(1)}) custom-call(s32[1,1,6]{2,1,0:T(1,128)S(1)} %copy-done.16, bf16[2,128,512]{2,1,0:T(8,128)(2,1)S(1)} %bitcast.24, bf16[768,512]{1,0:T(8,128)(2,1)S(1)} %bitcast.28, bf16[1536,512]{1,0:T(8,128)(2,1)S(1)} %copy-done.5, f32[1,512]{1,0:T(1,128)S(1)} %bitcast.33), custom_call_target="tpu_custom_call" | custom-call | flops 805306368 | bytes 4194304 | tf_op jit(solution)/shard_map/local_part/pallas_call | solution.py:149
  17.6 4.1 %collective-permute-done.1.refs_1_ = bf16[2,128,512]{2,1,0:T(8,128)(2,1)S(1)} collective-permute-done((bf16[2,128,512]{2,1,0:T(8,128)(2,1)S(1)}, bf16[2,128,512]{2,1,0:T(8,128)(2,1)S(1)}, u32[]{:S(2)}, u32[]{:S(2)}) %collective-permute-start.1) | collective-permute-done | bytes 262176 | tf_op jit(solution)/shard_map/ppermute | solution.py:104
  21.8 1.1 %copy-done.9 = bf16[1,1,768,512]{3,2,1,0:T(8,128)(2,1)S(1)} copy-done((bf16[1,1,768,512]{3,2,1,0:T(8,128)(2,1)S(1)}, bf16[1,1,768,512]{3,2,1,0:T(8,128)(2,1)}, u32[]{:S(2)}) %copy-start.9) | copy-done | bytes 786456
  22.9 1.1 %copy-done.10 = bf16[1,1,768,512]{3,2,1,0:T(8,128)(2,1)S(1)} copy-done((bf16[1,1,768,512]{3,2,1,0:T(8,128)(2,1)S(1)}, bf16[1,1,768,512]{3,2,1,0:T(8,128)(2,1)}, u32[]{:S(2)}) %copy-start.10) | copy-done | bytes 786456
  24.1 1.0 copy-done.11
  25.1 1.0 copy-done.12
  26.2 10.0 %layer.1 = (bf16[256,512]{1,0:T(8,128)(2,1)}, bf16[768,512]{1,0:T(8,128)(2,1)S(1)}, f32[256,512]{1,0:T(8,128)S(1)}, bf16[16,112,512]{2,1,0:T(8,128)(2,1)S(1)}, f32[16,112,512]{2,1,0:T(8,128)S(1)}) custom-call(bf16[2,128,512]{2,1,0:T(8,128)(2,1)S(1)} %collective-permute-done.refs_0_, bf16[2,128,512]{2,1,0:T(8,128)(2,1)S(1)} %collective-permute-done.1.refs_1_, ...), custom_call_target="tpu_custom_call" | custom-call | flops 4831838208 | bytes 12582912 | tf_op jit(solution)/shard_map/layer/pallas_call | solution.py:275
  36.2 3.8 %collective-permute-done.6 = bf16[16,112,512]{2,1,0:T(8,128)(2,1)S(1)} collective-permute-done((bf16[16,112,512]{2,1,0:T(8,128)(2,1)S(1)}, bf16[16,112,512]{2,1,0:T(8,128)(2,1)S(1)}, u32[]{:S(2)}, u32[]{:S(2)}) %collective-permute-start.6) | collective-permute-done | bytes 1835040 | tf_op jit(solution)/shard_map/ppermute | solution.py:18
  40.0 0.8 convert_add_fusion
  40.8 0.1 slice.57
  41.0 1.9 %collective-permute-start.7 = (bf16[8,112,512]{2,1,0:T(8,128)(2,1)S(1)}, bf16[8,112,512]{2,1,0:T(8,128)(2,1)S(1)}, u32[]{:S(2)}, u32[]{:S(2)}) collective-permute-start(bf16[8,112,512]{2,1,0:T(8,128)(2,1)S(1)} %slice.57), channel_id=1, source_target_pairs={{0,2},{1,5},{2,0},{3,7},{4,6},{5,1},{6,4},{7,3},{8,10},{9,13},{10,... | collective-permute-start | bytes 2752520 | tf_op jit(solution)/shard_map/ppermute | solution.py:18
  42.9 11.6 %collective-permute-done.7 = bf16[8,112,512]{2,1,0:T(8,128)(2,1)S(1)} collective-permute-done((bf16[8,112,512]{2,1,0:T(8,128)(2,1)S(1)}, bf16[8,112,512]{2,1,0:T(8,128)(2,1)S(1)}, u32[]{:S(2)}, u32[]{:S(2)}) %collective-permute-start.7) | collective-permute-done | bytes 917536 | tf_op jit(solution)/shard_map/ppermute | solution.py:18
  54.4 0.3 slice_add_fusion
  54.7 0.1 slice.58
  54.8 0.1 collective-permute-start.8
  54.9 8.5 %collective-permute-done.8 = bf16[4,112,512]{2,1,0:T(8,128)(2,1)S(1)} collective-permute-done((bf16[4,112,512]{2,1,0:T(8,128)(2,1)S(1)}, bf16[4,112,512]{2,1,0:T(8,128)(2,1)S(1)}, u32[]{:S(2)}, u32[]{:S(2)}) %collective-permute-start.8) | collective-permute-done | bytes 458784 | tf_op jit(solution)/shard_map/ppermute | solution.py:18
  63.4 0.2 fusion
  63.6 1.6 %collective-permute-start.9 = (bf16[112,512]{1,0:T(8,128)(2,1)S(1)}, bf16[112,512]{1,0:T(8,128)(2,1)S(1)}, u32[]{:S(2)}, u32[]{:S(2)}) collective-permute-start(bf16[112,512]{1,0:T(8,128)(2,1)S(1)} %get-tuple-element.42), channel_id=1, source_target_pairs={{0,8},{1,9},{2,10},{3,11},{4,12},{5,13},{6,14},{7,15},{8,0},{9,1},... | collective-permute-start | bytes 344072 | tf_op jit(solution)/shard_map/ppermute | solution.py:18
  65.2 6.0 %input_grads.1 = (bf16[768,512]{1,0:T(8,128)(2,1)}, f32[2,128,512]{2,1,0:T(8,128)S(1)}, bf16[2,128,512]{2,1,0:T(8,128)(2,1)S(1)}, bf16[2,128,512]{2,1,0:T(8,128)(2,1)S(1)}, bf16[2,128,512]{2,1,0:T(8,128)(2,1)S(1)}) custom-call(s32[1,1,6]{2,1,0:T(1,128)S(1)} %copy-done.17, s32[1,1,6]{2,1,0:T(1,128)S(1)} %copy-done.18, s32[6,128]{1,0:T(8,128)S(1)} %bitcast.27, ...), custom_call_target="tpu_custom_call" | custom-call | flops 1207959552 | bytes 6291456 | tf_op jit(solution)/shard_map/input_grads/pallas_call | solution.py:345
  71.3 0.7 collective-permute-start.3
  72.0 4.2 %collective-permute-start.4 = (bf16[2,128,512]{2,1,0:T(8,128)(2,1)S(1)}, bf16[2,128,512]{2,1,0:T(8,128)(2,1)S(1)}, u32[]{:S(2)}, u32[]{:S(2)}) collective-permute-start(bf16[2,128,512]{2,1,0:T(8,128)(2,1)S(1)} %get-tuple-element.31), channel_id=1, source_target_pairs={{0,2},{2,0},{4,6},{6,4},{8,10},{10,8},{12,14},{14,12},{16,18},{18,... | collective-permute-start | bytes 786440 | tf_op jit(solution)/shard_map/ppermute | solution.py:104
  76.1 2.6 %collective-permute-start.10 = (bf16[112,512]{1,0:T(8,128)(2,1)S(1)}, bf16[112,512]{1,0:T(8,128)(2,1)S(1)}, u32[]{:S(2)}, u32[]{:S(2)}) collective-permute-start(bf16[112,512]{1,0:T(8,128)(2,1)S(1)} %get-tuple-element.41), channel_id=1, source_target_pairs={{0,16},{1,17},{2,18},{3,19},{4,20},{5,21},{6,22},{7,23},{8,24},{9,... | collective-permute-start | bytes 344072 | tf_op jit(solution)/shard_map/ppermute | solution.py:18
  78.8 9.5 %collective-permute-done.10.refs_2_ = bf16[112,512]{1,0:T(8,128)(2,1)S(1)} collective-permute-done((bf16[112,512]{1,0:T(8,128)(2,1)S(1)}, bf16[112,512]{1,0:T(8,128)(2,1)S(1)}, u32[]{:S(2)}, u32[]{:S(2)}) %collective-permute-start.10) | collective-permute-done | bytes 114720 | tf_op jit(solution)/shard_map/ppermute | solution.py:18
  88.2 0.2 squares.1
  88.4 0.1 collective-permute-start.12
  88.5 1.1 %collective-permute-done.12 = f32[4,128]{1,0:T(4,128)S(1)} collective-permute-done((f32[4,128]{1,0:T(4,128)S(1)}, f32[4,128]{1,0:T(4,128)S(1)}, u32[]{:S(2)}, u32[]{:S(2)}) %collective-permute-start.12) | collective-permute-done | bytes 2080 | tf_op jit(solution)/shard_map/ppermute | solution.py:18
  89.6 3.6 %collective-permute-done.13 = f32[4,128]{1,0:T(4,128)S(1)} collective-permute-done((f32[4,128]{1,0:T(4,128)S(1)}, f32[4,128]{1,0:T(4,128)S(1)}, u32[]{:S(2)}, u32[]{:S(2)}) %collective-permute-start.13) | collective-permute-done | bytes 2080 | tf_op jit(solution)/shard_map/ppermute | solution.py:18
  93.2 0.3 collective-permute-start.14
  93.5 3.3 %collective-permute-done.14 = f32[4,128]{1,0:T(4,128)S(1)} collective-permute-done((f32[4,128]{1,0:T(4,128)S(1)}, f32[4,128]{1,0:T(4,128)S(1)}, u32[]{:S(2)}, u32[]{:S(2)}) %collective-permute-start.14) | collective-permute-done | bytes 2080 | tf_op jit(solution)/shard_map/ppermute | solution.py:18
  96.8 2.6 %collective-permute-start.15 = (f32[4,128]{1,0:T(4,128)S(1)}, f32[4,128]{1,0:T(4,128)S(1)}, u32[]{:S(2)}, u32[]{:S(2)}) collective-permute-start(f32[4,128]{1,0:T(4,128)S(1)} %add.29), channel_id=1, source_target_pairs={{0,8},{1,9},{2,10},{3,11},{4,12},{5,13},{6,14},{7,15},{8,0},{9,1},... | collective-permute-start | bytes 6152 | tf_op jit(solution)/shard_map/ppermute | solution.py:18
  99.4 1.6 %collective-permute-done.15 = f32[4,128]{1,0:T(4,128)S(1)} collective-permute-done((f32[4,128]{1,0:T(4,128)S(1)}, f32[4,128]{1,0:T(4,128)S(1)}, u32[]{:S(2)}, u32[]{:S(2)}) %collective-permute-start.15) | collective-permute-done | bytes 2080 | tf_op jit(solution)/shard_map/ppermute | solution.py:18
  101.0 2.7 %collective-permute-start.16 = (f32[4,128]{1,0:T(4,128)S(1)}, f32[4,128]{1,0:T(4,128)S(1)}, u32[]{:S(2)}, u32[]{:S(2)}) collective-permute-start(f32[4,128]{1,0:T(4,128)S(1)} %add.30), channel_id=1, source_target_pairs={{0,16},{1,17},{2,18},{3,19},{4,20},{5,21},{6,22},{7,23},{8,24},{9,... | collective-permute-start | bytes 6152 | tf_op jit(solution)/shard_map/ppermute | solution.py:18
  103.7 1.6 %node_grad.1 = bf16[2,128,512]{2,1,0:T(8,128)(2,1)} custom-call(s32[1,1,4]{2,1,0:T(1,128)S(1)} %copy-done.4, s32[1,1,4,2]{3,2,1,0:T(4,128)S(1)} %copy.19.list_ref, f32[2,128,512]{2,1,0:T(8,128)S(1)} %get-tuple-element.29.part_ref, bf16[2,128,512]{2,1,0:T(8,128)(2,1)S(1)} %collective-permute-done.3.refs_0_, ...), custom_call_target="tpu_custom_call" | custom-call | bytes 2097152 | tf_op jit(solution)/shard_map/node_grad/pallas_call | solution.py:375
  105.3 0.1 collective-permute-done.16
  105.5 0.1 scale.1
  105.6 0.7 copy.22
  (46 shorter events, 0.1 us)
Async XLA Ops:
  0.6 21.1 %copy-start.17 = (s32[1,1,6]{2,1,0:T(1,128)S(1)}, s32[1,1,6]{2,1,0:T(1,128)}, u32[]{:S(2)}) copy-start(s32[1,1,6]{2,1,0:T(1,128)} %recv_ref.3) | copy-start | bytes 76
  0.6 21.1 %copy-start.18 = (s32[1,1,6]{2,1,0:T(1,128)S(1)}, s32[1,1,6]{2,1,0:T(1,128)}, u32[]{:S(2)}) copy-start(s32[1,1,6]{2,1,0:T(1,128)} %send_ref.1) | copy-start | bytes 76
  0.7 21.1 %copy-start.15 = (f32[512]{0:T(512)S(1)}, f32[512]{0:T(512)}, u32[]{:S(2)}) copy-start(f32[512]{0:T(512)} %param.21) | copy-start | bytes 6148
  1.4 0.9 copy-start
  2.4 0.7 copy-start.3
  3.1 18.7 %copy-start.2 = (bf16[1,1,256,512]{3,2,1,0:T(8,128)(2,1)S(1)}, bf16[1,1,256,512]{3,2,1,0:T(8,128)(2,1)}, u32[]{:S(2)}) copy-start(bf16[1,1,256,512]{3,2,1,0:T(8,128)(2,1)} %param.15) | copy-start | bytes 786436
  3.8 13.9 %collective-permute-start = (bf16[2,128,512]{2,1,0:T(8,128)(2,1)S(1)}, bf16[2,128,512]{2,1,0:T(8,128)(2,1)S(1)}, u32[]{:S(2)}, u32[]{:S(2)}) collective-permute-start(bf16[2,128,512]{2,1,0:T(8,128)(2,1)S(1)} %get-tuple-element.21), channel_id=1, source_target_pairs={{2,4},{4,2},{6,8},{8,6},{10,12},{12,10},{14,16},{16,14},{18,20},{2... | collective-permute-start | bytes 786440 | tf_op jit(solution)/shard_map/ppermute | solution.py:104
  4.4 17.3 %collective-permute-start.1 = (bf16[2,128,512]{2,1,0:T(8,128)(2,1)S(1)}, bf16[2,128,512]{2,1,0:T(8,128)(2,1)S(1)}, u32[]{:S(2)}, u32[]{:S(2)}) collective-permute-start(bf16[2,128,512]{2,1,0:T(8,128)(2,1)S(1)} %get-tuple-element.22), channel_id=1, source_target_pairs={{0,2},{2,0},{4,6},{6,4},{8,10},{10,8},{12,14},{14,12},{16,18},{18,... | collective-permute-start | bytes 786440 | tf_op jit(solution)/shard_map/ppermute | solution.py:104
  10.2 11.6 %collective-permute-start.2 = (bf16[2,128,512]{2,1,0:T(8,128)(2,1)S(1)}, bf16[2,128,512]{2,1,0:T(8,128)(2,1)S(1)}, u32[]{:S(2)}, u32[]{:S(2)}) collective-permute-start(bf16[2,128,512]{2,1,0:T(8,128)(2,1)S(1)} %get-tuple-element.23), channel_id=1, source_target_pairs={{0,1},{1,0},{2,3},{3,2},{4,5},{5,4},{6,7},{7,6},{8,9},{9,8},{10,11... | collective-permute-start | bytes 786440 | tf_op jit(solution)/shard_map/ppermute | solution.py:104
  10.9 0.9 copy-start.1
  11.8 1.4 %copy-start.5 = (bf16[1536,512]{1,0:T(8,128)(2,1)S(1)}, bf16[1536,512]{1,0:T(8,128)(2,1)}, u32[]{:S(2)}) copy-start(bf16[1536,512]{1,0:T(8,128)(2,1)} %ew1_ref.3) | copy-start | bytes 4718596
  13.2 1.1 %copy-start.8 = (bf16[1,1,768,512]{3,2,1,0:T(8,128)(2,1)S(1)}, bf16[1,1,768,512]{3,2,1,0:T(8,128)(2,1)}, u32[]{:S(2)}) copy-start(bf16[1,1,768,512]{3,2,1,0:T(8,128)(2,1)} %param.16) | copy-start | bytes 2359300
  14.4 0.7 copy-start.14
  15.1 0.7 copy-start.16
  15.7 6.1 %copy-start.6 = (bf16[1536,512]{1,0:T(8,128)(2,1)S(1)}, bf16[1536,512]{1,0:T(8,128)(2,1)}, u32[]{:S(2)}) copy-start(bf16[1536,512]{1,0:T(8,128)(2,1)} %ew1_ref.3) | copy-start | bytes 4718596
  15.7 6.1 %copy-start.7 = (bf16[1024,512]{1,0:T(8,128)(2,1)S(1)}, bf16[1024,512]{1,0:T(8,128)(2,1)}, u32[]{:S(2)}) copy-start(bf16[1024,512]{1,0:T(8,128)(2,1)} %refs_12_.1) | copy-start | bytes 3145732
  15.7 6.1 %copy-start.13 = (bf16[1,1,256,512]{3,2,1,0:T(8,128)(2,1)S(1)}, bf16[1,1,256,512]{3,2,1,0:T(8,128)(2,1)}, u32[]{:S(2)}) copy-start(bf16[1,1,256,512]{3,2,1,0:T(8,128)(2,1)} %param.23) | copy-start | bytes 786436
  21.8 1.1 %copy-start.9 = (bf16[1,1,768,512]{3,2,1,0:T(8,128)(2,1)S(1)}, bf16[1,1,768,512]{3,2,1,0:T(8,128)(2,1)}, u32[]{:S(2)}) copy-start(bf16[1,1,768,512]{3,2,1,0:T(8,128)(2,1)} %param.16) | copy-start | bytes 2359300
  22.9 1.1 %copy-start.10 = (bf16[1,1,768,512]{3,2,1,0:T(8,128)(2,1)S(1)}, bf16[1,1,768,512]{3,2,1,0:T(8,128)(2,1)}, u32[]{:S(2)}) copy-start(bf16[1,1,768,512]{3,2,1,0:T(8,128)(2,1)} %param.24) | copy-start | bytes 2359300
  24.1 1.0 copy-start.11
  25.1 1.0 copy-start.12
  36.2 3.8 %collective-permute-start.6 = (bf16[16,112,512]{2,1,0:T(8,128)(2,1)S(1)}, bf16[16,112,512]{2,1,0:T(8,128)(2,1)S(1)}, u32[]{:S(2)}, u32[]{:S(2)}) collective-permute-start(bf16[16,112,512]{2,1,0:T(8,128)(2,1)S(1)} %get-tuple-element.35), channel_id=1, source_target_pairs={{0,1},{1,0},{2,3},{3,2},{4,5},{5,4},{6,7},{7,6},{8,9},{9,8},{10,11... | collective-permute-start | bytes 5505032 | tf_op jit(solution)/shard_map/ppermute | solution.py:18
  41.0 13.5 %collective-permute-start.7 = (bf16[8,112,512]{2,1,0:T(8,128)(2,1)S(1)}, bf16[8,112,512]{2,1,0:T(8,128)(2,1)S(1)}, u32[]{:S(2)}, u32[]{:S(2)}) collective-permute-start(bf16[8,112,512]{2,1,0:T(8,128)(2,1)S(1)} %slice.57), channel_id=1, source_target_pairs={{0,2},{1,5},{2,0},{3,7},{4,6},{5,1},{6,4},{7,3},{8,10},{9,13},{10,... | collective-permute-start | bytes 2752520 | tf_op jit(solution)/shard_map/ppermute | solution.py:18
  54.8 8.5 %collective-permute-start.8 = (bf16[4,112,512]{2,1,0:T(8,128)(2,1)S(1)}, bf16[4,112,512]{2,1,0:T(8,128)(2,1)S(1)}, u32[]{:S(2)}, u32[]{:S(2)}) collective-permute-start(bf16[4,112,512]{2,1,0:T(8,128)(2,1)S(1)} %slice.58), channel_id=1, source_target_pairs={{0,4},{1,3},{2,6},{3,1},{4,0},{5,7},{6,2},{7,5},{8,12},{9,11},{10,... | collective-permute-start | bytes 1376264 | tf_op jit(solution)/shard_map/ppermute | solution.py:18
  63.6 15.1 %collective-permute-start.9 = (bf16[112,512]{1,0:T(8,128)(2,1)S(1)}, bf16[112,512]{1,0:T(8,128)(2,1)S(1)}, u32[]{:S(2)}, u32[]{:S(2)}) collective-permute-start(bf16[112,512]{1,0:T(8,128)(2,1)S(1)} %get-tuple-element.42), channel_id=1, source_target_pairs={{0,8},{1,9},{2,10},{3,11},{4,12},{5,13},{6,14},{7,15},{8,0},{9,1},... | collective-permute-start | bytes 344072 | tf_op jit(solution)/shard_map/ppermute | solution.py:18
  65.2 38.5 %copy-start.4 = (s32[1,1,4]{2,1,0:T(1,128)S(1)}, s32[1,1,4]{2,1,0:T(1,128)}, u32[]{:S(2)}) copy-start(s32[1,1,4]{2,1,0:T(1,128)} %count_ref.3) | copy-start | bytes 52
  71.3 32.4 %collective-permute-start.3 = (bf16[2,128,512]{2,1,0:T(8,128)(2,1)S(1)}, bf16[2,128,512]{2,1,0:T(8,128)(2,1)S(1)}, u32[]{:S(2)}, u32[]{:S(2)}) collective-permute-start(bf16[2,128,512]{2,1,0:T(8,128)(2,1)S(1)} %get-tuple-element.30), channel_id=1, source_target_pairs={{2,4},{4,2},{6,8},{8,6},{10,12},{12,10},{14,16},{16,14},{18,20},{2... | collective-permute-start | bytes 786440 | tf_op jit(solution)/shard_map/ppermute | solution.py:104
  72.0 31.7 %collective-permute-start.4 = (bf16[2,128,512]{2,1,0:T(8,128)(2,1)S(1)}, bf16[2,128,512]{2,1,0:T(8,128)(2,1)S(1)}, u32[]{:S(2)}, u32[]{:S(2)}) collective-permute-start(bf16[2,128,512]{2,1,0:T(8,128)(2,1)S(1)} %get-tuple-element.31), channel_id=1, source_target_pairs={{0,2},{2,0},{4,6},{6,4},{8,10},{10,8},{12,14},{14,12},{16,18},{18,... | collective-permute-start | bytes 786440 | tf_op jit(solution)/shard_map/ppermute | solution.py:104
  76.1 27.6 %collective-permute-start.5 = (bf16[2,128,512]{2,1,0:T(8,128)(2,1)S(1)}, bf16[2,128,512]{2,1,0:T(8,128)(2,1)S(1)}, u32[]{:S(2)}, u32[]{:S(2)}) collective-permute-start(bf16[2,128,512]{2,1,0:T(8,128)(2,1)S(1)} %get-tuple-element.32), channel_id=1, source_target_pairs={{0,1},{1,0},{2,3},{3,2},{4,5},{5,4},{6,7},{7,6},{8,9},{9,8},{10,11... | collective-permute-start | bytes 786440 | tf_op jit(solution)/shard_map/ppermute | solution.py:104
  76.1 12.1 %collective-permute-start.10 = (bf16[112,512]{1,0:T(8,128)(2,1)S(1)}, bf16[112,512]{1,0:T(8,128)(2,1)S(1)}, u32[]{:S(2)}, u32[]{:S(2)}) collective-permute-start(bf16[112,512]{1,0:T(8,128)(2,1)S(1)} %get-tuple-element.41), channel_id=1, source_target_pairs={{0,16},{1,17},{2,18},{3,19},{4,20},{5,21},{6,22},{7,23},{8,24},{9,... | collective-permute-start | bytes 344072 | tf_op jit(solution)/shard_map/ppermute | solution.py:18
  78.7 9.5 %collective-permute-start.11 = (bf16[112,512]{1,0:T(8,128)(2,1)S(1)}, bf16[112,512]{1,0:T(8,128)(2,1)S(1)}, u32[]{:S(2)}, u32[]{:S(2)}) collective-permute-start(bf16[112,512]{1,0:T(8,128)(2,1)S(1)} %get-tuple-element.40), channel_id=1, source_target_pairs={{0,24},{1,25},{2,26},{3,27},{4,28},{5,29},{6,30},{7,31},{8,16},{9,... | collective-permute-start | bytes 344072 | tf_op jit(solution)/shard_map/ppermute | solution.py:18
  88.4 1.2 %collective-permute-start.12 = (f32[4,128]{1,0:T(4,128)S(1)}, f32[4,128]{1,0:T(4,128)S(1)}, u32[]{:S(2)}, u32[]{:S(2)}) collective-permute-start(f32[4,128]{1,0:T(4,128)S(1)} %get-tuple-element.37), channel_id=1, source_target_pairs={{0,1},{1,0},{2,3},{3,2},{4,5},{5,4},{6,7},{7,6},{8,9},{9,8},{10,11... | collective-permute-start | bytes 6152 | tf_op jit(solution)/shard_map/ppermute | solution.py:18
  89.6 3.6 %collective-permute-start.13 = (f32[4,128]{1,0:T(4,128)S(1)}, f32[4,128]{1,0:T(4,128)S(1)}, u32[]{:S(2)}, u32[]{:S(2)}) collective-permute-start(f32[4,128]{1,0:T(4,128)S(1)} %add.27), channel_id=1, source_target_pairs={{0,2},{1,3},{2,0},{3,1},{4,6},{5,7},{6,4},{7,5},{8,10},{9,11},{10,... | collective-permute-start | bytes 6152 | tf_op jit(solution)/shard_map/ppermute | solution.py:18
  93.2 3.6 %collective-permute-start.14 = (f32[4,128]{1,0:T(4,128)S(1)}, f32[4,128]{1,0:T(4,128)S(1)}, u32[]{:S(2)}, u32[]{:S(2)}) collective-permute-start(f32[4,128]{1,0:T(4,128)S(1)} %add.28), channel_id=1, source_target_pairs={{0,4},{1,5},{2,6},{3,7},{4,0},{5,1},{6,2},{7,3},{8,12},{9,13},{10,... | collective-permute-start | bytes 6152 | tf_op jit(solution)/shard_map/ppermute | solution.py:18
  96.8 4.2 %collective-permute-start.15 = (f32[4,128]{1,0:T(4,128)S(1)}, f32[4,128]{1,0:T(4,128)S(1)}, u32[]{:S(2)}, u32[]{:S(2)}) collective-permute-start(f32[4,128]{1,0:T(4,128)S(1)} %add.29), channel_id=1, source_target_pairs={{0,8},{1,9},{2,10},{3,11},{4,12},{5,13},{6,14},{7,15},{8,0},{9,1},... | collective-permute-start | bytes 6152 | tf_op jit(solution)/shard_map/ppermute | solution.py:18
  101.0 4.5 %collective-permute-start.16 = (f32[4,128]{1,0:T(4,128)S(1)}, f32[4,128]{1,0:T(4,128)S(1)}, u32[]{:S(2)}, u32[]{:S(2)}) collective-permute-start(f32[4,128]{1,0:T(4,128)S(1)} %add.30), channel_id=1, source_target_pairs={{0,16},{1,17},{2,18},{3,19},{4,20},{5,21},{6,22},{7,23},{8,24},{9,... | collective-permute-start | bytes 6152 | tf_op jit(solution)/shard_map/ppermute | solution.py:18

commit v4 on v3

--- a/solution.py
+++ b/solution.py
@@ -37,6 +37,21 @@
 LAYER_GRANT = 34 << 20
 VMEM = pl.BlockSpec(memory_space=pltpu.VMEM)
 SMEM = pl.BlockSpec(memory_space=pltpu.SMEM)
+HBM = pl.BlockSpec(memory_space=pltpu.HBM)
+
+
+def in_hbm(values):
+    return pltpu.with_memory_space_constraint(values, pltpu.HBM)
+
+
+def fetch(sources, targets, semaphores):
+    copies = [
+        pltpu.make_async_copy(source, target, semaphores.at[place])
+        for place, (source, target) in enumerate(zip(sources, targets))
+    ]
+    for copy in copies:
+        copy.start()
+    return copies
 
 
 def silu_slope(values):
@@ -104,7 +119,10 @@
     return lax.ppermute(values, axis, pairs)
 
 
-def pack_kernel(chosen, nodes_ref, count_ref, list_ref, *packet_refs):
+def pack_kernel(chosen, nodes_hbm, count_ref, list_ref, *refs):
+    packet_refs, (nodes_ref, semaphores) = refs[:-2], refs[-2:]
+    (copy,) = fetch([nodes_hbm], [nodes_ref], semaphores)
+    copy.wait()
     for packet_ref, route in zip(packet_refs, chosen):
         direction = sent_to(*route)
         for slot in range(packet_ref.shape[0]):
@@ -120,16 +138,26 @@
     return pl.pallas_call(
         functools.partial(pack_kernel, chosen),
         out_shape=[packet] * len(chosen),
-        in_specs=[VMEM, SMEM, SMEM],
+        in_specs=[HBM, SMEM, SMEM],
         out_specs=[VMEM] * len(chosen),
+        scratch_shapes=[
+            pltpu.VMEM(node_blocks.shape, node_blocks.dtype),
+            pltpu.SemaphoreType.DMA((1,)),
+        ],
         compiler_params=pltpu.CompilerParams(vmem_limit_bytes=4 << 20),
         name="pack",
-    )(node_blocks, send_count, send_list)
-
-
-def local_kernel(recv_ref, nodes_ref, edges_ref, ew1_ref, eb1_ref, part_ref, h_recv_ref):
+    )(in_hbm(node_blocks), in_hbm(send_count), in_hbm(send_list))
+
+
+def local_kernel(count, recv_ref, *refs):
+    sources, targets = refs[:count], refs[count : 2 * count]
+    part_ref, h_recv_ref, semaphores = refs[2 * count :]
+    copies = fetch(sources, targets, semaphores)
+    nodes_ref, edges_ref, eb1_ref, ew1_ref = targets[:4]
     block, feature = nodes_ref.shape[1:]
     tiles = edges_ref.shape[0] // block
+    for copy in copies[:4]:
+        copy.wait()
     for tile in range(tiles):
         h_recv_ref[tile * block : (tile + 1) * block, :] = nodes_ref[recv_ref[0, 0, tile]]
     chunk = 2 * block if tiles % 2 == 0 else block
@@ -142,24 +170,27 @@
         return 0
 
     lax.fori_loop(0, edges_ref.shape[0] // chunk, visit, 0)
-
-
-def local(recv, node_blocks, edges, edge_w1, edge_b1):
-    edge_count, feature = edges.shape
+    for copy in copies[4:]:
+        copy.wait()
+
+
+def local(recv, *operands):
+    edge_count, feature = operands[1].shape
+    results = [jax.ShapeDtypeStruct(operand.shape, operand.dtype) for operand in operands]
+    results.append(jax.ShapeDtypeStruct((edge_count, feature), jnp.float32))
+    results.append(jax.ShapeDtypeStruct((edge_count, feature), jnp.bfloat16))
     return pl.pallas_call(
-        local_kernel,
-        out_shape=[
-            jax.ShapeDtypeStruct((edge_count, feature), jnp.float32),
-            jax.ShapeDtypeStruct((edge_count, feature), jnp.bfloat16),
-        ],
-        in_specs=[SMEM] + [VMEM] * 4,
-        out_specs=[VMEM] * 2,
-        compiler_params=pltpu.CompilerParams(vmem_limit_bytes=12 << 20),
+        functools.partial(local_kernel, len(operands)),
+        out_shape=results,
+        in_specs=[SMEM] + [HBM] * len(operands),
+        out_specs=[VMEM] * len(results),
+        scratch_shapes=[pltpu.SemaphoreType.DMA((len(operands),))],
+        compiler_params=pltpu.CompilerParams(vmem_limit_bytes=16 << 20),
         cost_estimate=pl.CostEstimate(
-            flops=4 * feature * feature * edge_count, bytes_accessed=4 << 20, transcendentals=0
+            flops=4 * feature * feature * edge_count, bytes_accessed=8 << 20, transcendentals=0
         ),
         name="local_part",
-    )(recv, node_blocks, edges, edge_w1, edge_b1.reshape(1, feature))
+    )(in_hbm(recv), *[in_hbm(operand) for operand in operands])
 
 
 def main_kernel(chosen, rows, *refs):
@@ -294,8 +325,8 @@
         ),
         name="layer",
     )(
-        *halos, recv, send, perm, node_blocks, edges, part, h_recv, edge_w1, edge_w2,
-        node_w1, node_b1.reshape(1, feature), node_w2, node_cot, edge_cot,
+        *halos, in_hbm(recv), in_hbm(send), perm, node_blocks, edges, part, h_recv, edge_w1, edge_w2,
+        node_w1, node_b1, node_w2, node_cot, edge_cot,
     )
     if rows % 16:
         gx_index, gy_index = lax.axis_index("gx"), lax.axis_index("gy")
@@ -353,7 +384,7 @@
             flops=6 * feature * feature * edge_count, bytes_accessed=6 << 20, transcendentals=0
         ),
         name="input_grads",
-    )(recv, send, perm, gea, edge_w1, edge_cot, base)
+    )(in_hbm(recv), in_hbm(send), perm, gea, edge_w1, edge_cot, base)
 
 
 def finish_kernel(chosen, count_ref, list_ref, part_ref, *refs):
@@ -380,7 +411,7 @@
         compiler_params=pltpu.CompilerParams(vmem_limit_bytes=6 << 20),
         cost_estimate=pl.CostEstimate(flops=0, bytes_accessed=2 << 20, transcendentals=0),
         name="node_grad",
-    )(send_count, send_list, part, *packets)
+    )(in_hbm(send_count), in_hbm(send_list), part, *packets)
 
 
 def on_device(
@@ -411,8 +442,13 @@
     perm = tile_perm.reshape(tile_count, block_size)
     packets = pack(node_blocks, send_count, send_list)
     halos = [move(packet, *route) for packet, route in zip(packets, routes())]
-    partial, h_recv = local(tile_recv, node_blocks, edge_rows, edge_w1, edge_b1)
-    weights = (edge_w1, edge_w2, node_w1, node_b1, node_w2)
+    biases = edge_b1.reshape(1, feature), node_b1.reshape(1, feature)
+    *held, partial, h_recv = local(
+        tile_recv, node_blocks, edge_rows, biases[0], edge_w1, perm, edge_w2, node_w1, biases[1],
+        node_w2, cot_node, cot_edge,
+    )
+    node_blocks, edge_rows, _, edge_w1, perm, *weights, cot_node, cot_edge = held
+    weights = [edge_w1] + weights
     node_out, gea, base, away, keep = main(
         halos, tile_recv, tile_send, perm, node_blocks, edge_rows, partial, h_recv, weights,
         cot_node, cot_edge,

time: 107 us -> 101 us (0.944)
  local copies, waits for them, and re-layouts: 13.2 us -> 3.54 us
  waiting for transfers between devices: 47.1 us -> 52.8 us
  starting transfers between devices: 23.2 us -> 17.6 us
  Pallas kernels: 20.6 us -> 24.6 us
    unnamed x41 -> x3, local copies, waits for them, and re-layouts: 13 us -> 3.3 us
    ppermute x11, starting transfers between devices: 12 us -> 6.31 us  [swap(): return lax.ppermute(values, ('gx', 'gy'), pairs)]
    ppermute x11, waiting for transfers between devices: 42.9 us -> 47 us  [swap(): return lax.ppermute(values, ('gx', 'gy'), pairs)]
    pallas_call x1, Pallas kernels: 1.9 us -> 4.47 us  [local(): pl.pallas_call(functools.partial(local_kernel, len(operands)), out_shape=...]
    ppermute x6, waiting for transfers between devices: 4.12 us -> 5.8 us  [move(): return lax.ppermute(values, axis, pairs)]
  transfers between devices with their start and end apart: 17 -> 17, of which waited for: 10 -> 11; matrix products, arithmetic and copies ran while one was open for 1% -> 1% of each run, Pallas kernels for 9% -> 12%
where the time goes in v4:
time: 101 us
  waiting for transfers between devices  52.8 us (52%)
  Pallas kernels  24.6 us (24%)
  starting transfers between devices  17.6 us (17%)
  local copies, waits for them, and re-layouts  3.54 us (4%)
  other arithmetic  1.2 us (1%)
    ppermute x11, waiting for transfers between devices, swap(): return lax.ppermute(values, ('gx', 'gy'), pairs)  47 us
    ppermute x6, starting transfers between devices, move(): return lax.ppermute(values, axis, pairs)  11.3 us
    pallas_call x1, Pallas kernels, main(): pl.pallas_call(functools.partial(main_kernel, chosen, rows), out_shape=[j...  10.2 us
    ppermute x11, starting transfers between devices, swap(): return lax.ppermute(values, ('gx', 'gy'), pairs)  6.31 us
    pallas_call x1, Pallas kernels, tail(): pl.pallas_call(functools.partial(tail_kernel, chosen), out_shape=[jax.Sha...  6.18 us
    ppermute x6, waiting for transfers between devices, move(): return lax.ppermute(values, axis, pairs)  5.8 us
    pallas_call x1, Pallas kernels, local(): pl.pallas_call(functools.partial(local_kernel, len(operands)), out_shape=...  4.47 us
    unnamed x3, local copies, waits for them, and re-layouts  3.3 us
  transfers between devices with their start and end apart: 17, of which 11 were waited for; matrix products, arithmetic and copies ran while one was open for 1% of the time, Pallas kernels for 12%

profile of v4, /device:TPU:0, one launch (start us, length us, event | category | flops | bytes accessed | tf_op | source)
XLA Modules:
  0.0 100.5 jit_solution(13738468568277564039)
XLA Ops:
  0.6 1.3 %copy.19.list_ref = s32[1,1,4,2]{3,2,1,0:T(4,128)} copy(s32[1,1,4,2]{2,3,1,0:T(2,128)} %param.26) | data formatting | bytes 64 | tf_op args[11]
  2.0 1.8 %pack.1 = (bf16[2,128,512]{2,1,0:T(8,128)(2,1)S(1)}, bf16[2,128,512]{2,1,0:T(8,128)(2,1)S(1)}, bf16[2,128,512]{2,1,0:T(8,128)(2,1)S(1)}) custom-call(bf16[2,128,512]{2,1,0:T(8,128)(2,1)} %bitcast.23, s32[1,1,4]{2,1,0:T(1,128)} %count_ref.3, s32[1,1,4,2]{3,2,1,0:T(4,128)} %copy.19.list_ref), custom_call_target="tpu_custom_call" | custom-call | tf_op jit(solution)/shard_map/pack/pallas_call | solution.py:138
  3.7 0.7 collective-permute-start
  4.4 5.8 %collective-permute-start.1 = (bf16[2,128,512]{2,1,0:T(8,128)(2,1)S(1)}, bf16[2,128,512]{2,1,0:T(8,128)(2,1)S(1)}, u32[]{:S(2)}, u32[]{:S(2)}) collective-permute-start(bf16[2,128,512]{2,1,0:T(8,128)(2,1)S(1)} %get-tuple-element.32), channel_id=1, source_target_pairs={{0,2},{2,0},{4,6},{6,4},{8,10},{10,8},{12,14},{14,12},{16,18},{18,... | collective-permute-start | bytes 786440 | tf_op jit(solution)/shard_map/ppermute | solution.py:119
  10.2 0.0 collective-permute-start.2
  10.2 1.3 %copy.24 = s32[1,1,6,128]{3,2,1,0:T(8,128)} copy(s32[1,1,6,128]{3,1,2,0:T(1,128)} %param.29) | data formatting | bytes 6144
  11.5 4.5 %local_part.1 = (bf16[2,128,512]{2,1,0:T(8,128)(2,1)S(1)}, bf16[768,512]{1,0:T(8,128)(2,1)S(1)}, f32[1,512]{1,0:T(1,128)}, bf16[1536,512]{1,0:T(8,128)(2,1)S(1)}...) custom-call(s32[1,1,6]{2,1,0:T(1,128)} %recv_ref.3, ...), custom_call_target="tpu_custom_call" | custom-call | flops 805306368 | bytes 8388608 | tf_op jit(solution)/shard_map/local_part/pallas_call | solution.py:182
  15.9 0.0 collective-permute-done.refs_0_
  15.9 5.8 %collective-permute-done.1.refs_1_ = bf16[2,128,512]{2,1,0:T(8,128)(2,1)S(1)} collective-permute-done((bf16[2,128,512]{2,1,0:T(8,128)(2,1)S(1)}, bf16[2,128,512]{2,1,0:T(8,128)(2,1)S(1)}, u32[]{:S(2)}, u32[]{:S(2)}) %collective-permute-start.1) | collective-permute-done | bytes 262176 | tf_op jit(solution)/shard_map/ppermute | solution.py:119
  21.7 0.0 collective-permute-done.2.refs_2_
  21.7 10.2 %layer.1 = (bf16[256,512]{1,0:T(8,128)(2,1)}, bf16[768,512]{1,0:T(8,128)(2,1)S(1)}, f32[256,512]{1,0:T(8,128)S(1)}, bf16[16,112,512]{2,1,0:T(8,128)(2,1)S(1)}, f32[16,112,512]{2,1,0:T(8,128)S(1)}) custom-call(bf16[2,128,512]{2,1,0:T(8,128)(2,1)S(1)} %collective-permute-done.refs_0_, bf16[2,128,512]{2,1,0:T(8,128)(2,1)S(1)} %collective-permute-done.1.refs_1_, ...), custom_call_target="tpu_custom_call" | custom-call | flops 4831838208 | bytes 12582912 | tf_op jit(solution)/shard_map/layer/pallas_call | solution.py:306
  31.9 0.0 collective-permute-start.6
  31.9 3.8 %collective-permute-done.6 = bf16[16,112,512]{2,1,0:T(8,128)(2,1)S(1)} collective-permute-done((bf16[16,112,512]{2,1,0:T(8,128)(2,1)S(1)}, bf16[16,112,512]{2,1,0:T(8,128)(2,1)S(1)}, u32[]{:S(2)}, u32[]{:S(2)}) %collective-permute-start.6) | collective-permute-done | bytes 1835040 | tf_op jit(solution)/shard_map/ppermute | solution.py:18
  35.7 0.7 convert_add_fusion
  36.4 0.1 slice.57
  36.6 1.9 %collective-permute-start.7 = (bf16[8,112,512]{2,1,0:T(8,128)(2,1)S(1)}, bf16[8,112,512]{2,1,0:T(8,128)(2,1)S(1)}, u32[]{:S(2)}, u32[]{:S(2)}) collective-permute-start(bf16[8,112,512]{2,1,0:T(8,128)(2,1)S(1)} %slice.57), channel_id=1, source_target_pairs={{0,2},{1,5},{2,0},{3,7},{4,6},{5,1},{6,4},{7,3},{8,10},{9,13},{10,... | collective-permute-start | bytes 2752520 | tf_op jit(solution)/shard_map/ppermute | solution.py:18
  38.5 11.6 %collective-permute-done.7 = bf16[8,112,512]{2,1,0:T(8,128)(2,1)S(1)} collective-permute-done((bf16[8,112,512]{2,1,0:T(8,128)(2,1)S(1)}, bf16[8,112,512]{2,1,0:T(8,128)(2,1)S(1)}, u32[]{:S(2)}, u32[]{:S(2)}) %collective-permute-start.7) | collective-permute-done | bytes 917536 | tf_op jit(solution)/shard_map/ppermute | solution.py:18
  50.0 0.3 slice_add_fusion
  50.3 0.1 slice.58
  50.4 0.1 collective-permute-start.8
  50.5 8.5 %collective-permute-done.8 = bf16[4,112,512]{2,1,0:T(8,128)(2,1)S(1)} collective-permute-done((bf16[4,112,512]{2,1,0:T(8,128)(2,1)S(1)}, bf16[4,112,512]{2,1,0:T(8,128)(2,1)S(1)}, u32[]{:S(2)}, u32[]{:S(2)}) %collective-permute-start.8) | collective-permute-done | bytes 458784 | tf_op jit(solution)/shard_map/ppermute | solution.py:18
  58.9 0.2 fusion
  59.2 3.7 %collective-permute-start.11 = (bf16[112,512]{1,0:T(8,128)(2,1)S(1)}, bf16[112,512]{1,0:T(8,128)(2,1)S(1)}, u32[]{:S(2)}, u32[]{:S(2)}) collective-permute-start(bf16[112,512]{1,0:T(8,128)(2,1)S(1)} %get-tuple-element.60), channel_id=1, source_target_pairs={{0,24},{1,25},{2,26},{3,27},{4,28},{5,29},{6,30},{7,31},{8,16},{9,... | collective-permute-start | bytes 344072 | tf_op jit(solution)/shard_map/ppermute | solution.py:18
  62.9 6.2 %input_grads.1 = (bf16[768,512]{1,0:T(8,128)(2,1)}, f32[2,128,512]{2,1,0:T(8,128)S(1)}, bf16[2,128,512]{2,1,0:T(8,128)(2,1)S(1)}, bf16[2,128,512]{2,1,0:T(8,128)(2,1)S(1)}, bf16[2,128,512]{2,1,0:T(8,128)(2,1)S(1)}) custom-call(s32[1,1,6]{2,1,0:T(1,128)} %recv_ref.3, s32[1,1,6]{2,1,0:T(1,128)} %send_ref.1, s32[6,128]{1,0:T(8,128)S(1)} %get-tuple-element.34.refs_5_.perm_ref, ...), custom_call_target="tpu_custom_call" | custom-call | flops 1207959552 | bytes 6291456 | tf_op jit(solution)/shard_map/input_grads/pallas_call | solution.py:376
  69.0 0.7 collective-permute-start.3
  69.7 4.2 %collective-permute-start.4 = (bf16[2,128,512]{2,1,0:T(8,128)(2,1)S(1)}, bf16[2,128,512]{2,1,0:T(8,128)(2,1)S(1)}, u32[]{:S(2)}, u32[]{:S(2)}) collective-permute-start(bf16[2,128,512]{2,1,0:T(8,128)(2,1)S(1)} %get-tuple-element.51), channel_id=1, source_target_pairs={{0,2},{2,0},{4,6},{6,4},{8,10},{10,8},{12,14},{14,12},{16,18},{18,... | collective-permute-start | bytes 786440 | tf_op jit(solution)/shard_map/ppermute | solution.py:119
  73.9 0.0 collective-permute-start.5
  73.9 0.0 collective-permute-start.10
  73.9 0.0 collective-permute-done.11.refs_3_
  73.9 0.6 collective-permute-start.9
  74.5 8.0 %collective-permute-done.10.refs_2_ = bf16[112,512]{1,0:T(8,128)(2,1)S(1)} collective-permute-done((bf16[112,512]{1,0:T(8,128)(2,1)S(1)}, bf16[112,512]{1,0:T(8,128)(2,1)S(1)}, u32[]{:S(2)}, u32[]{:S(2)}) %collective-permute-start.10) | collective-permute-done | bytes 114720 | tf_op jit(solution)/shard_map/ppermute | solution.py:18
  82.4 0.7 collective-permute-done.9.refs_1_
  83.1 0.1 squares.1
  83.2 0.1 collective-permute-start.12
  83.3 1.1 %collective-permute-done.12 = f32[4,128]{1,0:T(4,128)S(1)} collective-permute-done((f32[4,128]{1,0:T(4,128)S(1)}, f32[4,128]{1,0:T(4,128)S(1)}, u32[]{:S(2)}, u32[]{:S(2)}) %collective-permute-start.12) | collective-permute-done | bytes 2080 | tf_op jit(solution)/shard_map/ppermute | solution.py:18
  84.5 0.0 collective-permute-start.13
  84.5 3.6 %collective-permute-done.13 = f32[4,128]{1,0:T(4,128)S(1)} collective-permute-done((f32[4,128]{1,0:T(4,128)S(1)}, f32[4,128]{1,0:T(4,128)S(1)}, u32[]{:S(2)}, u32[]{:S(2)}) %collective-permute-start.13) | collective-permute-done | bytes 2080 | tf_op jit(solution)/shard_map/ppermute | solution.py:18
  88.1 0.0 collective-permute-start.14
  88.1 3.6 %collective-permute-done.14 = f32[4,128]{1,0:T(4,128)S(1)} collective-permute-done((f32[4,128]{1,0:T(4,128)S(1)}, f32[4,128]{1,0:T(4,128)S(1)}, u32[]{:S(2)}, u32[]{:S(2)}) %collective-permute-start.14) | collective-permute-done | bytes 2080 | tf_op jit(solution)/shard_map/ppermute | solution.py:18
  91.7 0.0 collective-permute-start.15
  91.7 3.6 %collective-permute-done.15 = f32[4,128]{1,0:T(4,128)S(1)} collective-permute-done((f32[4,128]{1,0:T(4,128)S(1)}, f32[4,128]{1,0:T(4,128)S(1)}, u32[]{:S(2)}, u32[]{:S(2)}) %collective-permute-start.15) | collective-permute-done | bytes 2080 | tf_op jit(solution)/shard_map/ppermute | solution.py:18
  95.2 0.0 collective-permute-start.16
  95.2 0.0 collective-permute-done.3.refs_0_
  95.3 0.0 collective-permute-done.5.refs_2_
  95.3 1.7 %node_grad.1 = bf16[2,128,512]{2,1,0:T(8,128)(2,1)} custom-call(s32[1,1,4]{2,1,0:T(1,128)} %count_ref.3, s32[1,1,4,2]{3,2,1,0:T(4,128)} %copy.19.list_ref, f32[2,128,512]{2,1,0:T(8,128)S(1)} %get-tuple-element.49.part_ref, bf16[2,128,512]{2,1,0:T(8,128)(2,1)S(1)} %collective-permute-done.3.refs_0_, bf16[2,128,512]{2,1,0:T(8,128)(2,1)S(1)} %collective-permute-done.4.refs_1_, ...), custom_call_target="tpu_custom_call" | custom-call | bytes 2097152 | tf_op jit(solution)/shard_map/node_grad/pallas_call | solution.py:406
  97.0 2.7 %collective-permute-done.16 = f32[4,128]{1,0:T(4,128)S(1)} collective-permute-done((f32[4,128]{1,0:T(4,128)S(1)}, f32[4,128]{1,0:T(4,128)S(1)}, u32[]{:S(2)}, u32[]{:S(2)}) %collective-permute-start.16) | collective-permute-done | bytes 2080 | tf_op jit(solution)/shard_map/ppermute | solution.py:18
  99.7 0.1 scale.1
  99.9 0.7 copy.22
  (8 shorter events, 0.1 us)
Async XLA Ops:
  3.7 12.2 %collective-permute-start = (bf16[2,128,512]{2,1,0:T(8,128)(2,1)S(1)}, bf16[2,128,512]{2,1,0:T(8,128)(2,1)S(1)}, u32[]{:S(2)}, u32[]{:S(2)}) collective-permute-start(bf16[2,128,512]{2,1,0:T(8,128)(2,1)S(1)} %get-tuple-element.31), channel_id=1, source_target_pairs={{2,4},{4,2},{6,8},{8,6},{10,12},{12,10},{14,16},{16,14},{18,20},{2... | collective-permute-start | bytes 786440 | tf_op jit(solution)/shard_map/ppermute | solution.py:119
  4.4 17.3 %collective-permute-start.1 = (bf16[2,128,512]{2,1,0:T(8,128)(2,1)S(1)}, bf16[2,128,512]{2,1,0:T(8,128)(2,1)S(1)}, u32[]{:S(2)}, u32[]{:S(2)}) collective-permute-start(bf16[2,128,512]{2,1,0:T(8,128)(2,1)S(1)} %get-tuple-element.32), channel_id=1, source_target_pairs={{0,2},{2,0},{4,6},{6,4},{8,10},{10,8},{12,14},{14,12},{16,18},{18,... | collective-permute-start | bytes 786440 | tf_op jit(solution)/shard_map/ppermute | solution.py:119
  10.2 11.6 %collective-permute-start.2 = (bf16[2,128,512]{2,1,0:T(8,128)(2,1)S(1)}, bf16[2,128,512]{2,1,0:T(8,128)(2,1)S(1)}, u32[]{:S(2)}, u32[]{:S(2)}) collective-permute-start(bf16[2,128,512]{2,1,0:T(8,128)(2,1)S(1)} %get-tuple-element.33), channel_id=1, source_target_pairs={{0,1},{1,0},{2,3},{3,2},{4,5},{5,4},{6,7},{7,6},{8,9},{9,8},{10,11... | collective-permute-start | bytes 786440 | tf_op jit(solution)/shard_map/ppermute | solution.py:119
  31.9 3.8 %collective-permute-start.6 = (bf16[16,112,512]{2,1,0:T(8,128)(2,1)S(1)}, bf16[16,112,512]{2,1,0:T(8,128)(2,1)S(1)}, u32[]{:S(2)}, u32[]{:S(2)}) collective-permute-start(bf16[16,112,512]{2,1,0:T(8,128)(2,1)S(1)} %get-tuple-element.55), channel_id=1, source_target_pairs={{0,1},{1,0},{2,3},{3,2},{4,5},{5,4},{6,7},{7,6},{8,9},{9,8},{10,11... | collective-permute-start | bytes 5505032 | tf_op jit(solution)/shard_map/ppermute | solution.py:18
  36.6 13.5 %collective-permute-start.7 = (bf16[8,112,512]{2,1,0:T(8,128)(2,1)S(1)}, bf16[8,112,512]{2,1,0:T(8,128)(2,1)S(1)}, u32[]{:S(2)}, u32[]{:S(2)}) collective-permute-start(bf16[8,112,512]{2,1,0:T(8,128)(2,1)S(1)} %slice.57), channel_id=1, source_target_pairs={{0,2},{1,5},{2,0},{3,7},{4,6},{5,1},{6,4},{7,3},{8,10},{9,13},{10,... | collective-permute-start | bytes 2752520 | tf_op jit(solution)/shard_map/ppermute | solution.py:18
  50.4 8.5 %collective-permute-start.8 = (bf16[4,112,512]{2,1,0:T(8,128)(2,1)S(1)}, bf16[4,112,512]{2,1,0:T(8,128)(2,1)S(1)}, u32[]{:S(2)}, u32[]{:S(2)}) collective-permute-start(bf16[4,112,512]{2,1,0:T(8,128)(2,1)S(1)} %slice.58), channel_id=1, source_target_pairs={{0,4},{1,3},{2,6},{3,1},{4,0},{5,7},{6,2},{7,5},{8,12},{9,11},{10,... | collective-permute-start | bytes 1376264 | tf_op jit(solution)/shard_map/ppermute | solution.py:18
  59.2 14.7 %collective-permute-start.11 = (bf16[112,512]{1,0:T(8,128)(2,1)S(1)}, bf16[112,512]{1,0:T(8,128)(2,1)S(1)}, u32[]{:S(2)}, u32[]{:S(2)}) collective-permute-start(bf16[112,512]{1,0:T(8,128)(2,1)S(1)} %get-tuple-element.60), channel_id=1, source_target_pairs={{0,24},{1,25},{2,26},{3,27},{4,28},{5,29},{6,30},{7,31},{8,16},{9,... | collective-permute-start | bytes 344072 | tf_op jit(solution)/shard_map/ppermute | solution.py:18
  69.0 26.2 %collective-permute-start.3 = (bf16[2,128,512]{2,1,0:T(8,128)(2,1)S(1)}, bf16[2,128,512]{2,1,0:T(8,128)(2,1)S(1)}, u32[]{:S(2)}, u32[]{:S(2)}) collective-permute-start(bf16[2,128,512]{2,1,0:T(8,128)(2,1)S(1)} %get-tuple-element.50), channel_id=1, source_target_pairs={{2,4},{4,2},{6,8},{8,6},{10,12},{12,10},{14,16},{16,14},{18,20},{2... | collective-permute-start | bytes 786440 | tf_op jit(solution)/shard_map/ppermute | solution.py:119
  69.7 25.6 %collective-permute-start.4 = (bf16[2,128,512]{2,1,0:T(8,128)(2,1)S(1)}, bf16[2,128,512]{2,1,0:T(8,128)(2,1)S(1)}, u32[]{:S(2)}, u32[]{:S(2)}) collective-permute-start(bf16[2,128,512]{2,1,0:T(8,128)(2,1)S(1)} %get-tuple-element.51), channel_id=1, source_target_pairs={{0,2},{2,0},{4,6},{6,4},{8,10},{10,8},{12,14},{14,12},{16,18},{18,... | collective-permute-start | bytes 786440 | tf_op jit(solution)/shard_map/ppermute | solution.py:119
  73.9 21.4 %collective-permute-start.5 = (bf16[2,128,512]{2,1,0:T(8,128)(2,1)S(1)}, bf16[2,128,512]{2,1,0:T(8,128)(2,1)S(1)}, u32[]{:S(2)}, u32[]{:S(2)}) collective-permute-start(bf16[2,128,512]{2,1,0:T(8,128)(2,1)S(1)} %get-tuple-element.52), channel_id=1, source_target_pairs={{0,1},{1,0},{2,3},{3,2},{4,5},{5,4},{6,7},{7,6},{8,9},{9,8},{10,11... | collective-permute-start | bytes 786440 | tf_op jit(solution)/shard_map/ppermute | solution.py:119
  73.9 8.6 %collective-permute-start.10 = (bf16[112,512]{1,0:T(8,128)(2,1)S(1)}, bf16[112,512]{1,0:T(8,128)(2,1)S(1)}, u32[]{:S(2)}, u32[]{:S(2)}) collective-permute-start(bf16[112,512]{1,0:T(8,128)(2,1)S(1)} %get-tuple-element.61), channel_id=1, source_target_pairs={{0,16},{1,17},{2,18},{3,19},{4,20},{5,21},{6,22},{7,23},{8,24},{9,... | collective-permute-start | bytes 344072 | tf_op jit(solution)/shard_map/ppermute | solution.py:18
  73.9 9.2 %collective-permute-start.9 = (bf16[112,512]{1,0:T(8,128)(2,1)S(1)}, bf16[112,512]{1,0:T(8,128)(2,1)S(1)}, u32[]{:S(2)}, u32[]{:S(2)}) collective-permute-start(bf16[112,512]{1,0:T(8,128)(2,1)S(1)} %get-tuple-element.62), channel_id=1, source_target_pairs={{0,8},{1,9},{2,10},{3,11},{4,12},{5,13},{6,14},{7,15},{8,0},{9,1},... | collective-permute-start | bytes 344072 | tf_op jit(solution)/shard_map/ppermute | solution.py:18
  83.2 1.2 %collective-permute-start.12 = (f32[4,128]{1,0:T(4,128)S(1)}, f32[4,128]{1,0:T(4,128)S(1)}, u32[]{:S(2)}, u32[]{:S(2)}) collective-permute-start(f32[4,128]{1,0:T(4,128)S(1)} %get-tuple-element.57), channel_id=1, source_target_pairs={{0,1},{1,0},{2,3},{3,2},{4,5},{5,4},{6,7},{7,6},{8,9},{9,8},{10,11... | collective-permute-start | bytes 6152 | tf_op jit(solution)/shard_map/ppermute | solution.py:18
  84.5 3.6 %collective-permute-start.13 = (f32[4,128]{1,0:T(4,128)S(1)}, f32[4,128]{1,0:T(4,128)S(1)}, u32[]{:S(2)}, u32[]{:S(2)}) collective-permute-start(f32[4,128]{1,0:T(4,128)S(1)} %add.27), channel_id=1, source_target_pairs={{0,2},{1,3},{2,0},{3,1},{4,6},{5,7},{6,4},{7,5},{8,10},{9,11},{10,... | collective-permute-start | bytes 6152 | tf_op jit(solution)/shard_map/ppermute | solution.py:18
  88.1 3.6 %collective-permute-start.14 = (f32[4,128]{1,0:T(4,128)S(1)}, f32[4,128]{1,0:T(4,128)S(1)}, u32[]{:S(2)}, u32[]{:S(2)}) collective-permute-start(f32[4,128]{1,0:T(4,128)S(1)} %add.28), channel_id=1, source_target_pairs={{0,4},{1,5},{2,6},{3,7},{4,0},{5,1},{6,2},{7,3},{8,12},{9,13},{10,... | collective-permute-start | bytes 6152 | tf_op jit(solution)/shard_map/ppermute | solution.py:18
  91.7 3.6 %collective-permute-start.15 = (f32[4,128]{1,0:T(4,128)S(1)}, f32[4,128]{1,0:T(4,128)S(1)}, u32[]{:S(2)}, u32[]{:S(2)}) collective-permute-start(f32[4,128]{1,0:T(4,128)S(1)} %add.29), channel_id=1, source_target_pairs={{0,8},{1,9},{2,10},{3,11},{4,12},{5,13},{6,14},{7,15},{8,0},{9,1},... | collective-permute-start | bytes 6152 | tf_op jit(solution)/shard_map/ppermute | solution.py:18
  95.2 4.5 %collective-permute-start.16 = (f32[4,128]{1,0:T(4,128)S(1)}, f32[4,128]{1,0:T(4,128)S(1)}, u32[]{:S(2)}, u32[]{:S(2)}) collective-permute-start(f32[4,128]{1,0:T(4,128)S(1)} %add.30), channel_id=1, source_target_pairs={{0,16},{1,17},{2,18},{3,19},{4,20},{5,21},{6,22},{7,23},{8,24},{9,... | collective-permute-start | bytes 6152 | tf_op jit(solution)/shard_map/ppermute | solution.py:18

commit v5 on v4

--- a/solution.py
+++ b/solution.py
@@ -90,13 +90,12 @@
 
 
 def sender_hot(perm_ref, tile, block):
-    row = perm_ref[pl.ds(tile, 1), :]
-    return (lax.broadcasted_iota(jnp.int32, (block, block), 0) == row).astype(jnp.bfloat16)
+    return (lax.broadcasted_iota(jnp.int32, (block, block), 0) == perm_ref[tile]).astype(jnp.bfloat16)
 
 
 def routes():
-    kinds = [("gx", "odd"), ("gx", "even")]
-    return kinds + [("gy", kind) for kind in ("odd", "even")[lax.axis_size("gy") == 2 :]]
+    kinds = [("gx", "even"), ("gx", "odd"), ("gy", "even"), ("gy", "odd")]
+    return kinds[:3] if lax.axis_size("gy") == 2 else kinds
 
 
 def upward(axis, kind):
@@ -119,30 +118,33 @@
     return lax.ppermute(values, axis, pairs)
 
 
-def pack_kernel(chosen, nodes_hbm, count_ref, list_ref, *refs):
-    packet_refs, (nodes_ref, semaphores) = refs[:-2], refs[-2:]
-    (copy,) = fetch([nodes_hbm], [nodes_ref], semaphores)
-    copy.wait()
+def pack_kernel(chosen, *refs):
+    packet_refs, refs = refs[3:-4], refs[:3] + refs[-4:]
+    nodes_ref, count_ref, list_ref, semaphores = refs[3:]
+    for copy in fetch(refs[:3], refs[3:6], semaphores):
+        copy.wait()
     for packet_ref, route in zip(packet_refs, chosen):
         direction = sent_to(*route)
         for slot in range(packet_ref.shape[0]):
-            block = nodes_ref[list_ref[0, 0, direction, slot]]
+            block = nodes_ref[list_ref[0, 0, slot, direction]]
             live = slot < count_ref[0, 0, direction]
             packet_ref[slot] = jnp.where(live, block, jnp.zeros_like(block))
 
 
 def pack(node_blocks, send_count, send_list):
-    slots = send_list.shape[3]
     chosen = routes()
-    packet = jax.ShapeDtypeStruct((slots,) + node_blocks.shape[1:], node_blocks.dtype)
+    shape = (send_list.shape[2],) + node_blocks.shape[1:]
+    packet = jax.ShapeDtypeStruct(shape, node_blocks.dtype)
     return pl.pallas_call(
         functools.partial(pack_kernel, chosen),
         out_shape=[packet] * len(chosen),
-        in_specs=[HBM, SMEM, SMEM],
+        in_specs=[HBM] * 3,
         out_specs=[VMEM] * len(chosen),
         scratch_shapes=[
             pltpu.VMEM(node_blocks.shape, node_blocks.dtype),
-            pltpu.SemaphoreType.DMA((1,)),
+            pltpu.SMEM(send_count.shape, send_count.dtype),
+            pltpu.SMEM(send_list.shape, send_list.dtype),
+            pltpu.SemaphoreType.DMA((3,)),
         ],
         compiler_params=pltpu.CompilerParams(vmem_limit_bytes=4 << 20),
         name="pack",
@@ -198,7 +200,7 @@
     (
         recv_ref, send_ref, perm_ref, nodes_ref, edges_ref, part_ref, h_recv, ew1_ref, ew2_ref,
         nw1_ref, nb1_ref, nw2_ref, ncot_ref, ecot_ref,
-        out_ref, gea_ref, base_ref, away_ref, keep_ref,
+        out_ref, gea_ref, base_ref, near_ref, far_ref, keep_ref,
         ext, h_send, affine, hidden, message, inverse, total, gel, stacked,
     ) = refs
     blocks, block, feature = nodes_ref.shape
@@ -274,12 +276,14 @@
     core = lax.rem(gy_index, 2)
     own = piece_order(core, gx_index, gy_index)
     other = piece_order(1 - core, gx_index, gy_index ^ 1)
+    half = len(own) // 2
     if rows % 16 == 0:
         for place in range(len(own)):
             start = pl.multiple_of(own[place] * rows, 8)
             keep_ref[place] = stacked[pl.ds(start, rows), :]
             start = pl.multiple_of(other[place] * rows, 8)
-            away_ref[place] = stacked[pl.ds(start, rows), :].astype(jnp.bfloat16)
+            away = stacked[pl.ds(start, rows), :].astype(jnp.bfloat16)
+            (far_ref if place >= half else near_ref)[place % half] = away
     else:
         keep_ref[...] = stacked[...]
 
@@ -298,12 +302,13 @@
         ((nodes, feature), bf16),
         ((edge_count, feature), bf16),
         ((nodes, feature), f32),
-        ((count, rows, feature), bf16),
+        ((count // 2, rows, feature), bf16),
+        ((count // 2, rows, feature), bf16),
         (keep, f32),
     ]
     flops = 6 * feature * feature * (3 * edge_count + 3 * nodes)
     chosen = routes()
-    out, gea, base, away, kept = pl.pallas_call(
+    out, gea, base, near, far, kept = pl.pallas_call(
         functools.partial(main_kernel, chosen, rows),
         out_shape=[jax.ShapeDtypeStruct(*result) for result in results],
         in_specs=[VMEM] * len(halos) + [SMEM] * 2 + [VMEM] * 12,
@@ -334,14 +339,15 @@
         pieces = kept.reshape(2 * count, rows, feature)
         other = piece_order(1 - core, gx_index, gy_index ^ 1)
         away = pieces[jnp.stack(other)].astype(bf16)
+        near, far = away[: count // 2], away[count // 2 :]
         kept = pieces[jnp.stack(piece_order(core, gx_index, gy_index))]
-    return out, gea, base, away, kept
+    return out, gea, base, near, far, kept
 
 
 def tail_kernel(chosen, recv_ref, send_ref, perm_ref, gea_ref, ew1_ref, ecot_ref, base_ref, *refs):
     grad_ref, part_ref = refs[:2]
     packet_refs, (ext,) = refs[2:-1], refs[-1:]
-    tiles, block = perm_ref.shape
+    tiles, _, block = perm_ref.shape
     feature = gea_ref.shape[1]
     blocks = part_ref.shape[0]
     slots = packet_refs[0].shape[0]
@@ -367,7 +373,7 @@
 
 def tail(recv, send, perm, gea, edge_w1, edge_cot, base, blocks, slots):
     edge_count, feature = gea.shape
-    block = perm.shape[1]
+    block = perm.shape[2]
     chosen = routes()
     results = [
         ((edge_count, feature), jnp.bfloat16),
@@ -394,7 +400,7 @@
         for packet_ref, route in zip(packet_refs, chosen):
             direction = sent_to(*route)
             for slot in range(packet_ref.shape[0]):
-                here = list_ref[0, 0, direction, slot] == block
+                here = list_ref[0, 0, slot, direction] == block
                 live = here & (slot < count_ref[0, 0, direction])
                 given = packet_ref[slot].astype(jnp.float32)
                 value += jnp.where(live, given, jnp.zeros_like(given))
@@ -439,7 +445,8 @@
     edge_rows = edge_latents.reshape(tile_count * block_size, feature)
     cot_node = node_cot.reshape(node_count, feature)
     cot_edge = edge_cot.reshape(tile_count * block_size, feature)
-    perm = tile_perm.reshape(tile_count, block_size)
+    perm = tile_perm.reshape(tile_count, 1, block_size)
+    send_list = send_list.transpose(0, 1, 3, 2)
     packets = pack(node_blocks, send_count, send_list)
     halos = [move(packet, *route) for packet, route in zip(packets, routes())]
     biases = edge_b1.reshape(1, feature), node_b1.reshape(1, feature)
@@ -449,14 +456,14 @@
     )
     node_blocks, edge_rows, _, edge_w1, perm, *weights, cot_node, cot_edge = held
     weights = [edge_w1] + weights
-    node_out, gea, base, away, keep = main(
+    node_out, gea, base, near, far, keep = main(
         halos, tile_recv, tile_send, perm, node_blocks, edge_rows, partial, h_recv, weights,
         cot_node, cot_edge,
     )
     edge_grad, part, *packets = tail(
         tile_recv, tile_send, perm, gea, edge_w1, cot_edge, base, block_count, slot_count
     )
-    terms = scatter_sum(away, keep)
+    terms = scatter_sum(near, far, keep)
     halos = [move(packet, *route) for packet, route in zip(packets, routes())]
     node_grad = finish(send_count, send_list, part, halos)
     row_counts = (3 * feature, feature, 2 * feature, feature)
@@ -469,12 +476,17 @@
     )
 
 
-def scatter_sum(send, keep):
-    total = keep + swap(send, (0, 0), 1).astype(jnp.float32)
-    for masks in ((1, 2), (2, 1)):
-        total = total.reshape((2, total.shape[0] // 2) + total.shape[1:])
-        heard = swap(total[1].astype(jnp.bfloat16), masks, 0)
-        total = total[0] + heard.astype(jnp.float32)
+def hop(values, *masks):
+    return swap(values.astype(jnp.bfloat16), *masks).astype(jnp.float32)
+
+
+def scatter_sum(near, far, keep):
+    half, part = keep.shape[0] // 2, keep.shape[0] // 4
+    far = keep[half:] + hop(far, (0, 0), 1)
+    near = keep[:half] + hop(near, (0, 0), 1)
+    near_far = near[part:] + hop(far[part:], (1, 2), 0)
+    near_near = near[:part] + hop(far[:part], (1, 2), 0)
+    total = near_near + hop(near_far, (2, 1), 0)
     terms = [total[0]]
     for place, (mask_gx, mask_gy) in enumerate(group_masks()):
         if place:
@@ -483,14 +495,12 @@
 
 
 def sum_everywhere(values):
-    bit = 1
-    while bit < lax.axis_size("gy"):
-        values = values + swap(values, (0, 0), bit)
-        bit *= 2
-    bit = 1
-    while bit < lax.axis_size("gx"):
-        values = values + swap(values, (bit, bit), 0)
-        bit *= 2
+    for axis in ("gx", "gy"):
+        bit = lax.axis_size(axis) // 2
+        while bit:
+            mask = ((bit, bit), 0) if axis == "gx" else ((0, 0), bit)
+            values = values + swap(values, *mask)
+            bit //= 2
     return values
 
 

time: 101 us -> 95.2 us (0.943)
  waiting for transfers between devices: 52.8 us -> 49.5 us
  local copies, waits for them, and re-layouts: 3.54 us -> 0.79 us
  starting transfers between devices: 17.6 us -> 18.9 us
    ppermute x11 -> x13, starting transfers between devices: 6.31 us -> 12 us  [swap(): return lax.ppermute(values, ('gx', 'gy'), pairs)]
    ppermute x6, starting transfers between devices: 11.3 us -> 6.89 us  [move(): return lax.ppermute(values, axis, pairs)]
    ppermute x11 -> x13, waiting for transfers between devices: 47 us -> 43.5 us  [swap(): return lax.ppermute(values, ('gx', 'gy'), pairs)]
    unnamed x3 -> x1, local copies, waits for them, and re-layouts: 3.3 us -> 0.69 us
  transfers between devices with their start and end apart: 17 -> 19, of which waited for: 11 -> 12; matrix products, arithmetic and copies ran while one was open for 1% -> 0% of each run, Pallas kernels for 12% -> 13%
where the time goes in v5:
time: 95.2 us; the launch traced here: 95 us
  waiting for transfers between devices  49.5 us (52%)
  Pallas kernels  24 us (25%)
  starting transfers between devices  18.9 us (20%)
  other arithmetic  1.1 us (1%)
    ppermute x13, waiting for transfers between devices, swap(): return lax.ppermute(values, ('gx', 'gy'), pairs)  43.5 us
    ppermute x13, starting transfers between devices, swap(): return lax.ppermute(values, ('gx', 'gy'), pairs)  12 us
    pallas_call x1, Pallas kernels, main(): pl.pallas_call(functools.partial(main_kernel, chosen, rows), out_shape=[j...  10.2 us
    ppermute x6, starting transfers between devices, move(): return lax.ppermute(values, axis, pairs)  6.89 us
    pallas_call x1, Pallas kernels, tail(): pl.pallas_call(functools.partial(tail_kernel, chosen), out_shape=[jax.Sha...  6.17 us
    ppermute x6, waiting for transfers between devices, move(): return lax.ppermute(values, axis, pairs)  5.95 us
    pallas_call x1, Pallas kernels, local(): pl.pallas_call(functools.partial(local_kernel, len(operands)), out_shape=...  4.49 us
  transfers between devices with their start and end apart: 19, of which 12 were waited for; matrix products, arithmetic and copies ran while one was open for 0% of the time, Pallas kernels for 13%

profile of v5, /device:TPU:0, one launch (start us, length us, event | category | flops | bytes accessed | tf_op | source)
XLA Modules:
  0.0 95.0 jit_solution(14563188540585451552)
XLA Ops:
  0.6 1.1 %pack.1 = (bf16[2,128,512]{2,1,0:T(8,128)(2,1)S(1)}, bf16[2,128,512]{2,1,0:T(8,128)(2,1)S(1)}, bf16[2,128,512]{2,1,0:T(8,128)(2,1)S(1)}) custom-call(bf16[2,128,512]{2,1,0:T(8,128)(2,1)} %bitcast.22, s32[1,1,4]{2,1,0:T(1,128)} %count_ref.1, s32[1,1,2,4]{3,2,1,0:T(2,128)} %bitcast.29), custom_call_target="tpu_custom_call" | custom-call | tf_op jit(solution)/shard_map/pack/pallas_call | solution.py:138
  1.8 3.0 %collective-permute-start = (bf16[2,128,512]{2,1,0:T(8,128)(2,1)S(1)}, bf16[2,128,512]{2,1,0:T(8,128)(2,1)S(1)}, u32[]{:S(2)}, u32[]{:S(2)}) collective-permute-start(bf16[2,128,512]{2,1,0:T(8,128)(2,1)S(1)} %get-tuple-element.32), channel_id=1, source_target_pairs={{0,2},{2,0},{4,6},{6,4},{8,10},{10,8},{12,14},{14,12},{16,18},{18,... | collective-permute-start | bytes 786440 | tf_op jit(solution)/shard_map/ppermute | solution.py:118
  4.8 0.7 collective-permute-start.1
  5.5 0.1 collective-permute-start.2
  5.5 4.5 %local_part.1 = (bf16[2,128,512]{2,1,0:T(8,128)(2,1)S(1)}, bf16[768,512]{1,0:T(8,128)(2,1)S(1)}, f32[1,512]{1,0:T(1,128)}, bf16[1536,512]{1,0:T(8,128)(2,1)S(1)}...) custom-call(s32[1,1,6]{2,1,0:T(1,128)} %recv_ref.3, ...), custom_call_target="tpu_custom_call" | custom-call | flops 805306368 | bytes 8388608 | tf_op jit(solution)/shard_map/local_part/pallas_call | solution.py:184
  10.0 5.9 %collective-permute-done.refs_0_ = bf16[2,128,512]{2,1,0:T(8,128)(2,1)S(1)} collective-permute-done((bf16[2,128,512]{2,1,0:T(8,128)(2,1)S(1)}, bf16[2,128,512]{2,1,0:T(8,128)(2,1)S(1)}, u32[]{:S(2)}, u32[]{:S(2)}) %collective-permute-start) | collective-permute-done | bytes 262176 | tf_op jit(solution)/shard_map/ppermute | solution.py:118
  16.0 0.0 collective-permute-done.1.refs_1_
  16.0 0.0 collective-permute-done.2.refs_2_
  16.0 10.2 %layer.1 = (bf16[256,512]{1,0:T(8,128)(2,1)}, bf16[768,512]{1,0:T(8,128)(2,1)S(1)}, f32[256,512]{1,0:T(8,128)S(1)}, bf16[8,112,512]{2,1,0:T(8,128)(2,1)S(1)}, bf...) custom-call(bf16[2,128,512]{2,1,0:T(8,128)(2,1)S(1)} %collective-permute-done.refs_0_, ...), custom_call_target="tpu_custom_call" | custom-call | flops 4831838208 | bytes 12582912 | tf_op jit(solution)/shard_map/layer/pallas_call | solution.py:311
  26.2 0.0 collective-permute-start.6
  26.2 0.5 collective-permute-start.7
  26.7 2.0 %collective-permute-done.6 = bf16[8,112,512]{2,1,0:T(8,128)(2,1)S(1)} collective-permute-done((bf16[8,112,512]{2,1,0:T(8,128)(2,1)S(1)}, bf16[8,112,512]{2,1,0:T(8,128)(2,1)S(1)}, u32[]{:S(2)}, u32[]{:S(2)}) %collective-permute-start.6) | collective-permute-done | bytes 917536 | tf_op jit(solution)/shard_map/ppermute | solution.py:18
  28.7 1.3 %collective-permute-done.7 = bf16[8,112,512]{2,1,0:T(8,128)(2,1)S(1)} collective-permute-done((bf16[8,112,512]{2,1,0:T(8,128)(2,1)S(1)}, bf16[8,112,512]{2,1,0:T(8,128)(2,1)S(1)}, u32[]{:S(2)}, u32[]{:S(2)}) %collective-permute-start.7) | collective-permute-done | bytes 917536 | tf_op jit(solution)/shard_map/ppermute | solution.py:18
  30.0 0.7 add_convert_fusion
  30.7 0.1 fusion.4
  30.7 3.5 %collective-permute-start.9 = (bf16[4,112,512]{2,1,0:T(8,128)(2,1)S(1)}, bf16[4,112,512]{2,1,0:T(8,128)(2,1)S(1)}, u32[]{:S(2)}, u32[]{:S(2)}) collective-permute-start(bf16[4,112,512]{2,1,0:T(8,128)(2,1)S(1)} %get-tuple-element.65), channel_id=1, source_target_pairs={{0,2},{1,5},{2,0},{3,7},{4,6},{5,1},{6,4},{7,3},{8,10},{9,13},{10,... | collective-permute-start | bytes 1376264 | tf_op jit(solution)/shard_map/ppermute | solution.py:18
  34.2 0.1 collective-permute-start.8
  34.3 6.4 %collective-permute-done.9 = bf16[4,112,512]{2,1,0:T(8,128)(2,1)S(1)} collective-permute-done((bf16[4,112,512]{2,1,0:T(8,128)(2,1)S(1)}, bf16[4,112,512]{2,1,0:T(8,128)(2,1)S(1)}, u32[]{:S(2)}, u32[]{:S(2)}) %collective-permute-start.9) | collective-permute-done | bytes 458784 | tf_op jit(solution)/shard_map/ppermute | solution.py:18
  40.7 0.2 fusion
  40.9 0.9 collective-permute-start.10
  41.7 6.4 %collective-permute-done.8 = bf16[4,112,512]{2,1,0:T(8,128)(2,1)S(1)} collective-permute-done((bf16[4,112,512]{2,1,0:T(8,128)(2,1)S(1)}, bf16[4,112,512]{2,1,0:T(8,128)(2,1)S(1)}, u32[]{:S(2)}, u32[]{:S(2)}) %collective-permute-start.8) | collective-permute-done | bytes 458784 | tf_op jit(solution)/shard_map/ppermute | solution.py:18
  48.1 1.3 %collective-permute-done.10 = bf16[4,112,512]{2,1,0:T(8,128)(2,1)S(1)} collective-permute-done((bf16[4,112,512]{2,1,0:T(8,128)(2,1)S(1)}, bf16[4,112,512]{2,1,0:T(8,128)(2,1)S(1)}, u32[]{:S(2)}, u32[]{:S(2)}) %collective-permute-start.10) | collective-permute-done | bytes 458784 | tf_op jit(solution)/shard_map/ppermute | solution.py:18
  49.4 0.2 fusion.2
  49.7 3.7 %collective-permute-start.13 = (bf16[112,512]{1,0:T(8,128)(2,1)S(1)}, bf16[112,512]{1,0:T(8,128)(2,1)S(1)}, u32[]{:S(2)}, u32[]{:S(2)}) collective-permute-start(bf16[112,512]{1,0:T(8,128)(2,1)S(1)} %get-tuple-element.66), channel_id=1, source_target_pairs={{0,24},{1,25},{2,26},{3,27},{4,28},{5,29},{6,30},{7,31},{8,16},{9,... | collective-permute-start | bytes 344072 | tf_op jit(solution)/shard_map/ppermute | solution.py:18
  53.4 6.2 %input_grads.1 = (bf16[768,512]{1,0:T(8,128)(2,1)}, f32[2,128,512]{2,1,0:T(8,128)S(1)}, bf16[2,128,512]{2,1,0:T(8,128)(2,1)S(1)}, bf16[2,128,512]{2,1,0:T(8,128)(2,1)S(1)}, bf16[2,128,512]{2,1,0:T(8,128)(2,1)S(1)}) custom-call(s32[1,1,6]{2,1,0:T(1,128)} %recv_ref.3, s32[1,1,6]{2,1,0:T(1,128)} %send_ref.1, ...), custom_call_target="tpu_custom_call" | custom-call | flops 1207959552 | bytes 6291456 | tf_op jit(solution)/shard_map/input_grads/pallas_call | solution.py:382
  59.5 2.3 %collective-permute-start.3 = (bf16[2,128,512]{2,1,0:T(8,128)(2,1)S(1)}, bf16[2,128,512]{2,1,0:T(8,128)(2,1)S(1)}, u32[]{:S(2)}, u32[]{:S(2)}) collective-permute-start(bf16[2,128,512]{2,1,0:T(8,128)(2,1)S(1)} %get-tuple-element.51), channel_id=1, source_target_pairs={{0,2},{2,0},{4,6},{6,4},{8,10},{10,8},{12,14},{14,12},{16,18},{18,... | collective-permute-start | bytes 786440 | tf_op jit(solution)/shard_map/ppermute | solution.py:118
  61.8 0.7 collective-permute-start.4
  62.5 0.2 collective-permute-start.5
  62.7 2.2 %collective-permute-start.12 = (bf16[112,512]{1,0:T(8,128)(2,1)S(1)}, bf16[112,512]{1,0:T(8,128)(2,1)S(1)}, u32[]{:S(2)}, u32[]{:S(2)}) collective-permute-start(bf16[112,512]{1,0:T(8,128)(2,1)S(1)} %get-tuple-element.67), channel_id=1, source_target_pairs={{0,16},{1,17},{2,18},{3,19},{4,20},{5,21},{6,22},{7,23},{8,24},{9,... | collective-permute-start | bytes 344072 | tf_op jit(solution)/shard_map/ppermute | solution.py:18
  64.9 0.0 collective-permute-done.13.refs_3_
  64.9 1.1 %collective-permute-start.11 = (bf16[112,512]{1,0:T(8,128)(2,1)S(1)}, bf16[112,512]{1,0:T(8,128)(2,1)S(1)}, u32[]{:S(2)}, u32[]{:S(2)}) collective-permute-start(bf16[112,512]{1,0:T(8,128)(2,1)S(1)} %get-tuple-element.68), channel_id=1, source_target_pairs={{0,8},{1,9},{2,10},{3,11},{4,12},{5,13},{6,14},{7,15},{8,0},{9,1},... | collective-permute-start | bytes 344072 | tf_op jit(solution)/shard_map/ppermute | solution.py:18
  66.0 10.1 %collective-permute-done.12.refs_2_ = bf16[112,512]{1,0:T(8,128)(2,1)S(1)} collective-permute-done((bf16[112,512]{1,0:T(8,128)(2,1)S(1)}, bf16[112,512]{1,0:T(8,128)(2,1)S(1)}, u32[]{:S(2)}, u32[]{:S(2)}) %collective-permute-start.12) | collective-permute-done | bytes 114720 | tf_op jit(solution)/shard_map/ppermute | solution.py:18
  76.0 0.9 collective-permute-done.11.refs_1_
  77.0 0.1 squares.1
  77.1 0.1 collective-permute-start.14
  77.2 4.5 %collective-permute-done.14 = f32[4,128]{1,0:T(4,128)S(1)} collective-permute-done((f32[4,128]{1,0:T(4,128)S(1)}, f32[4,128]{1,0:T(4,128)S(1)}, u32[]{:S(2)}, u32[]{:S(2)}) %collective-permute-start.14) | collective-permute-done | bytes 2080 | tf_op jit(solution)/shard_map/ppermute | solution.py:18
  81.7 0.0 collective-permute-start.15
  81.7 3.6 %collective-permute-done.15 = f32[4,128]{1,0:T(4,128)S(1)} collective-permute-done((f32[4,128]{1,0:T(4,128)S(1)}, f32[4,128]{1,0:T(4,128)S(1)}, u32[]{:S(2)}, u32[]{:S(2)}) %collective-permute-start.15) | collective-permute-done | bytes 2080 | tf_op jit(solution)/shard_map/ppermute | solution.py:18
  85.2 0.0 collective-permute-start.16
  85.3 3.6 %collective-permute-done.16 = f32[4,128]{1,0:T(4,128)S(1)} collective-permute-done((f32[4,128]{1,0:T(4,128)S(1)}, f32[4,128]{1,0:T(4,128)S(1)}, u32[]{:S(2)}, u32[]{:S(2)}) %collective-permute-start.16) | collective-permute-done | bytes 2080 | tf_op jit(solution)/shard_map/ppermute | solution.py:18
  88.8 3.6 %collective-permute-done.17 = f32[4,128]{1,0:T(4,128)S(1)} collective-permute-done((f32[4,128]{1,0:T(4,128)S(1)}, f32[4,128]{1,0:T(4,128)S(1)}, u32[]{:S(2)}, u32[]{:S(2)}) %collective-permute-start.17) | collective-permute-done | bytes 2080 | tf_op jit(solution)/shard_map/ppermute | solution.py:18
  92.4 0.0 collective-permute-done.3.refs_0_
  92.4 0.0 collective-permute-done.4.refs_1_
  92.4 0.0 collective-permute-done.5.refs_2_
  92.5 1.7 %node_grad.1 = bf16[2,128,512]{2,1,0:T(8,128)(2,1)} custom-call(s32[1,1,4]{2,1,0:T(1,128)} %count_ref.1, s32[1,1,2,4]{3,2,1,0:T(2,128)} %bitcast.30, f32[2,128,512]{2,1,0:T(8,128)S(1)} %get-tuple-element.50.part_ref, bf16[2,128,512]{2,1,0:T(8,128)(2,1)S(1)} %collective-permute-done.3.refs_0_, bf16[2,128,512]{2,1,0:T(8,128)(2,1)S(1)} %collective-permute-done.4.refs_1_, ...), custom_call_target="tpu_custom_call" | custom-call | bytes 2097152 | tf_op jit(solution)/shard_map/node_grad/pallas_call | solution.py:412
  94.2 0.0 collective-permute-done.18
  94.2 0.1 scale.1
  94.3 0.7 copy.19
  (9 shorter events, 0.1 us)
Async XLA Ops:
  1.8 14.2 %collective-permute-start = (bf16[2,128,512]{2,1,0:T(8,128)(2,1)S(1)}, bf16[2,128,512]{2,1,0:T(8,128)(2,1)S(1)}, u32[]{:S(2)}, u32[]{:S(2)}) collective-permute-start(bf16[2,128,512]{2,1,0:T(8,128)(2,1)S(1)} %get-tuple-element.32), channel_id=1, source_target_pairs={{0,2},{2,0},{4,6},{6,4},{8,10},{10,8},{12,14},{14,12},{16,18},{18,... | collective-permute-start | bytes 786440 | tf_op jit(solution)/shard_map/ppermute | solution.py:118
  4.8 11.2 %collective-permute-start.1 = (bf16[2,128,512]{2,1,0:T(8,128)(2,1)S(1)}, bf16[2,128,512]{2,1,0:T(8,128)(2,1)S(1)}, u32[]{:S(2)}, u32[]{:S(2)}) collective-permute-start(bf16[2,128,512]{2,1,0:T(8,128)(2,1)S(1)} %get-tuple-element.33), channel_id=1, source_target_pairs={{2,4},{4,2},{6,8},{8,6},{10,12},{12,10},{14,16},{16,14},{18,20},{2... | collective-permute-start | bytes 786440 | tf_op jit(solution)/shard_map/ppermute | solution.py:118
  5.5 10.5 %collective-permute-start.2 = (bf16[2,128,512]{2,1,0:T(8,128)(2,1)S(1)}, bf16[2,128,512]{2,1,0:T(8,128)(2,1)S(1)}, u32[]{:S(2)}, u32[]{:S(2)}) collective-permute-start(bf16[2,128,512]{2,1,0:T(8,128)(2,1)S(1)} %get-tuple-element.34), channel_id=1, source_target_pairs={{0,1},{1,0},{2,3},{3,2},{4,5},{5,4},{6,7},{7,6},{8,9},{9,8},{10,11... | collective-permute-start | bytes 786440 | tf_op jit(solution)/shard_map/ppermute | solution.py:118
  26.2 2.5 %collective-permute-start.6 = (bf16[8,112,512]{2,1,0:T(8,128)(2,1)S(1)}, bf16[8,112,512]{2,1,0:T(8,128)(2,1)S(1)}, u32[]{:S(2)}, u32[]{:S(2)}) collective-permute-start(bf16[8,112,512]{2,1,0:T(8,128)(2,1)S(1)} %get-tuple-element.56), channel_id=1, source_target_pairs={{0,1},{1,0},{2,3},{3,2},{4,5},{5,4},{6,7},{7,6},{8,9},{9,8},{10,11... | collective-permute-start | bytes 2752520 | tf_op jit(solution)/shard_map/ppermute | solution.py:18
  26.2 3.8 %collective-permute-start.7 = (bf16[8,112,512]{2,1,0:T(8,128)(2,1)S(1)}, bf16[8,112,512]{2,1,0:T(8,128)(2,1)S(1)}, u32[]{:S(2)}, u32[]{:S(2)}) collective-permute-start(bf16[8,112,512]{2,1,0:T(8,128)(2,1)S(1)} %get-tuple-element.57), channel_id=1, source_target_pairs={{0,1},{1,0},{2,3},{3,2},{4,5},{5,4},{6,7},{7,6},{8,9},{9,8},{10,11... | collective-permute-start | bytes 2752520 | tf_op jit(solution)/shard_map/ppermute | solution.py:18
  30.7 10.0 %collective-permute-start.9 = (bf16[4,112,512]{2,1,0:T(8,128)(2,1)S(1)}, bf16[4,112,512]{2,1,0:T(8,128)(2,1)S(1)}, u32[]{:S(2)}, u32[]{:S(2)}) collective-permute-start(bf16[4,112,512]{2,1,0:T(8,128)(2,1)S(1)} %get-tuple-element.65), channel_id=1, source_target_pairs={{0,2},{1,5},{2,0},{3,7},{4,6},{5,1},{6,4},{7,3},{8,10},{9,13},{10,... | collective-permute-start | bytes 1376264 | tf_op jit(solution)/shard_map/ppermute | solution.py:18
  34.2 13.9 %collective-permute-start.8 = (bf16[4,112,512]{2,1,0:T(8,128)(2,1)S(1)}, bf16[4,112,512]{2,1,0:T(8,128)(2,1)S(1)}, u32[]{:S(2)}, u32[]{:S(2)}) collective-permute-start(bf16[4,112,512]{2,1,0:T(8,128)(2,1)S(1)} %get-tuple-element.64), channel_id=1, source_target_pairs={{0,2},{1,5},{2,0},{3,7},{4,6},{5,1},{6,4},{7,3},{8,10},{9,13},{10,... | collective-permute-start | bytes 1376264 | tf_op jit(solution)/shard_map/ppermute | solution.py:18
  40.9 8.5 %collective-permute-start.10 = (bf16[4,112,512]{2,1,0:T(8,128)(2,1)S(1)}, bf16[4,112,512]{2,1,0:T(8,128)(2,1)S(1)}, u32[]{:S(2)}, u32[]{:S(2)}) collective-permute-start(bf16[4,112,512]{2,1,0:T(8,128)(2,1)S(1)} %fusion), channel_id=1, source_target_pairs={{0,4},{1,3},{2,6},{3,1},{4,0},{5,7},{6,2},{7,5},{8,12},{9,11},{10,... | collective-permute-start | bytes 1376264 | tf_op jit(solution)/shard_map/ppermute | solution.py:18
  49.7 15.2 %collective-permute-start.13 = (bf16[112,512]{1,0:T(8,128)(2,1)S(1)}, bf16[112,512]{1,0:T(8,128)(2,1)S(1)}, u32[]{:S(2)}, u32[]{:S(2)}) collective-permute-start(bf16[112,512]{1,0:T(8,128)(2,1)S(1)} %get-tuple-element.66), channel_id=1, source_target_pairs={{0,24},{1,25},{2,26},{3,27},{4,28},{5,29},{6,30},{7,31},{8,16},{9,... | collective-permute-start | bytes 344072 | tf_op jit(solution)/shard_map/ppermute | solution.py:18
  59.5 32.9 %collective-permute-start.3 = (bf16[2,128,512]{2,1,0:T(8,128)(2,1)S(1)}, bf16[2,128,512]{2,1,0:T(8,128)(2,1)S(1)}, u32[]{:S(2)}, u32[]{:S(2)}) collective-permute-start(bf16[2,128,512]{2,1,0:T(8,128)(2,1)S(1)} %get-tuple-element.51), channel_id=1, source_target_pairs={{0,2},{2,0},{4,6},{6,4},{8,10},{10,8},{12,14},{14,12},{16,18},{18,... | collective-permute-start | bytes 786440 | tf_op jit(solution)/shard_map/ppermute | solution.py:118
  61.8 30.6 %collective-permute-start.4 = (bf16[2,128,512]{2,1,0:T(8,128)(2,1)S(1)}, bf16[2,128,512]{2,1,0:T(8,128)(2,1)S(1)}, u32[]{:S(2)}, u32[]{:S(2)}) collective-permute-start(bf16[2,128,512]{2,1,0:T(8,128)(2,1)S(1)} %get-tuple-element.52), channel_id=1, source_target_pairs={{2,4},{4,2},{6,8},{8,6},{10,12},{12,10},{14,16},{16,14},{18,20},{2... | collective-permute-start | bytes 786440 | tf_op jit(solution)/shard_map/ppermute | solution.py:118
  62.5 29.9 %collective-permute-start.5 = (bf16[2,128,512]{2,1,0:T(8,128)(2,1)S(1)}, bf16[2,128,512]{2,1,0:T(8,128)(2,1)S(1)}, u32[]{:S(2)}, u32[]{:S(2)}) collective-permute-start(bf16[2,128,512]{2,1,0:T(8,128)(2,1)S(1)} %get-tuple-element.53), channel_id=1, source_target_pairs={{0,1},{1,0},{2,3},{3,2},{4,5},{5,4},{6,7},{7,6},{8,9},{9,8},{10,11... | collective-permute-start | bytes 786440 | tf_op jit(solution)/shard_map/ppermute | solution.py:118
  62.7 13.4 %collective-permute-start.12 = (bf16[112,512]{1,0:T(8,128)(2,1)S(1)}, bf16[112,512]{1,0:T(8,128)(2,1)S(1)}, u32[]{:S(2)}, u32[]{:S(2)}) collective-permute-start(bf16[112,512]{1,0:T(8,128)(2,1)S(1)} %get-tuple-element.67), channel_id=1, source_target_pairs={{0,16},{1,17},{2,18},{3,19},{4,20},{5,21},{6,22},{7,23},{8,24},{9,... | collective-permute-start | bytes 344072 | tf_op jit(solution)/shard_map/ppermute | solution.py:18
  64.9 12.1 %collective-permute-start.11 = (bf16[112,512]{1,0:T(8,128)(2,1)S(1)}, bf16[112,512]{1,0:T(8,128)(2,1)S(1)}, u32[]{:S(2)}, u32[]{:S(2)}) collective-permute-start(bf16[112,512]{1,0:T(8,128)(2,1)S(1)} %get-tuple-element.68), channel_id=1, source_target_pairs={{0,8},{1,9},{2,10},{3,11},{4,12},{5,13},{6,14},{7,15},{8,0},{9,1},... | collective-permute-start | bytes 344072 | tf_op jit(solution)/shard_map/ppermute | solution.py:18
  77.1 4.5 %collective-permute-start.14 = (f32[4,128]{1,0:T(4,128)S(1)}, f32[4,128]{1,0:T(4,128)S(1)}, u32[]{:S(2)}, u32[]{:S(2)}) collective-permute-start(f32[4,128]{1,0:T(4,128)S(1)} %get-tuple-element.59), channel_id=1, source_target_pairs={{0,16},{1,17},{2,18},{3,19},{4,20},{5,21},{6,22},{7,23},{8,24},{9,... | collective-permute-start | bytes 6152 | tf_op jit(solution)/shard_map/ppermute | solution.py:18
  81.7 3.6 %collective-permute-start.15 = (f32[4,128]{1,0:T(4,128)S(1)}, f32[4,128]{1,0:T(4,128)S(1)}, u32[]{:S(2)}, u32[]{:S(2)}) collective-permute-start(f32[4,128]{1,0:T(4,128)S(1)} %add.35), channel_id=1, source_target_pairs={{0,8},{1,9},{2,10},{3,11},{4,12},{5,13},{6,14},{7,15},{8,0},{9,1},... | collective-permute-start | bytes 6152 | tf_op jit(solution)/shard_map/ppermute | solution.py:18
  85.2 3.6 %collective-permute-start.16 = (f32[4,128]{1,0:T(4,128)S(1)}, f32[4,128]{1,0:T(4,128)S(1)}, u32[]{:S(2)}, u32[]{:S(2)}) collective-permute-start(f32[4,128]{1,0:T(4,128)S(1)} %add.36), channel_id=1, source_target_pairs={{0,4},{1,5},{2,6},{3,7},{4,0},{5,1},{6,2},{7,3},{8,12},{9,13},{10,... | collective-permute-start | bytes 6152 | tf_op jit(solution)/shard_map/ppermute | solution.py:18
  88.8 3.6 %collective-permute-start.17 = (f32[4,128]{1,0:T(4,128)S(1)}, f32[4,128]{1,0:T(4,128)S(1)}, u32[]{:S(2)}, u32[]{:S(2)}) collective-permute-start(f32[4,128]{1,0:T(4,128)S(1)} %add.37), channel_id=1, source_target_pairs={{0,2},{1,3},{2,0},{3,1},{4,6},{5,7},{6,4},{7,5},{8,10},{9,11},{10,... | collective-permute-start | bytes 6152 | tf_op jit(solution)/shard_map/ppermute | solution.py:18
  92.4 1.8 %collective-permute-start.18 = (f32[4,128]{1,0:T(4,128)S(1)}, f32[4,128]{1,0:T(4,128)S(1)}, u32[]{:S(2)}, u32[]{:S(2)}) collective-permute-start(f32[4,128]{1,0:T(4,128)S(1)} %add.38), channel_id=1, source_target_pairs={{0,1},{1,0},{2,3},{3,2},{4,5},{5,4},{6,7},{7,6},{8,9},{9,8},{10,11... | collective-permute-start | bytes 6152 | tf_op jit(solution)/shard_map/ppermute | solution.py:18
